TPU v7x, 256 devices: a whole 4x4x8 slice. The times are simulated.
256 devices in a mesh: mem: 16 (over y, z_hi), lat: 16 (over x, z_lo, core).
Axes of the slice: x: 4, y: 4, z: 8 (z_hi: 4, z_lo: 2; z = z_hi * 2 + z_lo), core: 2. Of those that a mesh axis runs over, the one named last changes fastest.
Arguments:
- replica_variables: float32 [16, 4, 256, 4096], P('mem', None, 'lat'), may hold values from -40 to 40, as said below
- analysis: float32 [4, 256, 4096], P(None, 'lat'), may hold values from -4 to 4
- labels: int32 [256, 32], P('lat'), may hold values from 0 to 7, as said below
- pairing: int32 [16], replicated, may hold values from 0 to 15, as said below
Outputs:
- closing_ensemble_values: float32 [16, 4, 256, 4096], P('mem', None, 'lat')
- factor: float32 [16, 8], P('mem')
Inputs may be any that keep to these rules, and one draw needn't show every extreme that they name: `replica_variables`: member fields; the spread of members differs across rows and columns. `labels`: every label value occurs at least once. pairing[pairing[m]] = m and pairing[m] != m for every member m.
All inputs are finite; a program needn't handle non-finite values.
Results may differ from a plain program's by a relative error of at most 0.00015.
Values sent between devices are 32-bit elements; how exact they have to be, the bound alone decides.
No kernel may reach another device: no remote copies, remote signals or barrier semaphores. Data moves between devices by JAX's collectives and lax.ppermute only.
A program may use at most 64 MiB of HBM per device.

v0:
```python
import jax
import jax.numpy as jnp
from jax import lax
from jax.sharding import PartitionSpec as P

TILE = 128
REGIONS = 8
STEPS = 3


grav_coef = 0.1
depth_coef = 0.1
advect_coef = 0.05
diffuse_coef = 0.05
coriolis_coef = 0.05
target_size = 0.5
small_eps = 1e-06


def with_halo(array, sides, width):
    for axis, dim in sides:
        size, length = (lax.axis_size(axis), array.shape[dim])
        up = [(i, (i + 1) % size) for i in range(size - 1)]
        down = [(j, i) for i, j in up]
        last = lax.slice_in_dim(array, length - width, length, axis=dim)
        initial = lax.slice_in_dim(array, 0, width, axis=dim)
        before = lax.ppermute(last, axis, up)
        after = lax.ppermute(initial, axis, down)
        array = jnp.concatenate([before, array, after], axis=dim)
    return array


def diff_lon(field):
    return jnp.roll(field, -1, axis=-1) - jnp.roll(field, 1, axis=-1)


def trimmed_latitude_lines(field, have, want, offset=0):
    margin = have - want
    total = field.shape[-2]
    return field[..., margin + offset : total - margin + offset, :]


def model_step(extended, have, coriolis, height_rim):
    height = extended[:, 0]
    zonal = extended[:, 1]
    meridional = extended[:, 2]
    tracer = extended[:, 3]
    inner = have - 1
    new_height = trimmed_latitude_lines(height, have, inner) - depth_coef * (
        diff_lon(trimmed_latitude_lines(zonal, have, inner))
        + trimmed_latitude_lines(meridional, have, inner, 1)
        - trimmed_latitude_lines(meridional, have, inner, -1)
    )
    new_zonal = (
        trimmed_latitude_lines(zonal, have, inner)
        + trimmed_latitude_lines(coriolis, have, inner)
        * trimmed_latitude_lines(meridional, have, inner)
        - grav_coef * diff_lon(new_height)
    )
    padded_height, height_have = height_rim(new_height, inner)
    outer = height_have - 1
    zonal_out = trimmed_latitude_lines(new_zonal, inner, outer)
    new_meridional = (
        trimmed_latitude_lines(meridional, have, outer)
        - trimmed_latitude_lines(coriolis, have, outer) * zonal_out
        - grav_coef
        * (
            trimmed_latitude_lines(padded_height, height_have, outer, 1)
            - trimmed_latitude_lines(padded_height, height_have, outer, -1)
        )
    )
    centre = trimmed_latitude_lines(tracer, have, outer)
    upper = trimmed_latitude_lines(tracer, have, outer, 1)
    lower = trimmed_latitude_lines(tracer, have, outer, -1)
    new_tracer = (
        centre
        - advect_coef * (zonal_out * diff_lon(centre) + new_meridional * (upper - lower))
        + diffuse_coef
        * (
            jnp.roll(centre, -1, axis=-1)
            + jnp.roll(centre, 1, axis=-1)
            + upper
            + lower
            - 4.0 * centre
        )
    )
    quantity_bundle = jnp.stack(
        [
            trimmed_latitude_lines(padded_height, height_have, outer),
            zonal_out,
            new_meridional,
            new_tracer,
        ],
        axis=1,
    )
    return (quantity_bundle, outer)


def global_rows(local_rows, extra):
    start = lax.axis_index("lat") * local_rows
    return (start - extra + jnp.arange(local_rows + 2 * extra)).astype(jnp.float32)


def coriolis_rows(local_rows, extra):
    rows_all = local_rows * lax.axis_size("lat")
    where_rows = global_rows(local_rows, extra)
    return (coriolis_coef * (2.0 * (where_rows + 0.5) / rows_all - 1.0))[:, None]


def predicted_flow(quantity_bundle):
    local_rows = quantity_bundle.shape[2]
    coriolis = coriolis_rows(local_rows, 1)

    def shared_height(new_height, inner):
        return (with_halo(new_height, (("lat", 1),), 1), 1)

    for index in range(STEPS):
        extended = with_halo(quantity_bundle, (("lat", 2),), 1)
        quantity_bundle, _ = model_step(extended, 1, coriolis, shared_height)
    return quantity_bundle


def energy_tiles(spread, tile_labels):
    energy = 0.5 * jnp.sum(spread * spread, axis=1)
    padded = with_halo(energy, (("lat", 1),), 1)
    smoothed_field = 0.25 * (padded[:, 2:] + 2.0 * energy + padded[:, :-2])
    members, local_rows, width = smoothed_field.shape
    tile_sums = smoothed_field.reshape(members, local_rows, width // TILE, TILE).sum(-1)
    onehot = (tile_labels[..., None] == jnp.arange(REGIONS, dtype=jnp.int32)).astype(jnp.float32)
    region_sum = jnp.einsum("mrt,rtk->mk", tile_sums, onehot, precision=lax.Precision.HIGHEST)
    cells = onehot.sum((0, 1)) * TILE
    return (region_sum, cells, onehot)


def recentre(spread, centre_fields, region_sum, cells, onehot):
    factor = target_size / jnp.sqrt(region_sum / cells + small_eps)
    cell_factor = jnp.einsum("mk,rtk->mrt", factor, onehot, precision=lax.Precision.HIGHEST)
    members, fields_count, local_rows, width = spread.shape
    scaled = (
        spread.reshape(members, fields_count, local_rows, width // TILE, TILE)
        * cell_factor[:, None, :, :, None]
    ).reshape(spread.shape)
    return (centre_fields[None] + scaled, factor)


def local(replica_variables, analysis, labels, pairing):
    leading_replica = predicted_flow(replica_variables)
    member_index = lax.axis_index("mem")
    partner_index = pairing[member_index]
    piece = lax.all_gather(leading_replica, "mem", axis=0, tiled=True)
    present = (partner_index >= 0) & (partner_index < piece.shape[0])
    chosen = lax.dynamic_index_in_dim(
        piece, jnp.clip(partner_index, 0, piece.shape[0] - 1), 0, keepdims=True
    )
    partner = jnp.where(present, chosen, jnp.zeros_like(leading_replica))
    spread = 0.5 * (leading_replica - partner)
    region_sum, cells, onehot = energy_tiles(spread, labels)
    region_sum, cells = lax.psum((region_sum, cells), "lat")
    central_latitude_lines, factor = recentre(spread, analysis, region_sum, cells, onehot)
    closing_ensemble_values = predicted_flow(central_latitude_lines)
    return (closing_ensemble_values, factor)


def solution(mesh):
    return jax.shard_map(
        local,
        mesh=mesh,
        in_specs=(P("mem", None, "lat", None), P(None, "lat", None), P("lat", None), P()),
        out_specs=(P("mem", None, "lat", None), P("mem", None)),
        check_vma=False,
    )
```

profile of v0, /device:TPU:1, one launch (start us, length us, event | category | flops | bytes accessed | tf_op | source)
XLA Modules:
  0.0 377.2 jit_solution(1945998484526989301)
XLA Ops:
  8.5 4.9 %collective-permute-start = (f32[1,4,1,4096]{3,2,1,0:T(1,128)S(1)}, f32[1,4,1,4096]{3,2,1,0:T(1,128)S(1)}, u32[]{:S(2)}, u32[]{:S(2)}) collective-permute-start(f32[1,4,1,4096]{3,2,1,0:T(1,128)S(1)} %get-tuple-element.50), channel_id=1, source_target_pairs={{0,1},{1,2},{2,3},{3,4},{4,5},{5,6},{6,7},{7,8},{8,9},{9,10},{10,1... | collective-permute-start | bytes 196616 | tf_op jit(solution)/shard_map/ppermute | solution.py:27
  15.5 3.6 collective-permute-done.1
  23.3 3.6 collective-permute-start.3
  28.5 4.2 %collective-permute-start.4 = (f32[1,4,1,4096]{3,2,1,0:T(1,128)S(1)}, f32[1,4,1,4096]{3,2,1,0:T(1,128)S(1)}, u32[]{:S(2)}, u32[]{:S(2)}) collective-permute-start(f32[1,4,1,4096]{3,2,1,0:T(1,128)S(1)} %get-tuple-element.48), channel_id=1, source_target_pairs={{0,1},{1,2},{2,3},{3,4},{4,5},{5,6},{6,7},{7,8},{8,9},{9,10},{10,1... | collective-permute-start | bytes 196616 | tf_op jit(solution)/shard_map/ppermute | solution.py:27
  32.7 1.9 collective-permute-start.5
  34.6 3.8 %collective-permute-done.5 = f32[1,4,1,4096]{3,2,1,0:T(1,128)S(1)} collective-permute-done((f32[1,4,1,4096]{3,2,1,0:T(1,128)S(1)}, f32[1,4,1,4096]{3,2,1,0:T(1,128)S(1)}, u32[]{:S(2)}, u32[]{:S(2)}) %collective-permute-start.5) | collective-permute-done | bytes 65568 | tf_op jit(solution)/shard_map/ppermute | solution.py:28
  41.5 3.6 collective-permute-start.7
  46.7 4.7 %collective-permute-start.8 = (f32[1,4,1,4096]{3,2,1,0:T(1,128)S(1)}, f32[1,4,1,4096]{3,2,1,0:T(1,128)S(1)}, u32[]{:S(2)}, u32[]{:S(2)}) collective-permute-start(f32[1,4,1,4096]{3,2,1,0:T(1,128)S(1)} %get-tuple-element.46), channel_id=1, source_target_pairs={{0,1},{1,2},{2,3},{3,4},{4,5},{5,6},{6,7},{7,8},{8,9},{9,10},{10,1... | collective-permute-start | bytes 196616 | tf_op jit(solution)/shard_map/ppermute | solution.py:27
  51.4 1.9 collective-permute-start.9
  53.3 4.8 %collective-permute-done.9 = f32[1,4,1,4096]{3,2,1,0:T(1,128)S(1)} collective-permute-done((f32[1,4,1,4096]{3,2,1,0:T(1,128)S(1)}, f32[1,4,1,4096]{3,2,1,0:T(1,128)S(1)}, u32[]{:S(2)}, u32[]{:S(2)}) %collective-permute-start.9) | collective-permute-done | bytes 65568 | tf_op jit(solution)/shard_map/ppermute | solution.py:28
  59.2 1.9 collective-permute-start.10
  61.1 3.7 collective-permute-start.11
  70.0 207.9 %all-gather.2.cloned.1.call-done = f32[16,4,16,4096]{3,2,1,0:T(8,128)} async-done(((f32[1,4,16,4096]{3,2,1,0:T(8,128)}), f32[16,4,16,4096]{3,2,1,0:T(8,128)}) %all-gather.2.cloned.1.call-update) | async-done | bytes 16777232 | tf_op jit(solution)/shard_map/all_gather | solution.py:150
  279.5 4.0 %collective-permute-start.12 = (f32[1,1,4096]{2,1,0:T(1,128)S(1)}, f32[1,1,4096]{2,1,0:T(1,128)S(1)}, u32[]{:S(2)}, u32[]{:S(2)}) collective-permute-start(f32[1,1,4096]{2,1,0:T(1,128)S(1)} %get-tuple-element.118), channel_id=1, source_target_pairs={{1,0},{2,1},{3,2},{4,3},{5,4},{6,5},{7,6},{8,7},{9,8},{10,9},{11,1... | collective-permute-start | bytes 49160 | tf_op jit(solution)/shard_map/ppermute | solution.py:28
  283.4 1.9 collective-permute-start.13
  286.9 26.8 %all-reduce = (f32[1,8]{1,0:T(1,128)S(1)}, f32[1,8]{1,0:T(1,128)S(1)}) all-reduce(f32[1,8]{1,0:T(1,128)S(1)} %convolution_bitcast_fusion, f32[1,8]{1,0:T(1,128)S(1)} %multiply_bitcast_fusion), channel_id=1, replica_groups=mesh['mem'=16,'lat'=16] {'lat'}, use_global_device_ids=true, to_apply=%region_2.3 | all-reduce | flops 16 | bytes 128 | tf_op jit(solution)/shard_map/psum | solution.py:158
  317.7 3.8 %collective-permute-start.15 = (f32[1,4,1,4096]{3,2,1,0:T(1,128)S(1)}, f32[1,4,1,4096]{3,2,1,0:T(1,128)S(1)}, u32[]{:S(2)}, u32[]{:S(2)}) collective-permute-start(f32[1,4,1,4096]{3,2,1,0:T(1,128)S(1)} %get-tuple-element.45), channel_id=1, source_target_pairs={{1,0},{2,1},{3,2},{4,3},{5,4},{6,5},{7,6},{8,7},{9,8},{10,9},{11,1... | collective-permute-start | bytes 196616 | tf_op jit(solution)/shard_map/ppermute | solution.py:28
  326.4 3.6 collective-permute-start.17
  331.5 4.2 %collective-permute-start.18 = (f32[1,4,1,4096]{3,2,1,0:T(1,128)S(1)}, f32[1,4,1,4096]{3,2,1,0:T(1,128)S(1)}, u32[]{:S(2)}, u32[]{:S(2)}) collective-permute-start(f32[1,4,1,4096]{3,2,1,0:T(1,128)S(1)} %get-tuple-element.42), channel_id=1, source_target_pairs={{0,1},{1,2},{2,3},{3,4},{4,5},{5,6},{6,7},{7,8},{8,9},{9,10},{10,1... | collective-permute-start | bytes 196616 | tf_op jit(solution)/shard_map/ppermute | solution.py:27
  337.7 3.8 %collective-permute-done.19 = f32[1,4,1,4096]{3,2,1,0:T(1,128)S(1)} collective-permute-done((f32[1,4,1,4096]{3,2,1,0:T(1,128)S(1)}, f32[1,4,1,4096]{3,2,1,0:T(1,128)S(1)}, u32[]{:S(2)}, u32[]{:S(2)}) %collective-permute-start.19) | collective-permute-done | bytes 65568 | tf_op jit(solution)/shard_map/ppermute | solution.py:28
  344.6 3.6 collective-permute-start.21
  349.7 4.7 %collective-permute-start.22 = (f32[1,4,1,4096]{3,2,1,0:T(1,128)S(1)}, f32[1,4,1,4096]{3,2,1,0:T(1,128)S(1)}, u32[]{:S(2)}, u32[]{:S(2)}) collective-permute-start(f32[1,4,1,4096]{3,2,1,0:T(1,128)S(1)} %get-tuple-element.40), channel_id=1, source_target_pairs={{0,1},{1,2},{2,3},{3,4},{4,5},{5,6},{6,7},{7,8},{8,9},{9,10},{10,1... | collective-permute-start | bytes 196616 | tf_op jit(solution)/shard_map/ppermute | solution.py:27
  356.4 4.8 %collective-permute-done.23 = f32[1,4,1,4096]{3,2,1,0:T(1,128)S(1)} collective-permute-done((f32[1,4,1,4096]{3,2,1,0:T(1,128)S(1)}, f32[1,4,1,4096]{3,2,1,0:T(1,128)S(1)}, u32[]{:S(2)}, u32[]{:S(2)}) %collective-permute-start.23) | collective-permute-done | bytes 65568 | tf_op jit(solution)/shard_map/ppermute | solution.py:28
  364.2 3.7 collective-permute-start.25
  (137 shorter events, 44.8 us)
Async XLA Ops:
  7.2 270.8 %all-gather.2.cloned.1.call-start = ((), (), s32[]{:S(2)}) async-start(), calls=%async_computation | async-start | bytes 17825792 | tf_op jit(solution)/shard_map/all_gather | solution.py:150
  8.5 7.0 %collective-permute-start = (f32[1,4,1,4096]{3,2,1,0:T(1,128)S(1)}, f32[1,4,1,4096]{3,2,1,0:T(1,128)S(1)}, u32[]{:S(2)}, u32[]{:S(2)}) collective-permute-start(f32[1,4,1,4096]{3,2,1,0:T(1,128)S(1)} %get-tuple-element.50), channel_id=1, source_target_pairs={{0,1},{1,2},{2,3},{3,4},{4,5},{5,6},{6,7},{7,8},{8,9},{9,10},{10,1... | collective-permute-start | bytes 196616 | tf_op jit(solution)/shard_map/ppermute | solution.py:27
  13.5 5.6 %collective-permute-start.1 = (f32[1,4,1,4096]{3,2,1,0:T(1,128)S(1)}, f32[1,4,1,4096]{3,2,1,0:T(1,128)S(1)}, u32[]{:S(2)}, u32[]{:S(2)}) collective-permute-start(f32[1,4,1,4096]{3,2,1,0:T(1,128)S(1)} %get-tuple-element.51), channel_id=1, source_target_pairs={{1,0},{2,1},{3,2},{4,3},{5,4},{6,5},{7,6},{8,7},{9,8},{10,9},{11,1... | collective-permute-start | bytes 196616 | tf_op jit(solution)/shard_map/ppermute | solution.py:28
  21.4 5.7 %collective-permute-start.2 = (f32[1,1,4096]{2,1,0:T(1,128)S(1)}, f32[1,1,4096]{2,1,0:T(1,128)S(1)}, u32[]{:S(2)}, u32[]{:S(2)}) collective-permute-start(f32[1,1,4096]{2,1,0:T(1,128)S(1)} %get-tuple-element.136), channel_id=1, source_target_pairs={{1,0},{2,1},{3,2},{4,3},{5,4},{6,5},{7,6},{8,7},{9,8},{10,9},{11,1... | collective-permute-start | bytes 49160 | tf_op jit(solution)/shard_map/ppermute | solution.py:28
  23.3 4.5 %collective-permute-start.3 = (f32[1,1,4096]{2,1,0:T(1,128)S(1)}, f32[1,1,4096]{2,1,0:T(1,128)S(1)}, u32[]{:S(2)}, u32[]{:S(2)}) collective-permute-start(f32[1,1,4096]{2,1,0:T(1,128)S(1)} %get-tuple-element.137), channel_id=1, source_target_pairs={{0,1},{1,2},{2,3},{3,4},{4,5},{5,6},{6,7},{7,8},{8,9},{9,10},{10,1... | collective-permute-start | bytes 49160 | tf_op jit(solution)/shard_map/ppermute | solution.py:27
  28.5 6.1 %collective-permute-start.4 = (f32[1,4,1,4096]{3,2,1,0:T(1,128)S(1)}, f32[1,4,1,4096]{3,2,1,0:T(1,128)S(1)}, u32[]{:S(2)}, u32[]{:S(2)}) collective-permute-start(f32[1,4,1,4096]{3,2,1,0:T(1,128)S(1)} %get-tuple-element.48), channel_id=1, source_target_pairs={{0,1},{1,2},{2,3},{3,4},{4,5},{5,6},{6,7},{7,8},{8,9},{9,10},{10,1... | collective-permute-start | bytes 196616 | tf_op jit(solution)/shard_map/ppermute | solution.py:27
  32.7 5.8 %collective-permute-start.5 = (f32[1,4,1,4096]{3,2,1,0:T(1,128)S(1)}, f32[1,4,1,4096]{3,2,1,0:T(1,128)S(1)}, u32[]{:S(2)}, u32[]{:S(2)}) collective-permute-start(f32[1,4,1,4096]{3,2,1,0:T(1,128)S(1)} %get-tuple-element.49), channel_id=1, source_target_pairs={{1,0},{2,1},{3,2},{4,3},{5,4},{6,5},{7,6},{8,7},{9,8},{10,9},{11,1... | collective-permute-start | bytes 196616 | tf_op jit(solution)/shard_map/ppermute | solution.py:28
  39.6 5.7 %collective-permute-start.6 = (f32[1,1,4096]{2,1,0:T(1,128)S(1)}, f32[1,1,4096]{2,1,0:T(1,128)S(1)}, u32[]{:S(2)}, u32[]{:S(2)}) collective-permute-start(f32[1,1,4096]{2,1,0:T(1,128)S(1)} %get-tuple-element.130), channel_id=1, source_target_pairs={{1,0},{2,1},{3,2},{4,3},{5,4},{6,5},{7,6},{8,7},{9,8},{10,9},{11,1... | collective-permute-start | bytes 49160 | tf_op jit(solution)/shard_map/ppermute | solution.py:28
  41.5 4.5 %collective-permute-start.7 = (f32[1,1,4096]{2,1,0:T(1,128)S(1)}, f32[1,1,4096]{2,1,0:T(1,128)S(1)}, u32[]{:S(2)}, u32[]{:S(2)}) collective-permute-start(f32[1,1,4096]{2,1,0:T(1,128)S(1)} %get-tuple-element.131), channel_id=1, source_target_pairs={{0,1},{1,2},{2,3},{3,4},{4,5},{5,6},{6,7},{7,8},{8,9},{9,10},{10,1... | collective-permute-start | bytes 49160 | tf_op jit(solution)/shard_map/ppermute | solution.py:27
  46.7 6.6 %collective-permute-start.8 = (f32[1,4,1,4096]{3,2,1,0:T(1,128)S(1)}, f32[1,4,1,4096]{3,2,1,0:T(1,128)S(1)}, u32[]{:S(2)}, u32[]{:S(2)}) collective-permute-start(f32[1,4,1,4096]{3,2,1,0:T(1,128)S(1)} %get-tuple-element.46), channel_id=1, source_target_pairs={{0,1},{1,2},{2,3},{3,4},{4,5},{5,6},{6,7},{7,8},{8,9},{9,10},{10,1... | collective-permute-start | bytes 196616 | tf_op jit(solution)/shard_map/ppermute | solution.py:27
  51.4 6.7 %collective-permute-start.9 = (f32[1,4,1,4096]{3,2,1,0:T(1,128)S(1)}, f32[1,4,1,4096]{3,2,1,0:T(1,128)S(1)}, u32[]{:S(2)}, u32[]{:S(2)}) collective-permute-start(f32[1,4,1,4096]{3,2,1,0:T(1,128)S(1)} %get-tuple-element.47), channel_id=1, source_target_pairs={{1,0},{2,1},{3,2},{4,3},{5,4},{6,5},{7,6},{8,7},{9,8},{10,9},{11,1... | collective-permute-start | bytes 196616 | tf_op jit(solution)/shard_map/ppermute | solution.py:28
  59.2 5.7 %collective-permute-start.10 = (f32[1,1,4096]{2,1,0:T(1,128)S(1)}, f32[1,1,4096]{2,1,0:T(1,128)S(1)}, u32[]{:S(2)}, u32[]{:S(2)}) collective-permute-start(f32[1,1,4096]{2,1,0:T(1,128)S(1)} %get-tuple-element.124), channel_id=1, source_target_pairs={{1,0},{2,1},{3,2},{4,3},{5,4},{6,5},{7,6},{8,7},{9,8},{10,9},{11,1... | collective-permute-start | bytes 49160 | tf_op jit(solution)/shard_map/ppermute | solution.py:28
  61.1 4.6 %collective-permute-start.11 = (f32[1,1,4096]{2,1,0:T(1,128)S(1)}, f32[1,1,4096]{2,1,0:T(1,128)S(1)}, u32[]{:S(2)}, u32[]{:S(2)}) collective-permute-start(f32[1,1,4096]{2,1,0:T(1,128)S(1)} %get-tuple-element.125), channel_id=1, source_target_pairs={{0,1},{1,2},{2,3},{3,4},{4,5},{5,6},{6,7},{7,8},{8,9},{9,10},{10,1... | collective-permute-start | bytes 49160 | tf_op jit(solution)/shard_map/ppermute | solution.py:27
  279.5 5.9 %collective-permute-start.12 = (f32[1,1,4096]{2,1,0:T(1,128)S(1)}, f32[1,1,4096]{2,1,0:T(1,128)S(1)}, u32[]{:S(2)}, u32[]{:S(2)}) collective-permute-start(f32[1,1,4096]{2,1,0:T(1,128)S(1)} %get-tuple-element.118), channel_id=1, source_target_pairs={{1,0},{2,1},{3,2},{4,3},{5,4},{6,5},{7,6},{8,7},{9,8},{10,9},{11,1... | collective-permute-start | bytes 49160 | tf_op jit(solution)/shard_map/ppermute | solution.py:28
  315.8 5.7 %collective-permute-start.14 = (f32[1,4,1,4096]{3,2,1,0:T(1,128)S(1)}, f32[1,4,1,4096]{3,2,1,0:T(1,128)S(1)}, u32[]{:S(2)}, u32[]{:S(2)}) collective-permute-start(f32[1,4,1,4096]{3,2,1,0:T(1,128)S(1)} %get-tuple-element.44), channel_id=1, source_target_pairs={{0,1},{1,2},{2,3},{3,4},{4,5},{5,6},{6,7},{7,8},{8,9},{9,10},{10,1... | collective-permute-start | bytes 196616 | tf_op jit(solution)/shard_map/ppermute | solution.py:27
  317.7 5.6 %collective-permute-start.15 = (f32[1,4,1,4096]{3,2,1,0:T(1,128)S(1)}, f32[1,4,1,4096]{3,2,1,0:T(1,128)S(1)}, u32[]{:S(2)}, u32[]{:S(2)}) collective-permute-start(f32[1,4,1,4096]{3,2,1,0:T(1,128)S(1)} %get-tuple-element.45), channel_id=1, source_target_pairs={{1,0},{2,1},{3,2},{4,3},{5,4},{6,5},{7,6},{8,7},{9,8},{10,9},{11,1... | collective-permute-start | bytes 196616 | tf_op jit(solution)/shard_map/ppermute | solution.py:28
  324.4 5.7 %collective-permute-start.16 = (f32[1,1,4096]{2,1,0:T(1,128)S(1)}, f32[1,1,4096]{2,1,0:T(1,128)S(1)}, u32[]{:S(2)}, u32[]{:S(2)}) collective-permute-start(f32[1,1,4096]{2,1,0:T(1,128)S(1)} %get-tuple-element.116), channel_id=1, source_target_pairs={{1,0},{2,1},{3,2},{4,3},{5,4},{6,5},{7,6},{8,7},{9,8},{10,9},{11,1... | collective-permute-start | bytes 49160 | tf_op jit(solution)/shard_map/ppermute | solution.py:28
  331.5 6.1 %collective-permute-start.18 = (f32[1,4,1,4096]{3,2,1,0:T(1,128)S(1)}, f32[1,4,1,4096]{3,2,1,0:T(1,128)S(1)}, u32[]{:S(2)}, u32[]{:S(2)}) collective-permute-start(f32[1,4,1,4096]{3,2,1,0:T(1,128)S(1)} %get-tuple-element.42), channel_id=1, source_target_pairs={{0,1},{1,2},{2,3},{3,4},{4,5},{5,6},{6,7},{7,8},{8,9},{9,10},{10,1... | collective-permute-start | bytes 196616 | tf_op jit(solution)/shard_map/ppermute | solution.py:27
  335.7 5.8 %collective-permute-start.19 = (f32[1,4,1,4096]{3,2,1,0:T(1,128)S(1)}, f32[1,4,1,4096]{3,2,1,0:T(1,128)S(1)}, u32[]{:S(2)}, u32[]{:S(2)}) collective-permute-start(f32[1,4,1,4096]{3,2,1,0:T(1,128)S(1)} %get-tuple-element.43), channel_id=1, source_target_pairs={{1,0},{2,1},{3,2},{4,3},{5,4},{6,5},{7,6},{8,7},{9,8},{10,9},{11,1... | collective-permute-start | bytes 196616 | tf_op jit(solution)/shard_map/ppermute | solution.py:28
  342.6 5.7 %collective-permute-start.20 = (f32[1,1,4096]{2,1,0:T(1,128)S(1)}, f32[1,1,4096]{2,1,0:T(1,128)S(1)}, u32[]{:S(2)}, u32[]{:S(2)}) collective-permute-start(f32[1,1,4096]{2,1,0:T(1,128)S(1)} %get-tuple-element.110), channel_id=1, source_target_pairs={{1,0},{2,1},{3,2},{4,3},{5,4},{6,5},{7,6},{8,7},{9,8},{10,9},{11,1... | collective-permute-start | bytes 49160 | tf_op jit(solution)/shard_map/ppermute | solution.py:28
  349.7 6.6 %collective-permute-start.22 = (f32[1,4,1,4096]{3,2,1,0:T(1,128)S(1)}, f32[1,4,1,4096]{3,2,1,0:T(1,128)S(1)}, u32[]{:S(2)}, u32[]{:S(2)}) collective-permute-start(f32[1,4,1,4096]{3,2,1,0:T(1,128)S(1)} %get-tuple-element.40), channel_id=1, source_target_pairs={{0,1},{1,2},{2,3},{3,4},{4,5},{5,6},{6,7},{7,8},{8,9},{9,10},{10,1... | collective-permute-start | bytes 196616 | tf_op jit(solution)/shard_map/ppermute | solution.py:27
  354.4 6.7 %collective-permute-start.23 = (f32[1,4,1,4096]{3,2,1,0:T(1,128)S(1)}, f32[1,4,1,4096]{3,2,1,0:T(1,128)S(1)}, u32[]{:S(2)}, u32[]{:S(2)}) collective-permute-start(f32[1,4,1,4096]{3,2,1,0:T(1,128)S(1)} %get-tuple-element.41), channel_id=1, source_target_pairs={{1,0},{2,1},{3,2},{4,3},{5,4},{6,5},{7,6},{8,7},{9,8},{10,9},{11,1... | collective-permute-start | bytes 196616 | tf_op jit(solution)/shard_map/ppermute | solution.py:28
  362.2 5.7 %collective-permute-start.24 = (f32[1,1,4096]{2,1,0:T(1,128)S(1)}, f32[1,1,4096]{2,1,0:T(1,128)S(1)}, u32[]{:S(2)}, u32[]{:S(2)}) collective-permute-start(f32[1,1,4096]{2,1,0:T(1,128)S(1)} %get-tuple-element.104), channel_id=1, source_target_pairs={{1,0},{2,1},{3,2},{4,3},{5,4},{6,5},{7,6},{8,7},{9,8},{10,9},{11,1... | collective-permute-start | bytes 49160 | tf_op jit(solution)/shard_map/ppermute | solution.py:28
  364.2 4.6 %collective-permute-start.25 = (f32[1,1,4096]{2,1,0:T(1,128)S(1)}, f32[1,1,4096]{2,1,0:T(1,128)S(1)}, u32[]{:S(2)}, u32[]{:S(2)}) collective-permute-start(f32[1,1,4096]{2,1,0:T(1,128)S(1)} %get-tuple-element.105), channel_id=1, source_target_pairs={{0,1},{1,2},{2,3},{3,4},{4,5},{5,6},{6,7},{7,8},{8,9},{9,10},{10,1... | collective-permute-start | bytes 49160 | tf_op jit(solution)/shard_map/ppermute | solution.py:27
  (7 other events, 53.6 us)
Sparse Core Ops, SparseCore 0:
  67.5 210.4 all-gather.1
where the time goes:
time: 384 us; the launch traced here: 377 us
  waiting for transfers between devices  236 us (61%)
  starting transfers between devices  77.5 us (20%)
  blocking collectives  26.8 us (7%)
  between operations  16.8 us (4%)
  other arithmetic  12.6 us (3%)
  local copies, waits for them, and re-layouts  6.98 us (2%)
    all_gather x1, waiting for transfers between devices, local(): piece = lax.all_gather(leading_replica, 'mem', axis=0, tiled=True)  208 us
    ppermute x13, starting transfers between devices, with_halo(): before = lax.ppermute(last, axis, up)  48.6 us
    ppermute x13, starting transfers between devices, with_halo(): after = lax.ppermute(initial, axis, down)  28.9 us
    psum x1, blocking collectives, local(): region_sum, cells = lax.psum((region_sum, cells), 'lat')  26.8 us
    ppermute x13, waiting for transfers between devices, with_halo(): after = lax.ppermute(initial, axis, down)  22.6 us
  transfers between devices with their start and end apart: 27, of which 14 were waited for; matrix products, arithmetic and copies ran while one was open for 0% of the time, Pallas kernels for 0%

commit v1 on v0

v1 whole, which is shorter than its diff:
```python
import jax
import jax.numpy as jnp
from jax import lax
from jax.sharding import PartitionSpec as P

TILE = 128
REGIONS = 8
STEPS = 3
EDGE = 8


grav_coef = 0.1
depth_coef = 0.1
advect_coef = 0.05
diffuse_coef = 0.05
coriolis_coef = 0.05
target_size = 0.5
small_eps = 1e-06


def neighbours(axis):
    size = lax.axis_size(axis)
    up = [(i, i + 1) for i in range(size - 1)]
    return up, [(j, i) for i, j in up]


def edges(array, dim):
    up, down = neighbours("lat")
    length = array.shape[dim]
    last = lax.slice_in_dim(array, length - EDGE, length, axis=dim)
    initial = lax.slice_in_dim(array, 0, EDGE, axis=dim)
    return lax.ppermute(last, "lat", up), lax.ppermute(initial, "lat", down)


def east(field):
    return jnp.roll(field, -1, axis=-1)


def west(field):
    return jnp.roll(field, 1, axis=-1)


def step(fields, rows):
    h, u, v, q = fields
    total_rows = lax.axis_size("lat") * 16
    inside = ((rows >= 0) & (rows < total_rows)).astype(jnp.float32)[:, None]
    f = (coriolis_coef * (2.0 * (rows.astype(jnp.float32) + 0.5) / total_rows - 1.0))[:, None]
    c1 = slice(1, -1)
    h1 = (h[c1] - depth_coef * (east(u[c1]) - west(u[c1]) + v[2:] - v[:-2])) * inside[c1]
    c2 = slice(2, -2)
    ins = inside[c2]
    h1c = h1[c1]
    u1 = (u[c2] + f[c2] * v[c2] - grav_coef * (east(h1c) - west(h1c))) * ins
    v1 = (v[c2] - f[c2] * u1 - grav_coef * (h1[2:] - h1[:-2])) * ins
    qc, qn, qs = q[c2], q[3:-1], q[1:-3]
    qe, qw = east(qc), west(qc)
    q1 = (
        qc
        - advect_coef * (u1 * (qe - qw) + v1 * (qn - qs))
        + diffuse_coef * (qe + qw + qn + qs - 4.0 * qc)
    ) * ins
    return (h1c, u1, v1, q1), rows[c2]


def flow(before, middle, after):
    local_rows = middle.shape[1]
    rows = lax.axis_index("lat") * local_rows - EDGE + jnp.arange(local_rows + 2 * EDGE)
    ext = jnp.concatenate([before, middle, after], axis=1)
    fields = tuple(ext[i] for i in range(4))
    for _ in range(STEPS):
        fields, rows = step(fields, rows)
    spare = EDGE - 2 * STEPS
    return jnp.stack([x[spare:-spare] for x in fields])


def local(replica_variables, analysis, labels, pairing):
    members = lax.axis_size("mem")
    x = replica_variables[0]
    fields, local_rows, width = x.shape
    chunk = width // members
    before, after = edges(x, 1)
    first = flow(before, x, after)

    a_before, a_after = edges(analysis, 1)
    up, down = neighbours("lat")
    coded = labels + 1
    l_before, l_after = edges(coded, 0)
    coded = jnp.concatenate([l_before, coded, l_after], axis=0)
    region = jnp.arange(1, REGIONS + 1, dtype=jnp.int32)
    onehot = (coded[..., None] == region).astype(jnp.float32)
    mid = onehot[EDGE:-EDGE]
    weight = 0.25 * (onehot[EDGE - 1 : -EDGE - 1] + 2.0 * mid + onehot[EDGE + 1 : -EDGE + 1])
    cells = mid.sum((0, 1)) * TILE

    pieces = first.reshape(fields, local_rows, members, chunk).transpose(2, 0, 1, 3)
    everyone = lax.all_to_all(pieces, "mem", 0, 0, tiled=True)
    spread = 0.5 * (everyone - everyone[pairing])
    energy = 0.5 * jnp.sum(spread * spread, axis=1)
    tiles = chunk // TILE
    tile_sums = energy.reshape(members, local_rows, tiles, TILE).sum(-1)
    own_weight = lax.dynamic_slice_in_dim(weight, lax.axis_index("mem") * tiles, tiles, axis=1)
    partial = jnp.einsum("mrt,rtk->mk", tile_sums, own_weight, precision=lax.Precision.HIGHEST)
    sums = jnp.concatenate([partial, cells[None]], axis=0)
    lat_size = lax.axis_size("lat")
    sums = lax.all_to_all(
        jnp.broadcast_to(sums[None], (lat_size,) + sums.shape), "lat", 0, 0, tiled=True
    ).sum(0)
    region_sum = lax.all_to_all(sums[:members], "mem", 0, 0, tiled=True).sum(0)
    factor = target_size / jnp.sqrt(region_sum / sums[members] + small_eps)

    back = lax.all_to_all(spread, "mem", 0, 0, tiled=True)
    b_before, b_after = edges(back, 2)

    def joined(part):
        return part.transpose(1, 2, 0, 3).reshape(fields, part.shape[2], width)

    cell_factor = jnp.einsum("k,rtk->rt", factor, onehot, precision=lax.Precision.HIGHEST)

    def recentred(centre, part, scale):
        scale = jnp.repeat(scale, TILE, axis=1)
        return centre + scale[None] * joined(part)

    closing = flow(
        recentred(a_before, b_before, cell_factor[:EDGE]),
        recentred(analysis, back, cell_factor[EDGE:-EDGE]),
        recentred(a_after, b_after, cell_factor[-EDGE:]),
    )
    return closing[None], factor[None]


def solution(mesh):
    return jax.shard_map(
        local,
        mesh=mesh,
        in_specs=(P("mem", None, "lat", None), P(None, "lat", None), P("lat", None), P()),
        out_specs=(P("mem", None, "lat", None), P("mem", None)),
        check_vma=False,
    )
```

time: 384 us -> 163 us (0.42); the launches traced: 377 us -> 162 us
  waiting for transfers between devices: 236 us -> 61.4 us
  starting transfers between devices: 77.5 us -> 48.1 us
  between operations: 16.8 us -> 1.51 us
  local copies, waits for them, and re-layouts: 6.98 us -> 15.6 us
  blocking collectives: 26.8 us -> 19.7 us
    all_gather x1 -> x0, waiting for transfers between devices: 208 us -> none  [local(): piece = lax.all_gather(leading_replica, 'mem', axis=0, tiled=True)]
    ppermute x26 -> x8, starting transfers between devices: 77.4 us -> 26.7 us  [edges(): return (lax.ppermute(last, 'lat', up), lax.ppermute(initial, 'lat', down))]
    psum x1 -> x0, blocking collectives: 26.8 us -> none  [local(): region_sum, cells = lax.psum((region_sum, cells), 'lat')]
    all_to_all x0 -> x3, waiting for transfers between devices: none -> 25.6 us  [the longest x1 23.2 us: local(): back = lax.all_to_all(spread, 'mem', 0, 0, tiled=True)]
    all_to_all x0 -> x3, starting transfers between devices: none -> 21.4 us  [the longest x1 10.9 us: local(): everyone = lax.all_to_all(pieces, 'mem', 0, 0, tiled=True)]
    all_to_all x0 -> x1, blocking collectives: none -> 19.7 us  [local(): lax.all_to_all(jnp.broadcast_to(sums[None], (lat_size,) + sums.shape), 'l...]
    ppermute x26 -> x8, waiting for transfers between devices: 28.3 us -> 35.8 us  [edges(): return (lax.ppermute(last, 'lat', up), lax.ppermute(initial, 'lat', down))]
    mul x2 -> x17, other arithmetic: 0.03 us -> 5.38 us  [the longest x4 2.81 us: step(): (qc - advect_coef * (u1 * (qe - qw) + v1 * (qn - qs)) + diffuse_coef * (q...]
  transfers between devices with their start and end apart: 27 -> 11, of which waited for: 14 -> 8; matrix products, arithmetic and copies ran while one was open for 0% -> 4% of each run, Pallas kernels for 0% -> 0%
where the time goes in v1:
time: 163 us; the launch traced here: 162 us
  waiting for transfers between devices  61.4 us (38%)
  starting transfers between devices  48.1 us (30%)
  blocking collectives  19.7 us (12%)
  local copies, waits for them, and re-layouts  15.6 us (10%)
  other arithmetic  15.1 us (9%)
    ppermute x8, waiting for transfers between devices, edges(): return (lax.ppermute(last, 'lat', up), lax.ppermute(initial, 'lat', down))  35.8 us
    ppermute x8, starting transfers between devices, edges(): return (lax.ppermute(last, 'lat', up), lax.ppermute(initial, 'lat', down))  26.7 us
    all_to_all x1, waiting for transfers between devices, local(): back = lax.all_to_all(spread, 'mem', 0, 0, tiled=True)  23.2 us
    all_to_all x1, blocking collectives, local(): lax.all_to_all(jnp.broadcast_to(sums[None], (lat_size,) + sums.shape), 'l...  19.7 us
    all_to_all x1, starting transfers between devices, local(): everyone = lax.all_to_all(pieces, 'mem', 0, 0, tiled=True)  10.9 us
    all_to_all x1, starting transfers between devices, local(): back = lax.all_to_all(spread, 'mem', 0, 0, tiled=True)  6.65 us
    all_to_all x1, starting transfers between devices, local(): region_sum = lax.all_to_all(sums[:members], 'mem', 0, 0, tiled=True).sum(0)  3.85 us
  transfers between devices with their start and end apart: 11, of which 8 were waited for; matrix products, arithmetic and copies ran while one was open for 4% of the time, Pallas kernels for 0%

profile of v1, /device:TPU:1, one launch (start us, length us, event | category | flops | bytes accessed | tf_op | source)
XLA Modules:
  0.0 161.9 jit_solution(8223506321806041048)
XLA Ops:
  0.6 1.4 fusion.109
  2.0 4.9 %collective-permute-start.1 = (f32[4,8,4096]{2,1,0:T(8,128)S(1)}, f32[4,8,4096]{2,1,0:T(8,128)S(1)}, u32[]{:S(2)}, u32[]{:S(2)}) collective-permute-start(f32[4,8,4096]{2,1,0:T(8,128)S(1)} %get-tuple-element.36), channel_id=1, source_target_pairs={{0,1},{1,2},{2,3},{3,4},{4,5},{5,6},{6,7},{7,8},{8,9},{9,10},{10,1... | collective-permute-start | bytes 1572872 | tf_op jit(solution)/shard_map/ppermute | solution.py:32
  6.9 1.9 %collective-permute-start.2 = (f32[4,8,4096]{2,1,0:T(8,128)S(1)}, f32[4,8,4096]{2,1,0:T(8,128)S(1)}, u32[]{:S(2)}, u32[]{:S(2)}) collective-permute-start(f32[4,8,4096]{2,1,0:T(8,128)S(1)} %get-tuple-element.37), channel_id=1, source_target_pairs={{1,0},{2,1},{3,2},{4,3},{5,4},{6,5},{7,6},{8,7},{9,8},{10,9},{11,1... | collective-permute-start | bytes 1572872 | tf_op jit(solution)/shard_map/ppermute | solution.py:32
  10.0 3.1 %collective-permute-done.1 = f32[4,8,4096]{2,1,0:T(8,128)S(1)} collective-permute-done((f32[4,8,4096]{2,1,0:T(8,128)S(1)}, f32[4,8,4096]{2,1,0:T(8,128)S(1)}, u32[]{:S(2)}, u32[]{:S(2)}) %collective-permute-start.1) | collective-permute-done | bytes 524320 | tf_op jit(solution)/shard_map/ppermute | solution.py:32
  13.1 6.8 %collective-permute-done.2 = f32[4,8,4096]{2,1,0:T(8,128)S(1)} collective-permute-done((f32[4,8,4096]{2,1,0:T(8,128)S(1)}, f32[4,8,4096]{2,1,0:T(8,128)S(1)}, u32[]{:S(2)}, u32[]{:S(2)}) %collective-permute-start.2) | collective-permute-done | bytes 524320 | tf_op jit(solution)/shard_map/ppermute | solution.py:32
  27.8 10.9 %all-to-all-start = ((f32[16,4,16,256]{3,2,1,0:T(8,128)}), f32[16,4,16,256]{3,2,1,0:T(8,128)S(1)}, u32[]{:S(2)}, u32[]{:S(2)}) async-start(f32[16,4,16,256]{3,2,1,0:T(8,128)} %maximum_bitcast_fusion), calls=%async_computation | async-start | bytes 2097152 | tf_op jit(solution)/shard_map/all_to_all | solution.py:96
  38.8 2.0 %collective-permute-start.3 = (s32[8,32]{1,0:T(8,128)S(1)}, s32[8,32]{1,0:T(8,128)S(1)}, u32[]{:S(2)}, u32[]{:S(2)}) collective-permute-start(s32[8,32]{1,0:T(8,128)S(1)} %get-tuple-element.134), channel_id=1, source_target_pairs={{0,1},{1,2},{2,3},{3,4},{4,5},{5,6},{6,7},{7,8},{8,9},{9,10},{10,1... | collective-permute-start | bytes 3080 | tf_op jit(solution)/shard_map/ppermute | solution.py:32
  40.8 2.3 %collective-permute-start.4 = (s32[8,32]{1,0:T(8,128)S(1)}, s32[8,32]{1,0:T(8,128)S(1)}, u32[]{:S(2)}, u32[]{:S(2)}) collective-permute-start(s32[8,32]{1,0:T(8,128)S(1)} %get-tuple-element.135), channel_id=1, source_target_pairs={{1,0},{2,1},{3,2},{4,3},{5,4},{6,5},{7,6},{8,7},{9,8},{10,9},{11,1... | collective-permute-start | bytes 3080 | tf_op jit(solution)/shard_map/ppermute | solution.py:32
  43.2 5.6 %collective-permute-done.3 = s32[8,32]{1,0:T(8,128)S(1)} collective-permute-done((s32[8,32]{1,0:T(8,128)S(1)}, s32[8,32]{1,0:T(8,128)S(1)}, u32[]{:S(2)}, u32[]{:S(2)}) %collective-permute-start.3) | collective-permute-done | bytes 1056 | tf_op jit(solution)/shard_map/ppermute | solution.py:32
  48.8 9.5 %collective-permute-done.4 = s32[8,32]{1,0:T(8,128)S(1)} collective-permute-done((s32[8,32]{1,0:T(8,128)S(1)}, s32[8,32]{1,0:T(8,128)S(1)}, u32[]{:S(2)}, u32[]{:S(2)}) %collective-permute-start.4) | collective-permute-done | bytes 1056 | tf_op jit(solution)/shard_map/ppermute | solution.py:32
  60.0 1.3 multiply_reduce_fusion
  63.0 19.7 %all_to_all.24 = f32[16,1,136]{2,1,0:T(1,128)S(1)} all-to-all(f32[16,1,136]{2,1,0:T(1,128)S(1)} %reshape.99), channel_id=1, replica_groups=mesh['mem'=16,'lat'=16] {'lat'}, dimensions={0} | all-to-all | bytes 17408 | tf_op jit(solution)/shard_map/all_to_all | solution.py:105
  84.7 3.8 %all-to-all-start.2 = ((f32[16,1,8]{2,1,0:T(1,128)}), f32[16,1,8]{2,1,0:T(1,128)S(1)}, u32[]{:S(2)}, u32[]{:S(2)}) async-start(f32[16,1,8]{2,1,0:T(1,128)} %copy.66), calls=%async_computation.2 | async-start | bytes 16384 | tf_op jit(solution)/shard_map/all_to_all | solution.py:108
  89.6 2.8 %collective-permute-start = (f32[4,8,4096]{2,1,0:T(8,128)}, f32[4,8,4096]{2,1,0:T(8,128)}, u32[]{:S(2)}, u32[]{:S(2)}) collective-permute-start(f32[4,8,4096]{2,1,0:T(8,128)} %get-tuple-element.34), channel_id=1, source_target_pairs={{0,1},{1,2},{2,3},{3,4},{4,5},{5,6},{6,7},{7,8},{8,9},{9,10},{10,1... | collective-permute-start | bytes 1572872 | tf_op jit(solution)/shard_map/ppermute | solution.py:32
  92.4 2.3 %collective-permute-start.6 = (f32[4,8,4096]{2,1,0:T(8,128)}, f32[4,8,4096]{2,1,0:T(8,128)}, u32[]{:S(2)}, u32[]{:S(2)}) collective-permute-start(f32[4,8,4096]{2,1,0:T(8,128)} %get-tuple-element.35), channel_id=1, source_target_pairs={{1,0},{2,1},{3,2},{4,3},{5,4},{6,5},{7,6},{8,7},{9,8},{10,9},{11,1... | collective-permute-start | bytes 1572872 | tf_op jit(solution)/shard_map/ppermute | solution.py:32
  94.8 2.4 %all-to-all-done.2 = f32[16,1,8]{2,1,0:T(1,128)S(1)} async-done(((f32[16,1,8]{2,1,0:T(1,128)}), f32[16,1,8]{2,1,0:T(1,128)S(1)}, u32[]{:S(2)}, u32[]{:S(2)}) %all-to-all-start.2) | async-done | bytes 544 | tf_op jit(solution)/shard_map/all_to_all | solution.py:108
  97.2 6.7 %all-to-all-start.3 = ((f32[16,4,16,256]{3,2,1,0:T(8,128)}), f32[16,4,16,256]{3,2,1,0:T(8,128)S(1)}, u32[]{:S(2)}, u32[]{:S(2)}) async-start(f32[16,4,16,256]{3,2,1,0:T(8,128)} %get-tuple-element.23), calls=%async_computation.3 | async-start | bytes 2097152 | tf_op jit(solution)/shard_map/all_to_all | solution.py:111
  106.4 23.2 %all-to-all-done.3 = f32[16,4,16,256]{3,2,1,0:T(8,128)S(1)} async-done(((f32[16,4,16,256]{3,2,1,0:T(8,128)}), f32[16,4,16,256]{3,2,1,0:T(8,128)S(1)}, u32[]{:S(2)}, u32[]{:S(2)}) %all-to-all-start.3) | async-done | bytes 1048608 | tf_op jit(solution)/shard_map/all_to_all | solution.py:111
  129.6 8.3 %collective-permute-start.5 = (f32[16,4,8,256]{3,2,1,0:T(8,128)S(1)}, f32[16,4,8,256]{3,2,1,0:T(8,128)S(1)}, u32[]{:S(2)}, u32[]{:S(2)}) collective-permute-start(f32[16,4,8,256]{3,2,1,0:T(8,128)S(1)} %get-tuple-element.32), channel_id=1, source_target_pairs={{0,1},{1,2},{2,3},{3,4},{4,5},{5,6},{6,7},{7,8},{8,9},{9,10},{10,1... | collective-permute-start | bytes 1572872 | tf_op jit(solution)/shard_map/ppermute | solution.py:32
  138.1 2.1 %collective-permute-start.7 = (f32[16,4,8,256]{3,2,1,0:T(8,128)S(1)}, f32[16,4,8,256]{3,2,1,0:T(8,128)S(1)}, u32[]{:S(2)}, u32[]{:S(2)}) collective-permute-start(f32[16,4,8,256]{3,2,1,0:T(8,128)S(1)} %get-tuple-element.33), channel_id=1, source_target_pairs={{1,0},{2,1},{3,2},{4,3},{5,4},{6,5},{7,6},{8,7},{9,8},{10,9},{11,1... | collective-permute-start | bytes 1572872 | tf_op jit(solution)/shard_map/ppermute | solution.py:32
  140.4 3.7 %collective-permute-done.5 = f32[16,4,8,256]{3,2,1,0:T(8,128)S(1)} collective-permute-done((f32[16,4,8,256]{3,2,1,0:T(8,128)S(1)}, f32[16,4,8,256]{3,2,1,0:T(8,128)S(1)}, u32[]{:S(2)}, u32[]{:S(2)}) %collective-permute-start.5) | collective-permute-done | bytes 524320 | tf_op jit(solution)/shard_map/ppermute | solution.py:32
  144.1 7.1 %collective-permute-done.7 = f32[16,4,8,256]{3,2,1,0:T(8,128)S(1)} collective-permute-done((f32[16,4,8,256]{3,2,1,0:T(8,128)S(1)}, f32[16,4,8,256]{3,2,1,0:T(8,128)S(1)}, u32[]{:S(2)}, u32[]{:S(2)}) %collective-permute-start.7) | collective-permute-done | bytes 524320 | tf_op jit(solution)/shard_map/ppermute | solution.py:32
  151.3 1.1 multiply_add_fusion.2
  152.4 1.1 multiply_add_fusion.1
  (188 shorter events, 26.3 us)
Async XLA Ops:
  0.6 19.2 %copy-start.1 = (f32[1,4,16,4096]{3,2,1,0:T(8,128)S(1)}, f32[1,4,16,4096]{3,2,1,0:T(8,128)}, u32[]{:S(2)}) copy-start(f32[1,4,16,4096]{3,2,1,0:T(8,128)} %param.4) | copy-start | bytes 3145732
  2.0 11.0 %collective-permute-start.1 = (f32[4,8,4096]{2,1,0:T(8,128)S(1)}, f32[4,8,4096]{2,1,0:T(8,128)S(1)}, u32[]{:S(2)}, u32[]{:S(2)}) collective-permute-start(f32[4,8,4096]{2,1,0:T(8,128)S(1)} %get-tuple-element.36), channel_id=1, source_target_pairs={{0,1},{1,2},{2,3},{3,4},{4,5},{5,6},{6,7},{7,8},{8,9},{9,10},{10,1... | collective-permute-start | bytes 1572872 | tf_op jit(solution)/shard_map/ppermute | solution.py:32
  6.9 12.9 %collective-permute-start.2 = (f32[4,8,4096]{2,1,0:T(8,128)S(1)}, f32[4,8,4096]{2,1,0:T(8,128)S(1)}, u32[]{:S(2)}, u32[]{:S(2)}) collective-permute-start(f32[4,8,4096]{2,1,0:T(8,128)S(1)} %get-tuple-element.37), channel_id=1, source_target_pairs={{1,0},{2,1},{3,2},{4,3},{5,4},{6,5},{7,6},{8,7},{9,8},{10,9},{11,1... | collective-permute-start | bytes 1572872 | tf_op jit(solution)/shard_map/ppermute | solution.py:32
  9.0 12.1 %copy-start.14 = (f32[28]{0:T(128)}, f32[28]{0:T(128)S(1)}, u32[]{:S(2)}) copy-start(f32[28]{0:T(128)S(1)} %slice.748) | copy-start | bytes 340
  9.2 13.1 %copy-start.20 = (f32[26]{0:T(128)}, f32[26]{0:T(128)S(1)}, u32[]{:S(2)}) copy-start(f32[26]{0:T(128)S(1)} %slice.758) | copy-start | bytes 316
  9.3 13.9 %copy-start.10 = (f32[24]{0:T(128)}, f32[24]{0:T(128)S(1)}, u32[]{:S(2)}) copy-start(f32[24]{0:T(128)S(1)} %slice.767) | copy-start | bytes 292
  9.4 14.8 %copy-start.18 = (f32[22]{0:T(128)}, f32[22]{0:T(128)S(1)}, u32[]{:S(2)}) copy-start(f32[22]{0:T(128)S(1)} %slice.777) | copy-start | bytes 268
  9.5 15.6 %copy-start.6 = (f32[20]{0:T(128)}, f32[20]{0:T(128)S(1)}, u32[]{:S(2)}) copy-start(f32[20]{0:T(128)S(1)} %slice.786) | copy-start | bytes 244
  9.6 15.9 %copy-start.4 = (f32[16]{0:T(128)}, f32[16]{0:T(128)S(1)}, u32[]{:S(2)}) copy-start(f32[16]{0:T(128)S(1)} %slice.991) | copy-start | bytes 196
  9.8 13.3 %copy-start.12 = (f32[24]{0:T(128)}, f32[24]{0:T(128)S(1)}, u32[]{:S(2)}) copy-start(f32[24]{0:T(128)S(1)} %slice.761) | copy-start | bytes 292
  10.0 15.1 %copy-start.8 = (f32[20]{0:T(128)}, f32[20]{0:T(128)S(1)}, u32[]{:S(2)}) copy-start(f32[20]{0:T(128)S(1)} %slice.780) | copy-start | bytes 244
  26.7 16.4 %copy-start.26 = (s32[16]{0:T(128)S(1)}, s32[16]{0:T(128)}, u32[]{:S(2)}) copy-start(s32[16]{0:T(128)} %param.7) | copy-start | bytes 196
  27.8 31.6 %all-to-all-start = ((f32[16,4,16,256]{3,2,1,0:T(8,128)}), f32[16,4,16,256]{3,2,1,0:T(8,128)S(1)}, u32[]{:S(2)}, u32[]{:S(2)}) async-start(f32[16,4,16,256]{3,2,1,0:T(8,128)} %maximum_bitcast_fusion), calls=%async_computation | async-start | bytes 2097152 | tf_op jit(solution)/shard_map/all_to_all | solution.py:96
  38.8 10.0 %collective-permute-start.3 = (s32[8,32]{1,0:T(8,128)S(1)}, s32[8,32]{1,0:T(8,128)S(1)}, u32[]{:S(2)}, u32[]{:S(2)}) collective-permute-start(s32[8,32]{1,0:T(8,128)S(1)} %get-tuple-element.134), channel_id=1, source_target_pairs={{0,1},{1,2},{2,3},{3,4},{4,5},{5,6},{6,7},{7,8},{8,9},{9,10},{10,1... | collective-permute-start | bytes 3080 | tf_op jit(solution)/shard_map/ppermute | solution.py:32
  40.8 17.5 %collective-permute-start.4 = (s32[8,32]{1,0:T(8,128)S(1)}, s32[8,32]{1,0:T(8,128)S(1)}, u32[]{:S(2)}, u32[]{:S(2)}) collective-permute-start(s32[8,32]{1,0:T(8,128)S(1)} %get-tuple-element.135), channel_id=1, source_target_pairs={{1,0},{2,1},{3,2},{4,3},{5,4},{6,5},{7,6},{8,7},{9,8},{10,9},{11,1... | collective-permute-start | bytes 3080 | tf_op jit(solution)/shard_map/ppermute | solution.py:32
  43.1 16.2 %copy-start.24 = (s32[8]{0:T(128)}, s32[8]{0:T(128)S(1)}, u32[]{:S(2)}) copy-start(s32[8]{0:T(128)S(1)} %iota_add_fusion) | copy-start | bytes 100
  60.0 28.5 %copy-start = (f32[4,16,4096]{2,1,0:T(8,128)S(1)}, f32[4,16,4096]{2,1,0:T(8,128)}, u32[]{:S(2)}) copy-start(f32[4,16,4096]{2,1,0:T(8,128)} %param.5) | copy-start | bytes 3145732
  84.7 12.5 %all-to-all-start.2 = ((f32[16,1,8]{2,1,0:T(1,128)}), f32[16,1,8]{2,1,0:T(1,128)S(1)}, u32[]{:S(2)}, u32[]{:S(2)}) async-start(f32[16,1,8]{2,1,0:T(1,128)} %copy.66), calls=%async_computation.2 | async-start | bytes 16384 | tf_op jit(solution)/shard_map/all_to_all | solution.py:108
  88.5 15.6 %copy-start.25 = (s32[8]{0:T(128)S(1)}, s32[8]{0:T(128)}, u32[]{:S(2)}) copy-start(s32[8]{0:T(128)} %copy-done.24) | copy-start | bytes 100
  89.6 61.6 %collective-permute-start = (f32[4,8,4096]{2,1,0:T(8,128)}, f32[4,8,4096]{2,1,0:T(8,128)}, u32[]{:S(2)}, u32[]{:S(2)}) collective-permute-start(f32[4,8,4096]{2,1,0:T(8,128)} %get-tuple-element.34), channel_id=1, source_target_pairs={{0,1},{1,2},{2,3},{3,4},{4,5},{5,6},{6,7},{7,8},{8,9},{9,10},{10,1... | collective-permute-start | bytes 1572872 | tf_op jit(solution)/shard_map/ppermute | solution.py:32
  92.4 60.0 %collective-permute-start.6 = (f32[4,8,4096]{2,1,0:T(8,128)}, f32[4,8,4096]{2,1,0:T(8,128)}, u32[]{:S(2)}, u32[]{:S(2)}) collective-permute-start(f32[4,8,4096]{2,1,0:T(8,128)} %get-tuple-element.35), channel_id=1, source_target_pairs={{1,0},{2,1},{3,2},{4,3},{5,4},{6,5},{7,6},{8,7},{9,8},{10,9},{11,1... | collective-permute-start | bytes 1572872 | tf_op jit(solution)/shard_map/ppermute | solution.py:32
  97.2 32.3 %all-to-all-start.3 = ((f32[16,4,16,256]{3,2,1,0:T(8,128)}), f32[16,4,16,256]{3,2,1,0:T(8,128)S(1)}, u32[]{:S(2)}, u32[]{:S(2)}) async-start(f32[16,4,16,256]{3,2,1,0:T(8,128)} %get-tuple-element.23), calls=%async_computation.3 | async-start | bytes 2097152 | tf_op jit(solution)/shard_map/all_to_all | solution.py:111
  129.6 14.5 %collective-permute-start.5 = (f32[16,4,8,256]{3,2,1,0:T(8,128)S(1)}, f32[16,4,8,256]{3,2,1,0:T(8,128)S(1)}, u32[]{:S(2)}, u32[]{:S(2)}) collective-permute-start(f32[16,4,8,256]{3,2,1,0:T(8,128)S(1)} %get-tuple-element.32), channel_id=1, source_target_pairs={{0,1},{1,2},{2,3},{3,4},{4,5},{5,6},{6,7},{7,8},{8,9},{9,10},{10,1... | collective-permute-start | bytes 1572872 | tf_op jit(solution)/shard_map/ppermute | solution.py:32
  138.1 13.1 %collective-permute-start.7 = (f32[16,4,8,256]{3,2,1,0:T(8,128)S(1)}, f32[16,4,8,256]{3,2,1,0:T(8,128)S(1)}, u32[]{:S(2)}, u32[]{:S(2)}) collective-permute-start(f32[16,4,8,256]{3,2,1,0:T(8,128)S(1)} %get-tuple-element.33), channel_id=1, source_target_pairs={{1,0},{2,1},{3,2},{4,3},{5,4},{6,5},{7,6},{8,7},{9,8},{10,9},{11,1... | collective-permute-start | bytes 1572872 | tf_op jit(solution)/shard_map/ppermute | solution.py:32
  (14 other events, 52.5 us)

commit v2 on v1

v2 whole, which is shorter than its diff:
```python
import functools

import jax
import jax.numpy as jnp
from jax import lax
from jax.experimental import pallas as pl
from jax.experimental.pallas import tpu as pltpu
from jax.sharding import PartitionSpec as P

TILE = 128
REGIONS = 8
STEPS = 3
STRIP = 8

grav_coef = 0.1
depth_coef = 0.1
advect_coef = 0.05
diffuse_coef = 0.05
coriolis_coef = 0.05
target_size = 0.5
small_eps = 1e-06

VMEM = pl.BlockSpec(memory_space=pltpu.VMEM)
SMEM = pl.BlockSpec(memory_space=pltpu.SMEM)


def east(field):
    return pltpu.roll(field, field.shape[1] - 1, 1)


def west(field):
    return pltpu.roll(field, 1, 1)


def pack_edges(h, u, v, q, label_row):
    last, first = slice(8, 16), slice(0, 8)
    up = jnp.concatenate(
        [v[last], label_row(15), h[9:16], q[13:16], u[11:16]], axis=0
    )
    down = jnp.concatenate(
        [v[first], h[0:7], label_row(0), u[0:5], q[0:3]], axis=0
    )
    return up, down


def flow_kernel(total_rows, chunks, where_ref, mid_ref, before_ref, after_ref, out_ref, *state):
    hs, us, vs, qs, h1s = state
    lat = where_ref[0]
    last = where_ref[1]
    local_rows = mid_ref.shape[1]
    width = mid_ref.shape[2]
    strips = local_rows // STRIP + 2
    pad = STRIP

    def rows(s, shift=0):
        return pl.ds(pad + STRIP * s + shift, STRIP)

    zero = jnp.zeros((STRIP, width), jnp.float32)
    for ref in (hs, us, vs, qs, h1s):
        ref[0:pad, :] = zero
        ref[pad + STRIP * strips :, :] = zero
    for ref, field in ((hs, 0), (us, 1), (vs, 2), (qs, 3)):
        ref[pad + STRIP : pad + STRIP * (strips - 1), :] = mid_ref[field]
    for s, edge in ((0, before_ref), (strips - 1, after_ref)):
        vs[rows(s), :] = edge[0:8, :]
        hs[rows(s), :] = edge[8:16, :]
        us[rows(s), :] = edge[16:24, :]
    qs[rows(0), :] = pltpu.roll(before_ref[16:24, :], 5, 0)
    qs[rows(strips - 1), :] = pltpu.roll(after_ref[16:24, :], 3, 0)

    inside = [None] * strips
    inside[0] = jnp.where(lat > 0, 1.0, 0.0).astype(jnp.float32)
    inside[-1] = jnp.where(lat < last, 1.0, 0.0).astype(jnp.float32)

    def kept(value, s):
        return value if inside[s] is None else value * inside[s]

    lane_rows = lax.broadcasted_iota(jnp.int32, (STRIP, width), 0)

    def coriolis(s):
        row = (lane_rows + (lat * local_rows + STRIP * (s - 1))).astype(jnp.float32)
        return coriolis_coef * (2.0 * (row + 0.5) / total_rows - 1.0)

    for k in range(STEPS):
        final = k == STEPS - 1
        for s in range(strips):
            u = us[rows(s), :]
            h1s[rows(s), :] = kept(
                hs[rows(s), :]
                - depth_coef
                * ((east(u) - west(u)) + (vs[rows(s, 1), :] - vs[rows(s, -1), :])),
                s,
            )
        carried = qs[rows(0, -1), :]
        for s in range(1, strips - 1) if final else range(strips):
            f = coriolis(s)
            h1 = h1s[rows(s), :]
            v = vs[rows(s), :]
            u1 = us[rows(s), :] + f * v - grav_coef * (east(h1) - west(h1))
            v1 = v - f * u1 - grav_coef * (h1s[rows(s, 1), :] - h1s[rows(s, -1), :])
            q = qs[rows(s), :]
            if final:
                south = qs[rows(s, -1), :]
            else:
                south = carried
                if s < strips - 1:
                    carried = qs[rows(s + 1, -1), :]
            north = qs[rows(s, 1), :]
            e, w = east(q), west(q)
            q1 = (
                q
                - advect_coef * (u1 * (e - w) + v1 * (north - south))
                + diffuse_coef * ((e + w) + (north + south) - 4.0 * q)
            )
            if not final:
                us[rows(s), :] = kept(u1, s)
                vs[rows(s), :] = kept(v1, s)
                qs[rows(s), :] = kept(q1, s)
                hs[rows(s), :] = h1
            else:
                at = slice(STRIP * (s - 1), STRIP * s)
                for field, value in enumerate((h1, u1, v1, q1)):
                    if chunks == 1:
                        out_ref[field, at, :] = value
                    else:
                        size = width // chunks
                        for c in range(chunks):
                            out_ref[c, field, at, :] = value[:, c * size : (c + 1) * size]


def flow(where, middle, before, after, total_rows, chunks, name):
    fields, local_rows, width = middle.shape
    shape = (fields, local_rows, width)
    if chunks > 1:
        shape = (chunks, fields, local_rows, width // chunks)
    state = pltpu.VMEM((local_rows + 4 * STRIP, width), jnp.float32)
    return pl.pallas_call(
        functools.partial(flow_kernel, total_rows, chunks),
        out_shape=jax.ShapeDtypeStruct(shape, jnp.float32),
        in_specs=[SMEM, VMEM, VMEM, VMEM],
        out_specs=VMEM,
        scratch_shapes=[state] * 5,
        compiler_params=pltpu.CompilerParams(vmem_limit_bytes=24 << 20),
        cost_estimate=pl.CostEstimate(
            flops=60 * 10 * STRIP * width, bytes_accessed=1 << 22, transcendentals=0
        ),
        name=name,
    )(where, middle, before, after)


def pair_kernel(pairing_ref, all_ref, spread_ref):
    for m in range(all_ref.shape[0]):
        spread_ref[m] = 0.5 * (all_ref[m] - all_ref[pairing_ref[m]])


def pair_spread(pairing, everyone):
    return pl.pallas_call(
        pair_kernel,
        out_shape=jax.ShapeDtypeStruct(everyone.shape, jnp.float32),
        in_specs=[SMEM, VMEM],
        out_specs=VMEM,
        compiler_params=pltpu.CompilerParams(vmem_limit_bytes=8 << 20),
        cost_estimate=pl.CostEstimate(flops=1 << 19, bytes_accessed=3 << 20, transcendentals=0),
        name="pair_spread",
    )(pairing, everyone)


def region_kernel(spread_ref, labels_ref, out_ref):
    members = spread_ref.shape[0]
    local_rows = spread_ref.shape[2]
    lane = lax.broadcasted_iota(jnp.int32, (REGIONS, TILE), 1)

    def folded(x):
        x = x[:STRIP] + x[STRIP:]
        return x[:, :TILE] + x[:, TILE:]

    here = labels_ref[1]
    weights, counts = [], []
    for r in range(REGIONS):
        code = float(r + 1)

        def is_r(x):
            return jnp.where(x == code, 1.0, 0.0).astype(jnp.float32)

        own = is_r(here)
        counts.append(jnp.sum(folded(own), axis=0, keepdims=True))
        weights.append(0.125 * (is_r(labels_ref[0]) + 2.0 * own + is_r(labels_ref[2])))

    def placed(rows, at, total):
        column = jnp.sum(jnp.concatenate(rows, axis=0), axis=1, keepdims=True)
        return jnp.where(lane == at, column, total)

    total = placed(counts, members, jnp.zeros((REGIONS, TILE), jnp.float32))
    for m in range(members):
        square = None
        for field in range(spread_ref.shape[1]):
            x = spread_ref[m, field]
            square = x * x if square is None else square + x * x
        total = placed(
            [jnp.sum(folded(square * w), axis=0, keepdims=True) for w in weights], m, total
        )
    out_ref[...] = total


def region_share(spread, labels):
    return pl.pallas_call(
        region_kernel,
        out_shape=jax.ShapeDtypeStruct((REGIONS, TILE), jnp.float32),
        in_specs=[VMEM, VMEM],
        out_specs=VMEM,
        compiler_params=pltpu.CompilerParams(vmem_limit_bytes=8 << 20),
        cost_estimate=pl.CostEstimate(flops=1 << 20, bytes_accessed=1 << 20, transcendentals=0),
        name="region_share",
    )(spread, labels)


def recentre_kernel(factor_ref, labels_ref, analysis_ref, back_ref, mid_ref, up_ref, down_ref):
    chunks, fields, local_rows, size = back_ref.shape
    labels = labels_ref[...]
    factor = factor_ref[...]
    scale = jnp.zeros(labels.shape, jnp.float32)
    for r in range(REGIONS):
        scale = jnp.where(labels == float(r + 1), factor[r : r + 1, :], scale)
    for c in range(chunks):
        at = slice(c * size, (c + 1) * size)
        wide = jnp.concatenate(
            [
                jnp.broadcast_to(scale[:, t : t + 1], (local_rows, TILE))
                for t in range(c * size // TILE, (c + 1) * size // TILE)
            ],
            axis=1,
        )
        h, u, v, q = [analysis_ref[i, :, at] + wide * back_ref[c, i] for i in range(fields)]
        for i, value in enumerate((h, u, v, q)):
            mid_ref[i, :, at] = value
        row = lax.broadcasted_iota(jnp.int32, (STRIP, size), 0)
        up_ref[0:8, at] = v[8:16]
        up_ref[8:16, at] = h[8:16]
        up_ref[16:24, at] = jnp.where(row < 3, pltpu.roll(q[8:16], 3, 0), u[8:16])
        down_ref[0:8, at] = v[0:8]
        down_ref[8:16, at] = h[0:8]
        down_ref[16:24, at] = jnp.where(row >= 5, pltpu.roll(q[0:8], 5, 0), u[0:8])


def recentre(factor, labels, analysis, back):
    fields, local_rows, width = analysis.shape
    edge = jax.ShapeDtypeStruct((3 * STRIP, width), jnp.float32)
    return pl.pallas_call(
        recentre_kernel,
        out_shape=(jax.ShapeDtypeStruct(analysis.shape, jnp.float32), edge, edge),
        in_specs=[VMEM] * 4,
        out_specs=(VMEM,) * 3,
        compiler_params=pltpu.CompilerParams(vmem_limit_bytes=12 << 20),
        cost_estimate=pl.CostEstimate(flops=1 << 20, bytes_accessed=4 << 20, transcendentals=0),
        name="recentre",
    )(factor, labels, analysis, back)


def all_sum(value):
    for axis in ("lat", "mem"):
        size = lax.axis_size(axis)
        for stride in (1, 4):
            others = [
                lax.ppermute(value, axis, [(i, i ^ (d * stride)) for i in range(size)])
                for d in (1, 2, 3)
            ]
            value = (value + others[0]) + (others[1] + others[2])
    return value


def local(replica_variables, analysis, labels, pairing):
    members = lax.axis_size("mem")
    lat_size = lax.axis_size("lat")
    lat = lax.axis_index("lat")
    member = lax.axis_index("mem")
    x = replica_variables[0]
    fields, local_rows, width = x.shape
    chunk = width // members
    tiles = chunk // TILE
    total_rows = float(local_rows * lat_size)
    where = jnp.stack([lat, jnp.int32(lat_size - 1)]).astype(jnp.int32)
    up = [(i, i + 1) for i in range(lat_size - 1)]
    down = [(j, i) for i, j in up]

    coded = (labels + 1).astype(jnp.float32)
    wide = jnp.pad(coded, ((0, 0), (0, width - coded.shape[1])))
    last, first = pack_edges(x[0], x[1], x[2], x[3], lambda i: wide[i : i + 1])
    before = lax.ppermute(last, "lat", up)
    after = lax.ppermute(first, "lat", down)
    pieces = flow(where, x, before, after, total_rows, members, "first_flow")
    everyone = lax.all_to_all(pieces, "mem", 0, 0, tiled=True)

    tile_count = coded.shape[1]
    rows = jnp.concatenate([before[8:9, :tile_count], coded, after[15:16, :tile_count]], axis=0)
    own = lax.dynamic_slice_in_dim(rows, member * tiles, tiles, axis=1)
    own = jnp.repeat(own, TILE, axis=1)
    own = jnp.stack([own[:-2], own[1:-1], own[2:]])

    spread = pair_spread(pairing, everyone)
    back = lax.all_to_all(spread, "mem", 0, 0, tiled=True)
    sums = all_sum(region_share(spread, own))
    region_sum = lax.dynamic_slice_in_dim(sums, member, 1, axis=1)
    cells = sums[:, members : members + 1]
    factor = target_size / jnp.sqrt(region_sum / cells + small_eps)

    lane_labels = jnp.pad(coded, ((0, 0), (0, TILE - tile_count)))
    middle, last, first = recentre(
        jnp.broadcast_to(factor, (REGIONS, TILE)), lane_labels, analysis, back
    )
    before = lax.ppermute(last, "lat", up)
    after = lax.ppermute(first, "lat", down)
    closing = flow(where, middle, before, after, total_rows, 1, "closing_flow")
    return closing[None], factor.reshape(1, REGIONS)


def solution(mesh):
    return jax.shard_map(
        local,
        mesh=mesh,
        in_specs=(P("mem", None, "lat", None), P(None, "lat", None), P("lat", None), P()),
        out_specs=(P("mem", None, "lat", None), P("mem", None)),
        check_vma=False,
    )
```

time: 163 us -> 139 us (0.85)
  waiting for transfers between devices: 61.4 us -> 40.7 us
  other arithmetic: 15.1 us -> 0.38 us
  Pallas kernels: 0 us -> 11.8 us
  local copies, waits for them, and re-layouts: 15.6 us -> 4.83 us
  blocking collectives: 19.7 us -> 29.6 us
  starting transfers between devices: 48.1 us -> 50 us
    all_to_all x1, waiting for transfers between devices: 23.2 us -> 0.01 us  [local(): back = lax.all_to_all(spread, 'mem', 0, 0, tiled=True)]
    ppermute x8 -> x16, starting transfers between devices: 26.7 us -> 43.1 us  [the longest x12 27.5 us: all_sum(): lax.ppermute(value, axis, [(i, i ^ d * stride) for i in range(size)])]
    all_to_all x2 -> x0, starting transfers between devices: 14.8 us -> none  [the longest x1 10.9 us: local(): everyone = lax.all_to_all(pieces, 'mem', 0, 0, tiled=True)]
    pallas_call x0 -> x5, Pallas kernels: none -> 11.8 us  [the longest x2 8.29 us: flow(): pl.pallas_call(functools.partial(flow_kernel, total_rows, chunks), out_sh...]
    all_to_all x1, blocking collectives: 19.7 us -> 29.6 us  [local(): everyone = lax.all_to_all(pieces, 'mem', 0, 0, tiled=True)]
    mul x17 -> x0, other arithmetic: 5.38 us -> none  [the longest x4 2.81 us: step(): (qc - advect_coef * (u1 * (qe - qw) + v1 * (qn - qs)) + diffuse_coef * (q...]
    slice x56 -> x8, local copies, waits for them, and re-layouts: 8.25 us -> 3.12 us  [the longest x1 1.08 us: pack_edges(): q[0:3]]
    ppermute x8 -> x16, waiting for transfers between devices: 35.8 us -> 40.7 us  [the longest x12 22.4 us: all_sum(): lax.ppermute(value, axis, [(i, i ^ d * stride) for i in range(size)])]
  transfers between devices with their start and end apart: 11 -> 17, of which waited for: 8 -> 10; matrix products, arithmetic and copies ran while one was open for 4% -> 1% of each run, Pallas kernels for 0% -> 1%
where the time goes in v2:
time: 139 us; the launch traced here: 138 us
  starting transfers between devices  50 us (36%)
  waiting for transfers between devices  40.7 us (29%)
  blocking collectives  29.6 us (21%)
  Pallas kernels  11.8 us (8%)
  local copies, waits for them, and re-layouts  4.83 us (3%)
    all_to_all x1, blocking collectives, local(): everyone = lax.all_to_all(pieces, 'mem', 0, 0, tiled=True)  29.6 us
    ppermute x12, starting transfers between devices, all_sum(): lax.ppermute(value, axis, [(i, i ^ d * stride) for i in range(size)])  27.5 us
    ppermute x12, waiting for transfers between devices, all_sum(): lax.ppermute(value, axis, [(i, i ^ d * stride) for i in range(size)])  22.4 us
    ppermute x2, waiting for transfers between devices, local(): after = lax.ppermute(first, 'lat', down)  13.9 us
    ppermute x2, starting transfers between devices, local(): before = lax.ppermute(last, 'lat', up)  10.9 us
    pallas_call x2, Pallas kernels, flow(): pl.pallas_call(functools.partial(flow_kernel, total_rows, chunks), out_sh...  8.29 us
    all_to_all x1, starting transfers between devices, local(): back = lax.all_to_all(spread, 'mem', 0, 0, tiled=True)  6.9 us
    ppermute x2, starting transfers between devices, local(): after = lax.ppermute(first, 'lat', down)  4.8 us
  transfers between devices with their start and end apart: 17, of which 10 were waited for; matrix products, arithmetic and copies ran while one was open for 1% of the time, Pallas kernels for 1%

profile of v2, /device:TPU:1, one launch (start us, length us, event | category | flops | bytes accessed | tf_op | source)
XLA Modules:
  0.0 138.3 jit_solution(10386194969575883318)
XLA Ops:
  4.6 4.9 %collective-permute-start = (f32[24,4096]{1,0:T(8,128)S(1)}, f32[24,4096]{1,0:T(8,128)S(1)}, u32[]{:S(2)}, u32[]{:S(2)}) collective-permute-start(f32[24,4096]{1,0:T(8,128)S(1)} %concatenate.9), channel_id=1, source_target_pairs={{0,1},{1,2},{2,3},{3,4},{4,5},{5,6},{6,7},{7,8},{8,9},{9,10},{10,1... | collective-permute-start | bytes 1179656 | tf_op jit(solution)/shard_map/ppermute | solution.py:288
  9.6 1.9 %collective-permute-start.1 = (f32[24,4096]{1,0:T(8,128)S(1)}, f32[24,4096]{1,0:T(8,128)S(1)}, u32[]{:S(2)}, u32[]{:S(2)}) collective-permute-start(f32[24,4096]{1,0:T(8,128)S(1)} %concatenate.10), channel_id=1, source_target_pairs={{1,0},{2,1},{3,2},{4,3},{5,4},{6,5},{7,6},{8,7},{9,8},{10,9},{11,1... | collective-permute-start | bytes 1179656 | tf_op jit(solution)/shard_map/ppermute | solution.py:289
  11.6 2.6 %collective-permute-done.before_ref = f32[24,4096]{1,0:T(8,128)S(1)} collective-permute-done((f32[24,4096]{1,0:T(8,128)S(1)}, f32[24,4096]{1,0:T(8,128)S(1)}, u32[]{:S(2)}, u32[]{:S(2)}) %collective-permute-start) | collective-permute-done | bytes 393248 | tf_op jit(solution)/shard_map/ppermute | solution.py:288
  14.2 5.4 %collective-permute-done.1.after_ref = f32[24,4096]{1,0:T(8,128)S(1)} collective-permute-done((f32[24,4096]{1,0:T(8,128)S(1)}, f32[24,4096]{1,0:T(8,128)S(1)}, u32[]{:S(2)}, u32[]{:S(2)}) %collective-permute-start.1) | collective-permute-done | bytes 393248 | tf_op jit(solution)/shard_map/ppermute | solution.py:289
  19.6 3.6 %first_flow.1 = f32[16,4,16,256]{3,2,1,0:T(8,128)S(1)} custom-call(s32[2]{0:T(128)S(1)} %pad_add_fusion.where_ref, f32[4,16,4096]{2,1,0:T(8,128)S(1)} %bitcast.20, f32[24,4096]{1,0:T(8,128)S(1)} %collective-permute-done.before_ref, f32[24,4096]{1,0:T(8,128)S(1)} %collective-permute-done.1.after_ref), custom_call_target="tpu_custom_call" | custom-call | flops 19660800 | bytes 4194304 | tf_op jit(solution)/shard_map/first_flow/pallas_call | solution.py:137
  23.3 29.6 %all_to_all.10.all_ref = f32[16,4,16,256]{3,2,1,0:T(8,128)S(1)} all-to-all(f32[16,4,16,256]{3,2,1,0:T(8,128)S(1)} %first_flow.1), channel_id=1, replica_groups=mesh['mem'=16,'lat'=16] {'mem'}, dimensions={0} | all-to-all | bytes 2097152 | tf_op jit(solution)/shard_map/all_to_all | solution.py:291
  52.9 1.6 %pair_spread.1.spread_ref = f32[16,4,16,256]{3,2,1,0:T(8,128)} custom-call(s32[16]{0:T(128)S(1)} %copy-done.2, f32[16,4,16,256]{3,2,1,0:T(8,128)S(1)} %all_to_all.10.all_ref), custom_call_target="tpu_custom_call" | custom-call | flops 524288 | bytes 3145728 | tf_op jit(solution)/shard_map/pair_spread/pallas_call | solution.py:157
  54.5 6.9 %all-to-all-start.1 = ((f32[16,4,16,256]{3,2,1,0:T(8,128)}), f32[16,4,16,256]{3,2,1,0:T(8,128)S(1)}, u32[]{:S(2)}, u32[]{:S(2)}) async-start(f32[16,4,16,256]{3,2,1,0:T(8,128)} %pair_spread.1.spread_ref), calls=%async_computation.1 | async-start | bytes 2097152 | tf_op jit(solution)/shard_map/all_to_all | solution.py:300
  61.9 1.7 %region_share.1 = f32[8,128]{1,0:T(8,128)S(1)} custom-call(f32[16,4,16,256]{3,2,1,0:T(8,128)} %pair_spread.1.spread_ref, f32[3,16,256]{2,1,0:T(8,128)S(1)} %pad_maximum_fusion.labels_ref), custom_call_target="tpu_custom_call" | custom-call | flops 1048576 | bytes 1048576 | tf_op jit(solution)/shard_map/region_share/pallas_call | solution.py:206
  63.6 7.5 %collective-permute-start.4 = (f32[8,128]{1,0:T(8,128)S(1)}, f32[8,128]{1,0:T(8,128)S(1)}, u32[]{:S(2)}, u32[]{:S(2)}) collective-permute-start(f32[8,128]{1,0:T(8,128)S(1)} %region_share.1), channel_id=1, source_target_pairs={{0,3},{1,2},{2,1},{3,0},{4,7},{5,6},{6,5},{7,4},{8,11},{9,10},{10,... | collective-permute-start | bytes 12296 | tf_op jit(solution)/shard_map/ppermute | solution.py:264
  71.7 13.8 %collective-permute-done.4 = f32[8,128]{1,0:T(8,128)S(1)} collective-permute-done((f32[8,128]{1,0:T(8,128)S(1)}, f32[8,128]{1,0:T(8,128)S(1)}, u32[]{:S(2)}, u32[]{:S(2)}) %collective-permute-start.4) | collective-permute-done | bytes 4128 | tf_op jit(solution)/shard_map/ppermute | solution.py:264
  85.6 8.6 %collective-permute-start.6 = (f32[8,128]{1,0:T(8,128)S(1)}, f32[8,128]{1,0:T(8,128)S(1)}, u32[]{:S(2)}, u32[]{:S(2)}) collective-permute-start(f32[8,128]{1,0:T(8,128)S(1)} %add_add_fusion.3), channel_id=1, source_target_pairs={{0,8},{1,9},{2,10},{3,11},{4,12},{5,13},{6,14},{7,15},{8,0},{9,1},... | collective-permute-start | bytes 12296 | tf_op jit(solution)/shard_map/ppermute | solution.py:264
  95.1 1.5 %collective-permute-done.5 = f32[8,128]{1,0:T(8,128)S(1)} collective-permute-done((f32[8,128]{1,0:T(8,128)S(1)}, f32[8,128]{1,0:T(8,128)S(1)}, u32[]{:S(2)}, u32[]{:S(2)}) %collective-permute-start.5) | collective-permute-done | bytes 4128 | tf_op jit(solution)/shard_map/ppermute | solution.py:264
  97.8 4.7 %collective-permute-start.9 = (f32[8,128]{1,0:T(8,128)S(1)}, f32[8,128]{1,0:T(8,128)S(1)}, u32[]{:S(2)}, u32[]{:S(2)}) collective-permute-start(f32[8,128]{1,0:T(8,128)S(1)} %add_add_fusion.2), channel_id=1, source_target_pairs={{0,32},{16,48},{32,0},{48,16},{64,96},{80,112},{96,64},{112,80},{1... | collective-permute-start | bytes 12296 | tf_op jit(solution)/shard_map/ppermute | solution.py:264
  102.6 1.5 %collective-permute-done.9 = f32[8,128]{1,0:T(8,128)S(1)} collective-permute-done((f32[8,128]{1,0:T(8,128)S(1)}, f32[8,128]{1,0:T(8,128)S(1)}, u32[]{:S(2)}, u32[]{:S(2)}) %collective-permute-start.9) | collective-permute-done | bytes 4128 | tf_op jit(solution)/shard_map/ppermute | solution.py:264
  104.1 2.0 %collective-permute-done.8 = f32[8,128]{1,0:T(8,128)S(1)} collective-permute-done((f32[8,128]{1,0:T(8,128)S(1)}, f32[8,128]{1,0:T(8,128)S(1)}, u32[]{:S(2)}, u32[]{:S(2)}) %collective-permute-start.8) | collective-permute-done | bytes 4128 | tf_op jit(solution)/shard_map/ppermute | solution.py:264
  106.1 3.5 %collective-permute-start.13 = (f32[8,128]{1,0:T(8,128)S(1)}, f32[8,128]{1,0:T(8,128)S(1)}, u32[]{:S(2)}, u32[]{:S(2)}) collective-permute-start(f32[8,128]{1,0:T(8,128)S(1)} %add_add_fusion.1), channel_id=1, source_target_pairs={{0,192},{16,208},{32,224},{48,240},{64,128},{80,144},{96,160},{112... | collective-permute-start | bytes 12296 | tf_op jit(solution)/shard_map/ppermute | solution.py:264
  109.6 1.3 collective-permute-start.12
  110.9 2.6 %collective-permute-done.12 = f32[8,128]{1,0:T(8,128)S(1)} collective-permute-done((f32[8,128]{1,0:T(8,128)S(1)}, f32[8,128]{1,0:T(8,128)S(1)}, u32[]{:S(2)}, u32[]{:S(2)}) %collective-permute-start.12) | collective-permute-done | bytes 4128 | tf_op jit(solution)/shard_map/ppermute | solution.py:264
  114.5 5.9 %collective-permute-start.14 = (f32[24,4096]{1,0:T(8,128)S(1)}, f32[24,4096]{1,0:T(8,128)S(1)}, u32[]{:S(2)}, u32[]{:S(2)}) collective-permute-start(f32[24,4096]{1,0:T(8,128)S(1)} %get-tuple-element.6), channel_id=1, source_target_pairs={{0,1},{1,2},{2,3},{3,4},{4,5},{5,6},{6,7},{7,8},{8,9},{9,10},{10,1... | collective-permute-start | bytes 1179656 | tf_op jit(solution)/shard_map/ppermute | solution.py:310
  120.5 2.9 %collective-permute-start.15 = (f32[24,4096]{1,0:T(8,128)S(1)}, f32[24,4096]{1,0:T(8,128)S(1)}, u32[]{:S(2)}, u32[]{:S(2)}) collective-permute-start(f32[24,4096]{1,0:T(8,128)S(1)} %get-tuple-element.7), channel_id=1, source_target_pairs={{1,0},{2,1},{3,2},{4,3},{5,4},{6,5},{7,6},{8,7},{9,8},{10,9},{11,1... | collective-permute-start | bytes 1179656 | tf_op jit(solution)/shard_map/ppermute | solution.py:311
  123.3 1.8 %collective-permute-done.14.before_ref = f32[24,4096]{1,0:T(8,128)S(1)} collective-permute-done((f32[24,4096]{1,0:T(8,128)S(1)}, f32[24,4096]{1,0:T(8,128)S(1)}, u32[]{:S(2)}, u32[]{:S(2)}) %collective-permute-start.14) | collective-permute-done | bytes 393248 | tf_op jit(solution)/shard_map/ppermute | solution.py:310
  125.2 8.5 %collective-permute-done.15.after_ref = f32[24,4096]{1,0:T(8,128)S(1)} collective-permute-done((f32[24,4096]{1,0:T(8,128)S(1)}, f32[24,4096]{1,0:T(8,128)S(1)}, u32[]{:S(2)}, u32[]{:S(2)}) %collective-permute-start.15) | collective-permute-done | bytes 393248 | tf_op jit(solution)/shard_map/ppermute | solution.py:311
  133.6 4.6 %closing_flow.1 = f32[4,16,4096]{2,1,0:T(8,128)} custom-call(s32[2]{0:T(128)S(1)} %pad_add_fusion.where_ref, f32[4,16,4096]{2,1,0:T(8,128)S(1)} %get-tuple-element.5.mid_ref, f32[24,4096]{1,0:T(8,128)S(1)} %collective-permute-done.14.before_ref, f32[24,4096]{1,0:T(8,128)S(1)} %collective-permute-done.15.after_ref), custom_call_target="tpu_custom_call" | custom-call | flops 19660800 | bytes 4194304 | tf_op jit(solution)/shard_map/closing_flow/pallas_call | solution.py:137
  (53 shorter events, 8.3 us)
Async XLA Ops:
  0.6 3.1 %copy-start = (f32[1,4,16,4096]{3,2,1,0:T(8,128)S(1)}, f32[1,4,16,4096]{3,2,1,0:T(8,128)}, u32[]{:S(2)}) copy-start(f32[1,4,16,4096]{3,2,1,0:T(8,128)} %param.4) | copy-start | bytes 3145732
  3.7 0.7 copy-start.3
  4.6 9.6 %collective-permute-start = (f32[24,4096]{1,0:T(8,128)S(1)}, f32[24,4096]{1,0:T(8,128)S(1)}, u32[]{:S(2)}, u32[]{:S(2)}) collective-permute-start(f32[24,4096]{1,0:T(8,128)S(1)} %concatenate.9), channel_id=1, source_target_pairs={{0,1},{1,2},{2,3},{3,4},{4,5},{5,6},{6,7},{7,8},{8,9},{9,10},{10,1... | collective-permute-start | bytes 1179656 | tf_op jit(solution)/shard_map/ppermute | solution.py:288
  9.6 10.0 %collective-permute-start.1 = (f32[24,4096]{1,0:T(8,128)S(1)}, f32[24,4096]{1,0:T(8,128)S(1)}, u32[]{:S(2)}, u32[]{:S(2)}) collective-permute-start(f32[24,4096]{1,0:T(8,128)S(1)} %concatenate.10), channel_id=1, source_target_pairs={{1,0},{2,1},{3,2},{4,3},{5,4},{6,5},{7,6},{8,7},{9,8},{10,9},{11,1... | collective-permute-start | bytes 1179656 | tf_op jit(solution)/shard_map/ppermute | solution.py:289
  23.3 29.7 %copy-start.2 = (s32[16]{0:T(128)S(1)}, s32[16]{0:T(128)}, u32[]{:S(2)}) copy-start(s32[16]{0:T(128)} %pairing_ref.1) | copy-start | bytes 196
  54.5 59.2 %all-to-all-start.1 = ((f32[16,4,16,256]{3,2,1,0:T(8,128)}), f32[16,4,16,256]{3,2,1,0:T(8,128)S(1)}, u32[]{:S(2)}, u32[]{:S(2)}) async-start(f32[16,4,16,256]{3,2,1,0:T(8,128)} %pair_spread.1.spread_ref), calls=%async_computation.1 | async-start | bytes 2097152 | tf_op jit(solution)/shard_map/all_to_all | solution.py:300
  61.5 52.8 %copy-start.1 = (f32[4,16,4096]{2,1,0:T(8,128)S(1)}, f32[4,16,4096]{2,1,0:T(8,128)}, u32[]{:S(2)}) copy-start(f32[4,16,4096]{2,1,0:T(8,128)} %analysis_ref.1) | copy-start | bytes 3145732
  63.6 21.8 %collective-permute-start.4 = (f32[8,128]{1,0:T(8,128)S(1)}, f32[8,128]{1,0:T(8,128)S(1)}, u32[]{:S(2)}, u32[]{:S(2)}) collective-permute-start(f32[8,128]{1,0:T(8,128)S(1)} %region_share.1), channel_id=1, source_target_pairs={{0,3},{1,2},{2,1},{3,0},{4,7},{5,6},{6,5},{7,4},{8,11},{9,10},{10,... | collective-permute-start | bytes 12296 | tf_op jit(solution)/shard_map/ppermute | solution.py:264
  71.2 14.3 %collective-permute-start.3 = (f32[8,128]{1,0:T(8,128)S(1)}, f32[8,128]{1,0:T(8,128)S(1)}, u32[]{:S(2)}, u32[]{:S(2)}) collective-permute-start(f32[8,128]{1,0:T(8,128)S(1)} %region_share.1), channel_id=1, source_target_pairs={{0,2},{1,3},{2,0},{3,1},{4,6},{5,7},{6,4},{7,5},{8,10},{9,11},{10,... | collective-permute-start | bytes 12296 | tf_op jit(solution)/shard_map/ppermute | solution.py:264
  71.2 14.3 %collective-permute-start.2 = (f32[8,128]{1,0:T(8,128)S(1)}, f32[8,128]{1,0:T(8,128)S(1)}, u32[]{:S(2)}, u32[]{:S(2)}) collective-permute-start(f32[8,128]{1,0:T(8,128)S(1)} %region_share.1), channel_id=1, source_target_pairs={{0,1},{1,0},{2,3},{3,2},{4,5},{5,4},{6,7},{7,6},{8,9},{9,8},{10,11... | collective-permute-start | bytes 12296 | tf_op jit(solution)/shard_map/ppermute | solution.py:264
  85.5 8.7 %collective-permute-start.7 = (f32[8,128]{1,0:T(8,128)S(1)}, f32[8,128]{1,0:T(8,128)S(1)}, u32[]{:S(2)}, u32[]{:S(2)}) collective-permute-start(f32[8,128]{1,0:T(8,128)S(1)} %add_add_fusion.3), channel_id=1, source_target_pairs={{0,12},{1,13},{2,14},{3,15},{4,8},{5,9},{6,10},{7,11},{8,4},{9,5},... | collective-permute-start | bytes 12296 | tf_op jit(solution)/shard_map/ppermute | solution.py:264
  85.6 9.6 %collective-permute-start.6 = (f32[8,128]{1,0:T(8,128)S(1)}, f32[8,128]{1,0:T(8,128)S(1)}, u32[]{:S(2)}, u32[]{:S(2)}) collective-permute-start(f32[8,128]{1,0:T(8,128)S(1)} %add_add_fusion.3), channel_id=1, source_target_pairs={{0,8},{1,9},{2,10},{3,11},{4,12},{5,13},{6,14},{7,15},{8,0},{9,1},... | collective-permute-start | bytes 12296 | tf_op jit(solution)/shard_map/ppermute | solution.py:264
  94.2 2.5 %collective-permute-start.5 = (f32[8,128]{1,0:T(8,128)S(1)}, f32[8,128]{1,0:T(8,128)S(1)}, u32[]{:S(2)}, u32[]{:S(2)}) collective-permute-start(f32[8,128]{1,0:T(8,128)S(1)} %add_add_fusion.3), channel_id=1, source_target_pairs={{0,4},{1,5},{2,6},{3,7},{4,0},{5,1},{6,2},{7,3},{8,12},{9,13},{10,... | collective-permute-start | bytes 12296 | tf_op jit(solution)/shard_map/ppermute | solution.py:264
  96.6 6.0 %collective-permute-start.10 = (f32[8,128]{1,0:T(8,128)S(1)}, f32[8,128]{1,0:T(8,128)S(1)}, u32[]{:S(2)}, u32[]{:S(2)}) collective-permute-start(f32[8,128]{1,0:T(8,128)S(1)} %add_add_fusion.2), channel_id=1, source_target_pairs={{0,48},{16,32},{32,16},{48,0},{64,112},{80,96},{96,80},{112,64},{1... | collective-permute-start | bytes 12296 | tf_op jit(solution)/shard_map/ppermute | solution.py:264
  97.8 6.4 %collective-permute-start.9 = (f32[8,128]{1,0:T(8,128)S(1)}, f32[8,128]{1,0:T(8,128)S(1)}, u32[]{:S(2)}, u32[]{:S(2)}) collective-permute-start(f32[8,128]{1,0:T(8,128)S(1)} %add_add_fusion.2), channel_id=1, source_target_pairs={{0,32},{16,48},{32,0},{48,16},{64,96},{80,112},{96,64},{112,80},{1... | collective-permute-start | bytes 12296 | tf_op jit(solution)/shard_map/ppermute | solution.py:264
  102.4 3.7 %collective-permute-start.8 = (f32[8,128]{1,0:T(8,128)S(1)}, f32[8,128]{1,0:T(8,128)S(1)}, u32[]{:S(2)}, u32[]{:S(2)}) collective-permute-start(f32[8,128]{1,0:T(8,128)S(1)} %add_add_fusion.2), channel_id=1, source_target_pairs={{0,16},{16,0},{32,48},{48,32},{64,80},{80,64},{96,112},{112,96},{1... | collective-permute-start | bytes 12296 | tf_op jit(solution)/shard_map/ppermute | solution.py:264
  106.1 4.8 %collective-permute-start.13 = (f32[8,128]{1,0:T(8,128)S(1)}, f32[8,128]{1,0:T(8,128)S(1)}, u32[]{:S(2)}, u32[]{:S(2)}) collective-permute-start(f32[8,128]{1,0:T(8,128)S(1)} %add_add_fusion.1), channel_id=1, source_target_pairs={{0,192},{16,208},{32,224},{48,240},{64,128},{80,144},{96,160},{112... | collective-permute-start | bytes 12296 | tf_op jit(solution)/shard_map/ppermute | solution.py:264
  109.6 4.0 %collective-permute-start.12 = (f32[8,128]{1,0:T(8,128)S(1)}, f32[8,128]{1,0:T(8,128)S(1)}, u32[]{:S(2)}, u32[]{:S(2)}) collective-permute-start(f32[8,128]{1,0:T(8,128)S(1)} %add_add_fusion.1), channel_id=1, source_target_pairs={{0,128},{16,144},{32,160},{48,176},{64,192},{80,208},{96,224},{112... | collective-permute-start | bytes 12296 | tf_op jit(solution)/shard_map/ppermute | solution.py:264
  110.9 2.7 %collective-permute-start.11 = (f32[8,128]{1,0:T(8,128)S(1)}, f32[8,128]{1,0:T(8,128)S(1)}, u32[]{:S(2)}, u32[]{:S(2)}) collective-permute-start(f32[8,128]{1,0:T(8,128)S(1)} %add_add_fusion.1), channel_id=1, source_target_pairs={{0,64},{16,80},{32,96},{48,112},{64,0},{80,16},{96,32},{112,48},{1... | collective-permute-start | bytes 12296 | tf_op jit(solution)/shard_map/ppermute | solution.py:264
  113.8 0.5 copy-start.4
  114.5 10.6 %collective-permute-start.14 = (f32[24,4096]{1,0:T(8,128)S(1)}, f32[24,4096]{1,0:T(8,128)S(1)}, u32[]{:S(2)}, u32[]{:S(2)}) collective-permute-start(f32[24,4096]{1,0:T(8,128)S(1)} %get-tuple-element.6), channel_id=1, source_target_pairs={{0,1},{1,2},{2,3},{3,4},{4,5},{5,6},{6,7},{7,8},{8,9},{9,10},{10,1... | collective-permute-start | bytes 1179656 | tf_op jit(solution)/shard_map/ppermute | solution.py:310
  120.5 13.2 %collective-permute-start.15 = (f32[24,4096]{1,0:T(8,128)S(1)}, f32[24,4096]{1,0:T(8,128)S(1)}, u32[]{:S(2)}, u32[]{:S(2)}) collective-permute-start(f32[24,4096]{1,0:T(8,128)S(1)} %get-tuple-element.7), channel_id=1, source_target_pairs={{1,0},{2,1},{3,2},{4,3},{5,4},{6,5},{7,6},{8,7},{9,8},{10,9},{11,1... | collective-permute-start | bytes 1179656 | tf_op jit(solution)/shard_map/ppermute | solution.py:311

commit v3 on v2

v3 whole, which is shorter than its diff:
```python
import functools

import jax
import jax.numpy as jnp
from jax import lax
from jax.experimental import pallas as pl
from jax.experimental.pallas import tpu as pltpu
from jax.sharding import PartitionSpec as P

TILE = 128
REGIONS = 8
STEPS = 3
STRIP = 8

grav_coef = 0.1
depth_coef = 0.1
advect_coef = 0.05
diffuse_coef = 0.05
coriolis_coef = 0.05
target_size = 0.5
small_eps = 1e-06

VMEM = pl.BlockSpec(memory_space=pltpu.VMEM)
SMEM = pl.BlockSpec(memory_space=pltpu.SMEM)


def east(field):
    return pltpu.roll(field, field.shape[1] - 1, 1)


def west(field):
    return pltpu.roll(field, 1, 1)


def pack_rows(up_ref, down_ref, at, h, u, v, q):
    row = lax.broadcasted_iota(jnp.int32, (STRIP, v.shape[1]), 0)
    up_ref[0:8, at] = v[8:16]
    up_ref[8:16, at] = h[8:16]
    up_ref[16:24, at] = jnp.where(row < 3, pltpu.roll(q[8:16], 3, 0), u[8:16])
    down_ref[0:8, at] = v[0:8]
    down_ref[8:16, at] = h[0:8]
    down_ref[16:24, at] = jnp.where(row >= 5, pltpu.roll(q[0:8], 5, 0), u[0:8])


def edge_kernel(fields_ref, labels_ref, up_ref, down_ref):
    width = fields_ref.shape[2]
    size = width // 8
    for c in range(8):
        at = slice(c * size, (c + 1) * size)
        h, u, v, q = [fields_ref[i, :, at] for i in range(4)]
        pack_rows(up_ref, down_ref, at, h, u, v, q)
    up_ref[8:9, 0:TILE] = labels_ref[15:16, :]
    down_ref[15:16, 0:TILE] = labels_ref[0:1, :]


def packed_edges(fields, labels):
    edge = jax.ShapeDtypeStruct((3 * STRIP, fields.shape[2]), jnp.float32)
    return pl.pallas_call(
        edge_kernel,
        out_shape=(edge, edge),
        in_specs=[VMEM, VMEM],
        out_specs=(VMEM, VMEM),
        compiler_params=pltpu.CompilerParams(vmem_limit_bytes=8 << 20),
        cost_estimate=pl.CostEstimate(flops=1 << 18, bytes_accessed=2 << 20, transcendentals=0),
        name="packed_edges",
    )(fields, labels)


def flow_kernel(total_rows, chunks, where_ref, mid_ref, before_ref, after_ref, out_ref, *state):
    hs, us, vs, qs, h1s = state
    lat = where_ref[0]
    last = where_ref[1]
    local_rows = mid_ref.shape[1]
    width = mid_ref.shape[2]
    strips = local_rows // STRIP + 2
    pad = STRIP

    def rows(s, shift=0):
        return pl.ds(pad + STRIP * s + shift, STRIP)

    zero = jnp.zeros((STRIP, width), jnp.float32)
    for ref in (hs, us, vs, qs, h1s):
        ref[0:pad, :] = zero
        ref[pad + STRIP * strips :, :] = zero
    for ref, field in ((hs, 0), (us, 1), (vs, 2), (qs, 3)):
        ref[pad + STRIP : pad + STRIP * (strips - 1), :] = mid_ref[field]
    for s, edge in ((0, before_ref), (strips - 1, after_ref)):
        vs[rows(s), :] = edge[0:8, :]
        hs[rows(s), :] = edge[8:16, :]
        us[rows(s), :] = edge[16:24, :]
    qs[rows(0), :] = pltpu.roll(before_ref[16:24, :], 5, 0)
    qs[rows(strips - 1), :] = pltpu.roll(after_ref[16:24, :], 3, 0)

    inside = [None] * strips
    inside[0] = jnp.where(lat > 0, 1.0, 0.0).astype(jnp.float32)
    inside[-1] = jnp.where(lat < last, 1.0, 0.0).astype(jnp.float32)

    def kept(value, s):
        return value if inside[s] is None else value * inside[s]

    lane_rows = lax.broadcasted_iota(jnp.int32, (STRIP, width), 0)

    def coriolis(s):
        row = (lane_rows + (lat * local_rows + STRIP * (s - 1))).astype(jnp.float32)
        return coriolis_coef * (2.0 * (row + 0.5) / total_rows - 1.0)

    for k in range(STEPS):
        final = k == STEPS - 1
        for s in range(strips):
            u = us[rows(s), :]
            h1s[rows(s), :] = kept(
                hs[rows(s), :]
                - depth_coef
                * ((east(u) - west(u)) + (vs[rows(s, 1), :] - vs[rows(s, -1), :])),
                s,
            )
        carried = qs[rows(0, -1), :]
        for s in range(1, strips - 1) if final else range(strips):
            f = coriolis(s)
            h1 = h1s[rows(s), :]
            v = vs[rows(s), :]
            u1 = us[rows(s), :] + f * v - grav_coef * (east(h1) - west(h1))
            v1 = v - f * u1 - grav_coef * (h1s[rows(s, 1), :] - h1s[rows(s, -1), :])
            q = qs[rows(s), :]
            if final:
                south = qs[rows(s, -1), :]
            else:
                south = carried
                if s < strips - 1:
                    carried = qs[rows(s + 1, -1), :]
            north = qs[rows(s, 1), :]
            e, w = east(q), west(q)
            q1 = (
                q
                - advect_coef * (u1 * (e - w) + v1 * (north - south))
                + diffuse_coef * ((e + w) + (north + south) - 4.0 * q)
            )
            if not final:
                us[rows(s), :] = kept(u1, s)
                vs[rows(s), :] = kept(v1, s)
                qs[rows(s), :] = kept(q1, s)
                hs[rows(s), :] = h1
            else:
                at = slice(STRIP * (s - 1), STRIP * s)
                for field, value in enumerate((h1, u1, v1, q1)):
                    if chunks == 1:
                        out_ref[field, at, :] = value
                    else:
                        size = width // chunks
                        for c in range(chunks):
                            out_ref[c, field, at, :] = value[:, c * size : (c + 1) * size]


def flow(where, middle, before, after, total_rows, chunks, name):
    fields, local_rows, width = middle.shape
    shape = (fields, local_rows, width)
    if chunks > 1:
        shape = (chunks, fields, local_rows, width // chunks)
    state = pltpu.VMEM((local_rows + 4 * STRIP, width), jnp.float32)
    return pl.pallas_call(
        functools.partial(flow_kernel, total_rows, chunks),
        out_shape=jax.ShapeDtypeStruct(shape, jnp.float32),
        in_specs=[SMEM, VMEM, VMEM, VMEM],
        out_specs=VMEM,
        scratch_shapes=[state] * 5,
        compiler_params=pltpu.CompilerParams(vmem_limit_bytes=24 << 20),
        cost_estimate=pl.CostEstimate(
            flops=60 * 10 * STRIP * width, bytes_accessed=1 << 22, transcendentals=0
        ),
        name=name,
    )(where, middle, before, after)


def pair_kernel(pairing_ref, all_ref, labels_ref, spread_ref, share_ref):
    members, fields, local_rows, size = all_ref.shape
    tiles = size // TILE
    lane = lax.broadcasted_iota(jnp.int32, (REGIONS, TILE), 1)

    def folded(x):
        return x[:STRIP] + x[STRIP:]

    weights, counts = [], []
    shown = [
        [
            jnp.broadcast_to(labels_ref[i : i + local_rows, t : t + 1], (local_rows, TILE))
            for t in range(tiles)
        ]
        for i in range(3)
    ]
    for r in range(REGIONS):

        def is_r(x):
            return jnp.where(x == float(r + 1), 1.0, 0.0).astype(jnp.float32)

        count, weight = None, []
        for t in range(tiles):
            own = is_r(shown[1][t])
            count = folded(own) if count is None else count + folded(own)
            weight.append(0.125 * (is_r(shown[0][t]) + 2.0 * own + is_r(shown[2][t])))
        counts.append(jnp.sum(count, axis=0, keepdims=True))
        weights.append(weight)

    def placed(rows, at, total):
        column = jnp.sum(jnp.concatenate(rows, axis=0), axis=1, keepdims=True)
        return jnp.where(lane == at, column, total)

    total = placed(counts, members, jnp.zeros((REGIONS, TILE), jnp.float32))
    for m in range(members):
        partner = pairing_ref[m]
        squares = [None] * tiles
        for field in range(fields):
            spread = 0.5 * (all_ref[m, field] - all_ref[partner, field])
            for t in range(tiles):
                x = spread[:, t * TILE : (t + 1) * TILE]
                at = (field * tiles + t) * local_rows
                spread_ref[m, at : at + local_rows, :] = x
                squares[t] = x * x if squares[t] is None else squares[t] + x * x
        spread_ref[m, fields * tiles * local_rows :, :] = jnp.zeros((REGIONS, TILE), jnp.float32)
        parts = []
        for weight in weights:
            part = None
            for t in range(tiles):
                y = folded(squares[t] * weight[t])
                part = y if part is None else part + y
            parts.append(jnp.sum(part, axis=0, keepdims=True))
        total = placed(parts, m, total)
    share_ref[...] = total


def pair_spread(pairing, everyone, labels):
    members, fields, local_rows, size = everyone.shape
    rows = fields * local_rows * size // TILE + REGIONS
    return pl.pallas_call(
        pair_kernel,
        out_shape=(
            jax.ShapeDtypeStruct((members, rows, TILE), jnp.float32),
            jax.ShapeDtypeStruct((REGIONS, TILE), jnp.float32),
        ),
        in_specs=[SMEM, VMEM, VMEM],
        out_specs=(VMEM, VMEM),
        compiler_params=pltpu.CompilerParams(vmem_limit_bytes=8 << 20),
        cost_estimate=pl.CostEstimate(flops=1 << 20, bytes_accessed=3 << 20, transcendentals=0),
        name="pair_spread",
    )(pairing, everyone, labels)


def recentre_kernel(
    labels_ref, analysis_ref, back_ref, mid_ref, up_ref, down_ref, factor_ref
):
    chunks = back_ref.shape[0]
    fields, local_rows, width = analysis_ref.shape
    tiles = width // chunks // TILE
    tail = fields * tiles * local_rows
    sums = back_ref[0, tail:, :]
    for c in range(1, chunks):
        sums = sums + back_ref[c, tail:, :]
    region_sum = jnp.broadcast_to(sums[:, 0:1], (REGIONS, TILE))
    cells = jnp.broadcast_to(sums[:, 1:2], (REGIONS, TILE))
    factor = target_size / jnp.sqrt(region_sum / cells + small_eps)
    factor_ref[...] = factor
    labels = labels_ref[...]
    scale = jnp.zeros(labels.shape, jnp.float32)
    for r in range(REGIONS):
        scale = jnp.where(labels == float(r + 1), factor[r : r + 1, :], scale)
    for c in range(chunks):
        for t in range(tiles):
            tile = c * tiles + t
            at = slice(tile * TILE, (tile + 1) * TILE)
            wide = jnp.broadcast_to(scale[:, tile : tile + 1], (local_rows, TILE))
            values = []
            for i in range(fields):
                row = (i * tiles + t) * local_rows
                value = analysis_ref[i, :, at] + wide * back_ref[c, row : row + local_rows, :]
                mid_ref[i, :, at] = value
                values.append(value)
            pack_rows(up_ref, down_ref, at, *values)


def recentre(labels, analysis, back):
    edge = jax.ShapeDtypeStruct((3 * STRIP, analysis.shape[2]), jnp.float32)
    return pl.pallas_call(
        recentre_kernel,
        out_shape=(
            jax.ShapeDtypeStruct(analysis.shape, jnp.float32),
            edge,
            edge,
            jax.ShapeDtypeStruct((REGIONS, TILE), jnp.float32),
        ),
        in_specs=[VMEM] * 3,
        out_specs=(VMEM,) * 4,
        compiler_params=pltpu.CompilerParams(vmem_limit_bytes=12 << 20),
        cost_estimate=pl.CostEstimate(flops=1 << 20, bytes_accessed=4 << 20, transcendentals=0),
        name="recentre",
    )(labels, analysis, back)


def local(replica_variables, analysis, labels, pairing):
    members = lax.axis_size("mem")
    lat_size = lax.axis_size("lat")
    lat = lax.axis_index("lat")
    member = lax.axis_index("mem")
    x = replica_variables[0]
    fields, local_rows, width = x.shape
    tiles = width // members // TILE
    total_rows = float(local_rows * lat_size)
    where = jnp.stack([lat, jnp.int32(lat_size - 1)]).astype(jnp.int32)
    up = [(i, i + 1) for i in range(lat_size - 1)]
    down = [(j, i) for i, j in up]

    coded = (labels + 1).astype(jnp.float32)
    coded = jnp.pad(coded, ((0, 0), (0, TILE - labels.shape[1])))
    last, first = packed_edges(x, coded)
    before = lax.ppermute(last, "lat", up)
    after = lax.ppermute(first, "lat", down)
    pieces = flow(where, x, before, after, total_rows, members, "first_flow")
    everyone = lax.all_to_all(pieces, "mem", 0, 0, tiled=True)

    rows = jnp.concatenate([before[8:9, :TILE], coded, after[15:16, :TILE]], axis=0)
    own = lax.dynamic_slice_in_dim(rows, member * tiles, tiles, axis=1)
    own = jnp.pad(own, ((0, 6), (0, TILE - tiles)))
    spread, share = pair_spread(pairing, everyone, own)
    share = lax.all_to_all(
        jnp.broadcast_to(share[None], (lat_size,) + share.shape), "lat", 0, 0, tiled=True
    ).sum(0)
    lane = jnp.arange(TILE)
    tail = jnp.where(
        lane == 0,
        share.T[:members, :, None],
        jnp.where(lane == 1, share[None, :, members : members + 1], 0.0),
    )
    spread = lax.dynamic_update_slice(spread, tail, (0, spread.shape[1] - REGIONS, 0))
    back = lax.all_to_all(spread, "mem", 0, 0, tiled=True)

    middle, last, first, factor = recentre(coded, analysis, back)
    before = lax.ppermute(last, "lat", up)
    after = lax.ppermute(first, "lat", down)
    closing = flow(where, middle, before, after, total_rows, 1, "closing_flow")
    return closing[None], factor[:, 0].reshape(1, REGIONS)


def solution(mesh):
    return jax.shard_map(
        local,
        mesh=mesh,
        in_specs=(P("mem", None, "lat", None), P(None, "lat", None), P("lat", None), P()),
        out_specs=(P("mem", None, "lat", None), P("mem", None)),
        check_vma=False,
    )
```

time: 139 us -> 130 us (0.935)
  starting transfers between devices: 50 us -> 36.9 us
  blocking collectives: 29.6 us -> 33.5 us
  waiting for transfers between devices: 40.7 us -> 44.3 us
  local copies, waits for them, and re-layouts: 4.83 us -> 2.78 us
    ppermute x12 -> x0, starting transfers between devices: 27.5 us -> none  [all_sum(): lax.ppermute(value, axis, [(i, i ^ d * stride) for i in range(size)])]
    all_to_all x1 -> x2, waiting for transfers between devices: 0.01 us -> 27.5 us  [the longest x1 21.6 us: local(): everyone = lax.all_to_all(pieces, 'mem', 0, 0, tiled=True)]
    ppermute x12 -> x0, waiting for transfers between devices: 22.4 us -> none  [all_sum(): lax.ppermute(value, axis, [(i, i ^ d * stride) for i in range(size)])]
    all_to_all x1 -> x2, starting transfers between devices: 6.9 us -> 24 us  [the longest x1 13 us: local(): lax.all_to_all(jnp.broadcast_to(share[None], (lat_size,) + share.shape),...]
    ppermute x2, starting transfers between devices: 10.9 us -> 6.99 us  [local(): before = lax.ppermute(last, 'lat', up)]
    all_to_all x1, blocking collectives: 29.6 us -> 33.5 us  [local(): back = lax.all_to_all(spread, 'mem', 0, 0, tiled=True)]
    slice x8 -> x5, local copies, waits for them, and re-layouts: 3.12 us -> 0.89 us  [the longest x1 0.63 us: local(): return (closing[None], factor[:, 0].reshape(1, REGIONS))]
    pallas_call x2, Pallas kernels: 3.34 us -> 1.22 us  [the longest x1 1.15 us: pair_spread(): pl.pallas_call(pair_kernel, out_shape=(jax.ShapeDtypeStruct((members, row...]
  transfers between devices with their start and end apart: 17 -> 6, of which waited for: 10 -> 6; matrix products, arithmetic and copies ran while one was open for 1% -> 1% of each run, Pallas kernels for 1% -> 0%
where the time goes in v3:
time: 130 us
  waiting for transfers between devices  44.3 us (34%)
  starting transfers between devices  36.9 us (28%)
  blocking collectives  33.5 us (26%)
  Pallas kernels  10.8 us (8%)
  local copies, waits for them, and re-layouts  2.78 us (2%)
    all_to_all x1, blocking collectives, local(): back = lax.all_to_all(spread, 'mem', 0, 0, tiled=True)  33.5 us
    all_to_all x1, waiting for transfers between devices, local(): everyone = lax.all_to_all(pieces, 'mem', 0, 0, tiled=True)  21.6 us
    ppermute x2, waiting for transfers between devices, local(): after = lax.ppermute(first, 'lat', down)  14 us
    all_to_all x1, starting transfers between devices, local(): lax.all_to_all(jnp.broadcast_to(share[None], (lat_size,) + share.shape),...  13 us
    all_to_all x1, starting transfers between devices, local(): everyone = lax.all_to_all(pieces, 'mem', 0, 0, tiled=True)  11.1 us
    pallas_call x2, Pallas kernels, flow(): pl.pallas_call(functools.partial(flow_kernel, total_rows, chunks), out_sh...  9.23 us
    ppermute x2, starting transfers between devices, local(): before = lax.ppermute(last, 'lat', up)  6.99 us
    ppermute x2, starting transfers between devices, local(): after = lax.ppermute(first, 'lat', down)  5.83 us
  transfers between devices with their start and end apart: 6, of which 6 were waited for; matrix products, arithmetic and copies ran while one was open for 1% of the time, Pallas kernels for 0%

profile of v3, /device:TPU:1, one launch (start us, length us, event | category | flops | bytes accessed | tf_op | source)
XLA Modules:
  0.0 130.0 jit_solution(16243840612303224933)
XLA Ops:
  0.6 0.7 add_convert_fusion
  1.3 1.2 copy-done
  2.6 5.1 %collective-permute-start = (f32[24,4096]{1,0:T(8,128)S(1)}, f32[24,4096]{1,0:T(8,128)S(1)}, u32[]{:S(2)}, u32[]{:S(2)}) collective-permute-start(f32[24,4096]{1,0:T(8,128)S(1)} %get-tuple-element.10), channel_id=1, source_target_pairs={{0,1},{1,2},{2,3},{3,4},{4,5},{5,6},{6,7},{7,8},{8,9},{9,10},{10,1... | collective-permute-start | bytes 1179656 | tf_op jit(solution)/shard_map/ppermute | solution.py:313
  7.7 1.9 %collective-permute-start.1 = (f32[24,4096]{1,0:T(8,128)S(1)}, f32[24,4096]{1,0:T(8,128)S(1)}, u32[]{:S(2)}, u32[]{:S(2)}) collective-permute-start(f32[24,4096]{1,0:T(8,128)S(1)} %get-tuple-element.11), channel_id=1, source_target_pairs={{1,0},{2,1},{3,2},{4,3},{5,4},{6,5},{7,6},{8,7},{9,8},{10,9},{11,1... | collective-permute-start | bytes 1179656 | tf_op jit(solution)/shard_map/ppermute | solution.py:314
  9.7 2.7 %collective-permute-done.before_ref = f32[24,4096]{1,0:T(8,128)S(1)} collective-permute-done((f32[24,4096]{1,0:T(8,128)S(1)}, f32[24,4096]{1,0:T(8,128)S(1)}, u32[]{:S(2)}, u32[]{:S(2)}) %collective-permute-start) | collective-permute-done | bytes 393248 | tf_op jit(solution)/shard_map/ppermute | solution.py:313
  12.4 5.4 %collective-permute-done.1.after_ref = f32[24,4096]{1,0:T(8,128)S(1)} collective-permute-done((f32[24,4096]{1,0:T(8,128)S(1)}, f32[24,4096]{1,0:T(8,128)S(1)}, u32[]{:S(2)}, u32[]{:S(2)}) %collective-permute-start.1) | collective-permute-done | bytes 393248 | tf_op jit(solution)/shard_map/ppermute | solution.py:314
  17.8 4.6 %first_flow.1 = f32[16,4,16,256]{3,2,1,0:T(8,128)} custom-call(s32[2]{0:T(128)S(1)} %pad_add_fusion.where_ref, f32[4,16,4096]{2,1,0:T(8,128)S(1)} %bitcast.7, f32[24,4096]{1,0:T(8,128)S(1)} %collective-permute-done.before_ref, f32[24,4096]{1,0:T(8,128)S(1)} %collective-permute-done.1.after_ref), custom_call_target="tpu_custom_call" | custom-call | flops 19660800 | bytes 4194304 | tf_op jit(solution)/shard_map/first_flow/pallas_call | solution.py:160
  22.4 11.1 %all-to-all-start = ((f32[16,4,16,256]{3,2,1,0:T(8,128)}), f32[16,4,16,256]{3,2,1,0:T(8,128)S(1)}, u32[]{:S(2)}, u32[]{:S(2)}) async-start(f32[16,4,16,256]{3,2,1,0:T(8,128)} %first_flow.1), calls=%async_computation | async-start | bytes 2097152 | tf_op jit(solution)/shard_map/all_to_all | solution.py:316
  33.5 0.1 dynamic-slice_maximum_fusion
  33.6 21.6 %all-to-all-done.all_ref = f32[16,4,16,256]{3,2,1,0:T(8,128)S(1)} async-done(((f32[16,4,16,256]{3,2,1,0:T(8,128)}), f32[16,4,16,256]{3,2,1,0:T(8,128)S(1)}, u32[]{:S(2)}, u32[]{:S(2)}) %all-to-all-start) | async-done | bytes 1048608 | tf_op jit(solution)/shard_map/all_to_all | solution.py:316
  55.2 1.2 pair_spread.1
  56.4 0.6 broadcast_in_dim.50
  57.0 13.0 %all-to-all-start.1 = ((f32[16,8,128]{2,1,0:T(8,128)}), f32[16,8,128]{2,1,0:T(8,128)S(1)}, u32[]{:S(2)}, u32[]{:S(2)}) async-start(f32[16,8,128]{2,1,0:T(8,128)} %broadcast_in_dim.50), calls=%async_computation.1 | async-start | bytes 131072 | tf_op jit(solution)/shard_map/all_to_all | solution.py:322
  70.0 5.8 %all-to-all-done.1 = f32[16,8,128]{2,1,0:T(8,128)S(1)} async-done(((f32[16,8,128]{2,1,0:T(8,128)}), f32[16,8,128]{2,1,0:T(8,128)S(1)}, u32[]{:S(2)}, u32[]{:S(2)}) %all-to-all-start.1) | async-done | bytes 65568 | tf_op jit(solution)/shard_map/all_to_all | solution.py:322
  75.8 0.2 slice_reduce_fusion.1
  76.2 0.1 select_dynamic-update-slice_fusion
  76.3 33.5 %all_to_all.15.back_ref = f32[16,136,128]{2,1,0:T(8,128)S(1)} all-to-all(f32[16,136,128]{2,1,0:T(8,128)S(1)} %select_dynamic-update-slice_fusion), channel_id=1, replica_groups=mesh['mem'=16,'lat'=16] {'mem'}, dimensions={0} | all-to-all | bytes 2228224 | tf_op jit(solution)/shard_map/all_to_all | solution.py:332
  109.8 0.3 recentre.1
  110.1 1.9 %collective-permute-start.2 = (f32[24,4096]{1,0:T(8,128)S(1)}, f32[24,4096]{1,0:T(8,128)S(1)}, u32[]{:S(2)}, u32[]{:S(2)}) collective-permute-start(f32[24,4096]{1,0:T(8,128)S(1)} %get-tuple-element.15), channel_id=1, source_target_pairs={{0,1},{1,2},{2,3},{3,4},{4,5},{5,6},{6,7},{7,8},{8,9},{9,10},{10,1... | collective-permute-start | bytes 1179656 | tf_op jit(solution)/shard_map/ppermute | solution.py:335
  112.0 3.9 %collective-permute-start.3 = (f32[24,4096]{1,0:T(8,128)S(1)}, f32[24,4096]{1,0:T(8,128)S(1)}, u32[]{:S(2)}, u32[]{:S(2)}) collective-permute-start(f32[24,4096]{1,0:T(8,128)S(1)} %get-tuple-element.16), channel_id=1, source_target_pairs={{1,0},{2,1},{3,2},{4,3},{5,4},{6,5},{7,6},{8,7},{9,8},{10,9},{11,1... | collective-permute-start | bytes 1179656 | tf_op jit(solution)/shard_map/ppermute | solution.py:336
  115.9 0.6 slice_reduce_fusion
  116.6 0.2 collective-permute-done.2.before_ref
  116.7 8.6 %collective-permute-done.3.after_ref = f32[24,4096]{1,0:T(8,128)S(1)} collective-permute-done((f32[24,4096]{1,0:T(8,128)S(1)}, f32[24,4096]{1,0:T(8,128)S(1)}, u32[]{:S(2)}, u32[]{:S(2)}) %collective-permute-start.3) | collective-permute-done | bytes 393248 | tf_op jit(solution)/shard_map/ppermute | solution.py:336
  125.3 4.6 %closing_flow.1 = f32[4,16,4096]{2,1,0:T(8,128)} custom-call(s32[2]{0:T(128)S(1)} %pad_add_fusion.where_ref, f32[4,16,4096]{2,1,0:T(8,128)S(1)} %get-tuple-element.14.mid_ref, f32[24,4096]{1,0:T(8,128)S(1)} %collective-permute-done.2.before_ref, f32[24,4096]{1,0:T(8,128)S(1)} %collective-permute-done.3.after_ref), custom_call_target="tpu_custom_call" | custom-call | flops 19660800 | bytes 4194304 | tf_op jit(solution)/shard_map/closing_flow/pallas_call | solution.py:160
  (18 shorter events, 0.3 us)
Async XLA Ops:
  1.3 1.2 copy-start
  2.6 15.3 %copy-start.1 = (f32[1,4,16,4096]{3,2,1,0:T(8,128)S(1)}, f32[1,4,16,4096]{3,2,1,0:T(8,128)}, u32[]{:S(2)}) copy-start(f32[1,4,16,4096]{3,2,1,0:T(8,128)} %param.4) | copy-start | bytes 3145732
  2.6 9.8 %collective-permute-start = (f32[24,4096]{1,0:T(8,128)S(1)}, f32[24,4096]{1,0:T(8,128)S(1)}, u32[]{:S(2)}, u32[]{:S(2)}) collective-permute-start(f32[24,4096]{1,0:T(8,128)S(1)} %get-tuple-element.10), channel_id=1, source_target_pairs={{0,1},{1,2},{2,3},{3,4},{4,5},{5,6},{6,7},{7,8},{8,9},{9,10},{10,1... | collective-permute-start | bytes 1179656 | tf_op jit(solution)/shard_map/ppermute | solution.py:313
  7.7 10.1 %collective-permute-start.1 = (f32[24,4096]{1,0:T(8,128)S(1)}, f32[24,4096]{1,0:T(8,128)S(1)}, u32[]{:S(2)}, u32[]{:S(2)}) collective-permute-start(f32[24,4096]{1,0:T(8,128)S(1)} %get-tuple-element.11), channel_id=1, source_target_pairs={{1,0},{2,1},{3,2},{4,3},{5,4},{6,5},{7,6},{8,7},{9,8},{10,9},{11,1... | collective-permute-start | bytes 1179656 | tf_op jit(solution)/shard_map/ppermute | solution.py:314
  22.4 32.8 %copy-start.3 = (s32[16]{0:T(128)S(1)}, s32[16]{0:T(128)}, u32[]{:S(2)}) copy-start(s32[16]{0:T(128)} %pairing_ref.1) | copy-start | bytes 196
  22.4 32.8 %all-to-all-start = ((f32[16,4,16,256]{3,2,1,0:T(8,128)}), f32[16,4,16,256]{3,2,1,0:T(8,128)S(1)}, u32[]{:S(2)}, u32[]{:S(2)}) async-start(f32[16,4,16,256]{3,2,1,0:T(8,128)} %first_flow.1), calls=%async_computation | async-start | bytes 2097152 | tf_op jit(solution)/shard_map/all_to_all | solution.py:316
  57.0 18.8 %all-to-all-start.1 = ((f32[16,8,128]{2,1,0:T(8,128)}), f32[16,8,128]{2,1,0:T(8,128)S(1)}, u32[]{:S(2)}, u32[]{:S(2)}) async-start(f32[16,8,128]{2,1,0:T(8,128)} %broadcast_in_dim.50), calls=%async_computation.1 | async-start | bytes 131072 | tf_op jit(solution)/shard_map/all_to_all | solution.py:322
  76.3 33.5 %copy-start.2 = (f32[4,16,4096]{2,1,0:T(8,128)S(1)}, f32[4,16,4096]{2,1,0:T(8,128)}, u32[]{:S(2)}) copy-start(f32[4,16,4096]{2,1,0:T(8,128)} %analysis_ref.1) | copy-start | bytes 3145732
  110.1 6.6 %collective-permute-start.2 = (f32[24,4096]{1,0:T(8,128)S(1)}, f32[24,4096]{1,0:T(8,128)S(1)}, u32[]{:S(2)}, u32[]{:S(2)}) collective-permute-start(f32[24,4096]{1,0:T(8,128)S(1)} %get-tuple-element.15), channel_id=1, source_target_pairs={{0,1},{1,2},{2,3},{3,4},{4,5},{5,6},{6,7},{7,8},{8,9},{9,10},{10,1... | collective-permute-start | bytes 1179656 | tf_op jit(solution)/shard_map/ppermute | solution.py:335
  112.0 13.3 %collective-permute-start.3 = (f32[24,4096]{1,0:T(8,128)S(1)}, f32[24,4096]{1,0:T(8,128)S(1)}, u32[]{:S(2)}, u32[]{:S(2)}) collective-permute-start(f32[24,4096]{1,0:T(8,128)S(1)} %get-tuple-element.16), channel_id=1, source_target_pairs={{1,0},{2,1},{3,2},{4,3},{5,4},{6,5},{7,6},{8,7},{9,8},{10,9},{11,1... | collective-permute-start | bytes 1179656 | tf_op jit(solution)/shard_map/ppermute | solution.py:336

commit v4 on v3

--- a/solution.py
+++ b/solution.py
@@ -171,7 +171,7 @@
     )(where, middle, before, after)
 
 
-def pair_kernel(pairing_ref, all_ref, labels_ref, spread_ref, share_ref):
+def pair_kernel(pairing_ref, all_ref, labels_ref, spread_ref):
     members, fields, local_rows, size = all_ref.shape
     tiles = size // TILE
     lane = lax.broadcasted_iota(jnp.int32, (REGIONS, TILE), 1)
@@ -200,11 +200,10 @@
         counts.append(jnp.sum(count, axis=0, keepdims=True))
         weights.append(weight)
 
-    def placed(rows, at, total):
-        column = jnp.sum(jnp.concatenate(rows, axis=0), axis=1, keepdims=True)
-        return jnp.where(lane == at, column, total)
-
-    total = placed(counts, members, jnp.zeros((REGIONS, TILE), jnp.float32))
+    def column(rows):
+        return jnp.sum(jnp.concatenate(rows, axis=0), axis=1, keepdims=True)
+
+    empty = jnp.where(lane == 1, column(counts), 0.0)
     for m in range(members):
         partner = pairing_ref[m]
         squares = [None] * tiles
@@ -215,7 +214,6 @@
                 at = (field * tiles + t) * local_rows
                 spread_ref[m, at : at + local_rows, :] = x
                 squares[t] = x * x if squares[t] is None else squares[t] + x * x
-        spread_ref[m, fields * tiles * local_rows :, :] = jnp.zeros((REGIONS, TILE), jnp.float32)
         parts = []
         for weight in weights:
             part = None
@@ -223,8 +221,9 @@
                 y = folded(squares[t] * weight[t])
                 part = y if part is None else part + y
             parts.append(jnp.sum(part, axis=0, keepdims=True))
-        total = placed(parts, m, total)
-    share_ref[...] = total
+        spread_ref[m, fields * tiles * local_rows :, :] = jnp.where(
+            lane == 0, column(parts), empty
+        )
 
 
 def pair_spread(pairing, everyone, labels):
@@ -232,12 +231,9 @@
     rows = fields * local_rows * size // TILE + REGIONS
     return pl.pallas_call(
         pair_kernel,
-        out_shape=(
-            jax.ShapeDtypeStruct((members, rows, TILE), jnp.float32),
-            jax.ShapeDtypeStruct((REGIONS, TILE), jnp.float32),
-        ),
+        out_shape=jax.ShapeDtypeStruct((members, rows, TILE), jnp.float32),
         in_specs=[SMEM, VMEM, VMEM],
-        out_specs=(VMEM, VMEM),
+        out_specs=VMEM,
         compiler_params=pltpu.CompilerParams(vmem_limit_bytes=8 << 20),
         cost_estimate=pl.CostEstimate(flops=1 << 20, bytes_accessed=3 << 20, transcendentals=0),
         name="pair_spread",
@@ -245,15 +241,12 @@
 
 
 def recentre_kernel(
-    labels_ref, analysis_ref, back_ref, mid_ref, up_ref, down_ref, factor_ref
+    labels_ref, analysis_ref, back_ref, shares_ref, mid_ref, up_ref, down_ref, factor_ref
 ):
     chunks = back_ref.shape[0]
     fields, local_rows, width = analysis_ref.shape
     tiles = width // chunks // TILE
-    tail = fields * tiles * local_rows
-    sums = back_ref[0, tail:, :]
-    for c in range(1, chunks):
-        sums = sums + back_ref[c, tail:, :]
+    sums = jnp.sum(shares_ref[...], axis=0)
     region_sum = jnp.broadcast_to(sums[:, 0:1], (REGIONS, TILE))
     cells = jnp.broadcast_to(sums[:, 1:2], (REGIONS, TILE))
     factor = target_size / jnp.sqrt(region_sum / cells + small_eps)
@@ -276,7 +269,7 @@
             pack_rows(up_ref, down_ref, at, *values)
 
 
-def recentre(labels, analysis, back):
+def recentre(labels, analysis, back, shares):
     edge = jax.ShapeDtypeStruct((3 * STRIP, analysis.shape[2]), jnp.float32)
     return pl.pallas_call(
         recentre_kernel,
@@ -286,12 +279,12 @@
             edge,
             jax.ShapeDtypeStruct((REGIONS, TILE), jnp.float32),
         ),
-        in_specs=[VMEM] * 3,
+        in_specs=[VMEM] * 4,
         out_specs=(VMEM,) * 4,
         compiler_params=pltpu.CompilerParams(vmem_limit_bytes=12 << 20),
         cost_estimate=pl.CostEstimate(flops=1 << 20, bytes_accessed=4 << 20, transcendentals=0),
         name="recentre",
-    )(labels, analysis, back)
+    )(labels, analysis, back, shares)
 
 
 def local(replica_variables, analysis, labels, pairing):
@@ -318,20 +311,13 @@
     rows = jnp.concatenate([before[8:9, :TILE], coded, after[15:16, :TILE]], axis=0)
     own = lax.dynamic_slice_in_dim(rows, member * tiles, tiles, axis=1)
     own = jnp.pad(own, ((0, 6), (0, TILE - tiles)))
-    spread, share = pair_spread(pairing, everyone, own)
-    share = lax.all_to_all(
+    spread = pair_spread(pairing, everyone, own)
+    back = lax.all_to_all(spread, "mem", 0, 0, tiled=True)
+    share = back[:, back.shape[1] - REGIONS :, :].sum(0)
+    shares = lax.all_to_all(
         jnp.broadcast_to(share[None], (lat_size,) + share.shape), "lat", 0, 0, tiled=True
-    ).sum(0)
-    lane = jnp.arange(TILE)
-    tail = jnp.where(
-        lane == 0,
-        share.T[:members, :, None],
-        jnp.where(lane == 1, share[None, :, members : members + 1], 0.0),
     )
-    spread = lax.dynamic_update_slice(spread, tail, (0, spread.shape[1] - REGIONS, 0))
-    back = lax.all_to_all(spread, "mem", 0, 0, tiled=True)
-
-    middle, last, first, factor = recentre(coded, analysis, back)
+    middle, last, first, factor = recentre(coded, analysis, back, shares)
     before = lax.ppermute(last, "lat", up)
     after = lax.ppermute(first, "lat", down)
     closing = flow(where, middle, before, after, total_rows, 1, "closing_flow")

time: 130 us -> 127 us (0.977)
  blocking collectives: 33.5 us -> 52.4 us
  starting transfers between devices: 36.9 us -> 22.6 us
  waiting for transfers between devices: 44.3 us -> 37.6 us
    all_to_all x0 -> x1, blocking collectives: none -> 30.1 us  [local(): lax.all_to_all(jnp.broadcast_to(share[None], (lat_size,) + share.shape),...]
    all_to_all x1 -> x0, starting transfers between devices: 13 us -> none  [local(): lax.all_to_all(jnp.broadcast_to(share[None], (lat_size,) + share.shape),...]
    all_to_all x1, blocking collectives: 33.5 us -> 22.3 us  [local(): back = lax.all_to_all(spread, 'mem', 0, 0, tiled=True)]
    all_to_all x1 -> x0, waiting for transfers between devices: 5.8 us -> none  [local(): lax.all_to_all(jnp.broadcast_to(share[None], (lat_size,) + share.shape),...]
    ppermute x2, waiting for transfers between devices: 14 us -> 11.1 us  [local(): after = lax.ppermute(first, 'lat', down)]
    ppermute x2, waiting for transfers between devices: 2.85 us -> 4.84 us  [local(): before = lax.ppermute(last, 'lat', up)]
    ppermute x2, starting transfers between devices: 5.83 us -> 3.84 us  [local(): after = lax.ppermute(first, 'lat', down)]
  transfers between devices with their start and end apart: 6 -> 5, of which waited for: 6 -> 5; matrix products, arithmetic and copies ran while one was open for 1% -> 1% of each run, Pallas kernels for 0% -> 0%
where the time goes in v4:
time: 127 us
  blocking collectives  52.4 us (41%)
  waiting for transfers between devices  37.6 us (30%)
  starting transfers between devices  22.6 us (18%)
  Pallas kernels  10.8 us (9%)
  local copies, waits for them, and re-layouts  1.89 us (1%)
    all_to_all x1, blocking collectives, local(): lax.all_to_all(jnp.broadcast_to(share[None], (lat_size,) + share.shape),...  30.1 us
    all_to_all x1, blocking collectives, local(): back = lax.all_to_all(spread, 'mem', 0, 0, tiled=True)  22.3 us
    all_to_all x1, waiting for transfers between devices, local(): everyone = lax.all_to_all(pieces, 'mem', 0, 0, tiled=True)  21.6 us
    ppermute x2, waiting for transfers between devices, local(): after = lax.ppermute(first, 'lat', down)  11.1 us
    all_to_all x1, starting transfers between devices, local(): everyone = lax.all_to_all(pieces, 'mem', 0, 0, tiled=True)  11.1 us
    pallas_call x2, Pallas kernels, flow(): pl.pallas_call(functools.partial(flow_kernel, total_rows, chunks), out_sh...  9.23 us
    ppermute x2, starting transfers between devices, local(): before = lax.ppermute(last, 'lat', up)  7.67 us
    ppermute x2, waiting for transfers between devices, local(): before = lax.ppermute(last, 'lat', up)  4.84 us
  transfers between devices with their start and end apart: 5, of which 5 were waited for; matrix products, arithmetic and copies ran while one was open for 1% of the time, Pallas kernels for 0%

profile of v4, /device:TPU:1, one launch (start us, length us, event | category | flops | bytes accessed | tf_op | source)
XLA Modules:
  0.0 126.9 jit_solution(1201115528188722355)
XLA Ops:
  0.6 0.7 add_convert_fusion
  1.3 1.2 copy-done
  2.6 0.1 packed_edges.1
  2.6 5.1 %collective-permute-start = (f32[24,4096]{1,0:T(8,128)S(1)}, f32[24,4096]{1,0:T(8,128)S(1)}, u32[]{:S(2)}, u32[]{:S(2)}) collective-permute-start(f32[24,4096]{1,0:T(8,128)S(1)} %get-tuple-element.8), channel_id=1, source_target_pairs={{0,1},{1,2},{2,3},{3,4},{4,5},{5,6},{6,7},{7,8},{8,9},{9,10},{10,1... | collective-permute-start | bytes 1179656 | tf_op jit(solution)/shard_map/ppermute | solution.py:306
  7.7 1.9 %collective-permute-start.1 = (f32[24,4096]{1,0:T(8,128)S(1)}, f32[24,4096]{1,0:T(8,128)S(1)}, u32[]{:S(2)}, u32[]{:S(2)}) collective-permute-start(f32[24,4096]{1,0:T(8,128)S(1)} %get-tuple-element.9), channel_id=1, source_target_pairs={{1,0},{2,1},{3,2},{4,3},{5,4},{6,5},{7,6},{8,7},{9,8},{10,9},{11,1... | collective-permute-start | bytes 1179656 | tf_op jit(solution)/shard_map/ppermute | solution.py:307
  9.6 0.1 pad_add_fusion.where_ref
  9.7 2.7 %collective-permute-done.before_ref = f32[24,4096]{1,0:T(8,128)S(1)} collective-permute-done((f32[24,4096]{1,0:T(8,128)S(1)}, f32[24,4096]{1,0:T(8,128)S(1)}, u32[]{:S(2)}, u32[]{:S(2)}) %collective-permute-start) | collective-permute-done | bytes 393248 | tf_op jit(solution)/shard_map/ppermute | solution.py:306
  12.4 5.4 %collective-permute-done.1.after_ref = f32[24,4096]{1,0:T(8,128)S(1)} collective-permute-done((f32[24,4096]{1,0:T(8,128)S(1)}, f32[24,4096]{1,0:T(8,128)S(1)}, u32[]{:S(2)}, u32[]{:S(2)}) %collective-permute-start.1) | collective-permute-done | bytes 393248 | tf_op jit(solution)/shard_map/ppermute | solution.py:307
  17.8 0.0 copy-done.1
  17.8 4.6 %first_flow.1 = f32[16,4,16,256]{3,2,1,0:T(8,128)} custom-call(s32[2]{0:T(128)S(1)} %pad_add_fusion.where_ref, f32[4,16,4096]{2,1,0:T(8,128)S(1)} %bitcast.5, f32[24,4096]{1,0:T(8,128)S(1)} %collective-permute-done.before_ref, f32[24,4096]{1,0:T(8,128)S(1)} %collective-permute-done.1.after_ref), custom_call_target="tpu_custom_call" | custom-call | flops 19660800 | bytes 4194304 | tf_op jit(solution)/shard_map/first_flow/pallas_call | solution.py:160
  22.4 11.1 %all-to-all-start = ((f32[16,4,16,256]{3,2,1,0:T(8,128)}), f32[16,4,16,256]{3,2,1,0:T(8,128)S(1)}, u32[]{:S(2)}, u32[]{:S(2)}) async-start(f32[16,4,16,256]{3,2,1,0:T(8,128)} %first_flow.1), calls=%async_computation | async-start | bytes 2097152 | tf_op jit(solution)/shard_map/all_to_all | solution.py:309
  33.5 0.1 dynamic-slice_maximum_fusion
  33.6 21.6 %all-to-all-done.all_ref = f32[16,4,16,256]{3,2,1,0:T(8,128)S(1)} async-done(((f32[16,4,16,256]{3,2,1,0:T(8,128)}), f32[16,4,16,256]{3,2,1,0:T(8,128)S(1)}, u32[]{:S(2)}, u32[]{:S(2)}) %all-to-all-start) | async-done | bytes 1048608 | tf_op jit(solution)/shard_map/all_to_all | solution.py:309
  55.2 0.0 copy-done.3
  55.2 1.2 pair_spread.1
  56.4 22.3 %all_to_all.15.back_ref = f32[16,136,128]{2,1,0:T(8,128)S(1)} all-to-all(f32[16,136,128]{2,1,0:T(8,128)S(1)} %pair_spread.1), channel_id=1, replica_groups=mesh['mem'=16,'lat'=16] {'mem'}, dimensions={0} | all-to-all | bytes 2228224 | tf_op jit(solution)/shard_map/all_to_all | solution.py:315
  78.7 30.1 %all_to_all.16.shares_ref = f32[16,8,128]{2,1,0:T(8,128)S(1)} all-to-all(f32[16,8,128]{2,1,0:T(8,128)S(1)} %broadcast_in_dim.4), channel_id=1, replica_groups=mesh['mem'=16,'lat'=16] {'lat'}, dimensions={0} | all-to-all | bytes 131072 | tf_op jit(solution)/shard_map/all_to_all | solution.py:317
  108.8 0.3 recentre.1
  109.2 2.6 %collective-permute-start.2 = (f32[24,4096]{1,0:T(8,128)S(1)}, f32[24,4096]{1,0:T(8,128)S(1)}, u32[]{:S(2)}, u32[]{:S(2)}) collective-permute-start(f32[24,4096]{1,0:T(8,128)S(1)} %get-tuple-element.11), channel_id=1, source_target_pairs={{0,1},{1,2},{2,3},{3,4},{4,5},{5,6},{6,7},{7,8},{8,9},{9,10},{10,1... | collective-permute-start | bytes 1179656 | tf_op jit(solution)/shard_map/ppermute | solution.py:321
  111.8 1.9 %collective-permute-start.3 = (f32[24,4096]{1,0:T(8,128)S(1)}, f32[24,4096]{1,0:T(8,128)S(1)}, u32[]{:S(2)}, u32[]{:S(2)}) collective-permute-start(f32[24,4096]{1,0:T(8,128)S(1)} %get-tuple-element.12), channel_id=1, source_target_pairs={{1,0},{2,1},{3,2},{4,3},{5,4},{6,5},{7,6},{8,7},{9,8},{10,9},{11,1... | collective-permute-start | bytes 1179656 | tf_op jit(solution)/shard_map/ppermute | solution.py:322
  113.7 0.6 slice_reduce_fusion.1
  114.4 2.1 %collective-permute-done.2.before_ref = f32[24,4096]{1,0:T(8,128)S(1)} collective-permute-done((f32[24,4096]{1,0:T(8,128)S(1)}, f32[24,4096]{1,0:T(8,128)S(1)}, u32[]{:S(2)}, u32[]{:S(2)}) %collective-permute-start.2) | collective-permute-done | bytes 393248 | tf_op jit(solution)/shard_map/ppermute | solution.py:321
  116.5 5.7 %collective-permute-done.3.after_ref = f32[24,4096]{1,0:T(8,128)S(1)} collective-permute-done((f32[24,4096]{1,0:T(8,128)S(1)}, f32[24,4096]{1,0:T(8,128)S(1)}, u32[]{:S(2)}, u32[]{:S(2)}) %collective-permute-start.3) | collective-permute-done | bytes 393248 | tf_op jit(solution)/shard_map/ppermute | solution.py:322
  122.2 4.6 %closing_flow.1 = f32[4,16,4096]{2,1,0:T(8,128)} custom-call(s32[2]{0:T(128)S(1)} %pad_add_fusion.where_ref, f32[4,16,4096]{2,1,0:T(8,128)S(1)} %get-tuple-element.10.mid_ref, f32[24,4096]{1,0:T(8,128)S(1)} %collective-permute-done.2.before_ref, f32[24,4096]{1,0:T(8,128)S(1)} %collective-permute-done.3.after_ref), custom_call_target="tpu_custom_call" | custom-call | flops 19660800 | bytes 4194304 | tf_op jit(solution)/shard_map/closing_flow/pallas_call | solution.py:160
  (11 shorter events, 0.1 us)
Async XLA Ops:
  1.3 1.2 copy-start
  2.6 15.3 %copy-start.1 = (f32[1,4,16,4096]{3,2,1,0:T(8,128)S(1)}, f32[1,4,16,4096]{3,2,1,0:T(8,128)}, u32[]{:S(2)}) copy-start(f32[1,4,16,4096]{3,2,1,0:T(8,128)} %param.4) | copy-start | bytes 3145732
  2.6 9.8 %collective-permute-start = (f32[24,4096]{1,0:T(8,128)S(1)}, f32[24,4096]{1,0:T(8,128)S(1)}, u32[]{:S(2)}, u32[]{:S(2)}) collective-permute-start(f32[24,4096]{1,0:T(8,128)S(1)} %get-tuple-element.8), channel_id=1, source_target_pairs={{0,1},{1,2},{2,3},{3,4},{4,5},{5,6},{6,7},{7,8},{8,9},{9,10},{10,1... | collective-permute-start | bytes 1179656 | tf_op jit(solution)/shard_map/ppermute | solution.py:306
  7.7 10.1 %collective-permute-start.1 = (f32[24,4096]{1,0:T(8,128)S(1)}, f32[24,4096]{1,0:T(8,128)S(1)}, u32[]{:S(2)}, u32[]{:S(2)}) collective-permute-start(f32[24,4096]{1,0:T(8,128)S(1)} %get-tuple-element.9), channel_id=1, source_target_pairs={{1,0},{2,1},{3,2},{4,3},{5,4},{6,5},{7,6},{8,7},{9,8},{10,9},{11,1... | collective-permute-start | bytes 1179656 | tf_op jit(solution)/shard_map/ppermute | solution.py:307
  22.4 32.8 %copy-start.3 = (s32[16]{0:T(128)S(1)}, s32[16]{0:T(128)}, u32[]{:S(2)}) copy-start(s32[16]{0:T(128)} %pairing_ref.1) | copy-start | bytes 196
  22.4 32.8 %all-to-all-start = ((f32[16,4,16,256]{3,2,1,0:T(8,128)}), f32[16,4,16,256]{3,2,1,0:T(8,128)S(1)}, u32[]{:S(2)}, u32[]{:S(2)}) async-start(f32[16,4,16,256]{3,2,1,0:T(8,128)} %first_flow.1), calls=%async_computation | async-start | bytes 2097152 | tf_op jit(solution)/shard_map/all_to_all | solution.py:309
  56.4 52.5 %copy-start.2 = (f32[4,16,4096]{2,1,0:T(8,128)S(1)}, f32[4,16,4096]{2,1,0:T(8,128)}, u32[]{:S(2)}) copy-start(f32[4,16,4096]{2,1,0:T(8,128)} %analysis_ref.1) | copy-start | bytes 3145732
  109.2 7.3 %collective-permute-start.2 = (f32[24,4096]{1,0:T(8,128)S(1)}, f32[24,4096]{1,0:T(8,128)S(1)}, u32[]{:S(2)}, u32[]{:S(2)}) collective-permute-start(f32[24,4096]{1,0:T(8,128)S(1)} %get-tuple-element.11), channel_id=1, source_target_pairs={{0,1},{1,2},{2,3},{3,4},{4,5},{5,6},{6,7},{7,8},{8,9},{9,10},{10,1... | collective-permute-start | bytes 1179656 | tf_op jit(solution)/shard_map/ppermute | solution.py:321
  111.8 10.4 %collective-permute-start.3 = (f32[24,4096]{1,0:T(8,128)S(1)}, f32[24,4096]{1,0:T(8,128)S(1)}, u32[]{:S(2)}, u32[]{:S(2)}) collective-permute-start(f32[24,4096]{1,0:T(8,128)S(1)} %get-tuple-element.12), channel_id=1, source_target_pairs={{1,0},{2,1},{3,2},{4,3},{5,4},{6,5},{7,6},{8,7},{9,8},{10,9},{11,1... | collective-permute-start | bytes 1179656 | tf_op jit(solution)/shard_map/ppermute | solution.py:322

commit v5 on v4

--- a/solution.py
+++ b/solution.py
@@ -42,28 +42,31 @@
     down_ref[16:24, at] = jnp.where(row >= 5, pltpu.roll(q[0:8], 5, 0), u[0:8])
 
 
-def edge_kernel(fields_ref, labels_ref, up_ref, down_ref):
+def edge_kernel(label_rows, fields_ref, labels_ref, after_ref, up_ref, down_ref):
     width = fields_ref.shape[2]
     size = width // 8
     for c in range(8):
         at = slice(c * size, (c + 1) * size)
         h, u, v, q = [fields_ref[i, :, at] for i in range(4)]
         pack_rows(up_ref, down_ref, at, h, u, v, q)
-    up_ref[8:9, 0:TILE] = labels_ref[15:16, :]
-    down_ref[15:16, 0:TILE] = labels_ref[0:1, :]
-
-
-def packed_edges(fields, labels):
+    for k in range(label_rows):
+        at = slice(k * TILE, (k + 1) * TILE)
+        row = labels_ref.shape[0] - label_rows + k
+        up_ref[8:9, at] = labels_ref[row : row + 1, :]
+        down_ref[15:16, at] = labels_ref[k : k + 1, :]
+
+
+def packed_edges(fields, labels, after, label_rows, name):
     edge = jax.ShapeDtypeStruct((3 * STRIP, fields.shape[2]), jnp.float32)
     return pl.pallas_call(
-        edge_kernel,
+        functools.partial(edge_kernel, label_rows),
         out_shape=(edge, edge),
-        in_specs=[VMEM, VMEM],
+        in_specs=[VMEM, VMEM, pl.BlockSpec(memory_space=pl.ANY)],
         out_specs=(VMEM, VMEM),
         compiler_params=pltpu.CompilerParams(vmem_limit_bytes=8 << 20),
         cost_estimate=pl.CostEstimate(flops=1 << 18, bytes_accessed=2 << 20, transcendentals=0),
-        name="packed_edges",
-    )(fields, labels)
+        name=name,
+    )(fields, labels, after)
 
 
 def flow_kernel(total_rows, chunks, where_ref, mid_ref, before_ref, after_ref, out_ref, *state):
@@ -240,8 +243,43 @@
     )(pairing, everyone, labels)
 
 
+def spread_edge_kernel(shape, back_ref, up_ref, down_ref, share_ref):
+    fields, local_rows, width = shape
+    chunks = back_ref.shape[0]
+    tiles = width // chunks // TILE
+    tail = fields * tiles * local_rows
+    share = back_ref[0, tail:, :]
+    for c in range(1, chunks):
+        share = share + back_ref[c, tail:, :]
+    for i in range(share_ref.shape[0]):
+        share_ref[i] = share
+    for c in range(chunks):
+        for t in range(tiles):
+            tile = c * tiles + t
+            at = slice(tile * TILE, (tile + 1) * TILE)
+            values = []
+            for i in range(fields):
+                row = (i * tiles + t) * local_rows
+                values.append(back_ref[c, row : row + local_rows, :])
+            pack_rows(up_ref, down_ref, at, *values)
+
+
+def spread_edges(back, shape, lat_size):
+    edge = jax.ShapeDtypeStruct((3 * STRIP, shape[2]), jnp.float32)
+    return pl.pallas_call(
+        functools.partial(spread_edge_kernel, shape),
+        out_shape=(edge, edge, jax.ShapeDtypeStruct((lat_size, REGIONS, TILE), jnp.float32)),
+        in_specs=[VMEM],
+        out_specs=(VMEM,) * 3,
+        compiler_params=pltpu.CompilerParams(vmem_limit_bytes=8 << 20),
+        cost_estimate=pl.CostEstimate(flops=1 << 18, bytes_accessed=2 << 20, transcendentals=0),
+        name="spread_edges",
+    )(back)
+
+
 def recentre_kernel(
-    labels_ref, analysis_ref, back_ref, shares_ref, mid_ref, up_ref, down_ref, factor_ref
+    labels_ref, analysis_ref, a_before_ref, a_after_ref, back_ref, b_before_ref, b_after_ref,
+    shares_ref, mid_ref, before_ref, after_ref, factor_ref
 ):
     chunks = back_ref.shape[0]
     fields, local_rows, width = analysis_ref.shape
@@ -251,26 +289,50 @@
     cells = jnp.broadcast_to(sums[:, 1:2], (REGIONS, TILE))
     factor = target_size / jnp.sqrt(region_sum / cells + small_eps)
     factor_ref[...] = factor
-    labels = labels_ref[...]
-    scale = jnp.zeros(labels.shape, jnp.float32)
-    for r in range(REGIONS):
-        scale = jnp.where(labels == float(r + 1), factor[r : r + 1, :], scale)
+
+    def scale_of(labels):
+        scale = jnp.zeros(labels.shape, jnp.float32)
+        for r in range(REGIONS):
+            scale = jnp.where(labels == float(r + 1), factor[r : r + 1, :], scale)
+        return scale
+
+    def rows_of(ref, row):
+        parts = [ref[row : row + 1, k * TILE : (k + 1) * TILE] for k in range(STRIP)]
+        return jnp.concatenate(parts, axis=0)
+
+    scale = scale_of(labels_ref[...])
+    below = scale_of(rows_of(a_before_ref, 8))
+    above = scale_of(rows_of(a_after_ref, 15))
+    row = lax.broadcasted_iota(jnp.int32, (STRIP, TILE), 0)
+    below_uq = jnp.where(row < 3, pltpu.roll(below, 3, 0), below)
+    above_uq = jnp.where(row >= 5, pltpu.roll(above, 5, 0), above)
+
     for c in range(chunks):
         for t in range(tiles):
             tile = c * tiles + t
             at = slice(tile * TILE, (tile + 1) * TILE)
-            wide = jnp.broadcast_to(scale[:, tile : tile + 1], (local_rows, TILE))
-            values = []
+
+            def wide(x):
+                return jnp.broadcast_to(x[:, tile : tile + 1], (x.shape[0], TILE))
+
+            own = wide(scale)
             for i in range(fields):
-                row = (i * tiles + t) * local_rows
-                value = analysis_ref[i, :, at] + wide * back_ref[c, row : row + local_rows, :]
-                mid_ref[i, :, at] = value
-                values.append(value)
-            pack_rows(up_ref, down_ref, at, *values)
-
-
-def recentre(labels, analysis, back, shares):
-    edge = jax.ShapeDtypeStruct((3 * STRIP, analysis.shape[2]), jnp.float32)
+                first = (i * tiles + t) * local_rows
+                mid_ref[i, :, at] = (
+                    analysis_ref[i, :, at] + own * back_ref[c, first : first + local_rows, :]
+                )
+            for out, a_ref, b_ref, near, mixed in (
+                (before_ref, a_before_ref, b_before_ref, below, below_uq),
+                (after_ref, a_after_ref, b_after_ref, above, above_uq),
+            ):
+                near = wide(near)
+                for rows, factor_rows in ((0, near), (8, near), (16, wide(mixed))):
+                    pack = slice(rows, rows + STRIP)
+                    out[pack, at] = a_ref[pack, at] + factor_rows * b_ref[pack, at]
+
+
+def recentre(labels, analysis, a_before, a_after, back, b_before, b_after, shares):
+    edge = jax.ShapeDtypeStruct(a_before.shape, jnp.float32)
     return pl.pallas_call(
         recentre_kernel,
         out_shape=(
@@ -279,12 +341,12 @@
             edge,
             jax.ShapeDtypeStruct((REGIONS, TILE), jnp.float32),
         ),
-        in_specs=[VMEM] * 4,
+        in_specs=[VMEM] * 8,
         out_specs=(VMEM,) * 4,
-        compiler_params=pltpu.CompilerParams(vmem_limit_bytes=12 << 20),
+        compiler_params=pltpu.CompilerParams(vmem_limit_bytes=16 << 20),
         cost_estimate=pl.CostEstimate(flops=1 << 20, bytes_accessed=4 << 20, transcendentals=0),
         name="recentre",
-    )(labels, analysis, back, shares)
+    )(labels, analysis, a_before, a_after, back, b_before, b_after, shares)
 
 
 def local(replica_variables, analysis, labels, pairing):
@@ -302,9 +364,12 @@
 
     coded = (labels + 1).astype(jnp.float32)
     coded = jnp.pad(coded, ((0, 0), (0, TILE - labels.shape[1])))
-    last, first = packed_edges(x, coded)
+    last, first = packed_edges(x, coded, coded, 1, "packed_edges")
     before = lax.ppermute(last, "lat", up)
     after = lax.ppermute(first, "lat", down)
+    last, first = packed_edges(analysis, coded, before, STRIP, "analysis_edges")
+    a_before = lax.ppermute(last, "lat", up)
+    a_after = lax.ppermute(first, "lat", down)
     pieces = flow(where, x, before, after, total_rows, members, "first_flow")
     everyone = lax.all_to_all(pieces, "mem", 0, 0, tiled=True)
 
@@ -313,13 +378,13 @@
     own = jnp.pad(own, ((0, 6), (0, TILE - tiles)))
     spread = pair_spread(pairing, everyone, own)
     back = lax.all_to_all(spread, "mem", 0, 0, tiled=True)
-    share = back[:, back.shape[1] - REGIONS :, :].sum(0)
-    shares = lax.all_to_all(
-        jnp.broadcast_to(share[None], (lat_size,) + share.shape), "lat", 0, 0, tiled=True
+    last, first, share = spread_edges(back, x.shape, lat_size)
+    b_before = lax.ppermute(last, "lat", up)
+    b_after = lax.ppermute(first, "lat", down)
+    shares = lax.all_to_all(share, "lat", 0, 0, tiled=True)
+    middle, before, after, factor = recentre(
+        coded, analysis, a_before, a_after, back, b_before, b_after, shares
     )
-    middle, last, first, factor = recentre(coded, analysis, back, shares)
-    before = lax.ppermute(last, "lat", up)
-    after = lax.ppermute(first, "lat", down)
     closing = flow(where, middle, before, after, total_rows, 1, "closing_flow")
     return closing[None], factor[:, 0].reshape(1, REGIONS)
 

time: 127 us -> 125 us (0.984)
  blocking collectives: 52.4 us -> 0 us
  starting transfers between devices: 22.6 us -> 66.1 us
  Pallas kernels: 10.8 us -> 14.8 us
  waiting for transfers between devices: 37.6 us -> 40.1 us
    all_to_all x2 -> x0, blocking collectives: 52.4 us -> none  [the longest x1 30.1 us: local(): lax.all_to_all(jnp.broadcast_to(share[None], (lat_size,) + share.shape),...]
    ppermute x0 -> x4, starting transfers between devices: none -> 34.2 us  [the longest x1 20.1 us: local(): b_before = lax.ppermute(last, 'lat', up)]
    all_to_all x0 -> x2, starting transfers between devices: none -> 13.9 us  [the longest x1 7.75 us: local(): shares = lax.all_to_all(share, 'lat', 0, 0, tiled=True)]
    all_to_all x0 -> x2, waiting for transfers between devices: none -> 10.4 us  [the longest x1 5.81 us: local(): shares = lax.all_to_all(share, 'lat', 0, 0, tiled=True)]
    ppermute x2 -> x1, waiting for transfers between devices: 11.1 us -> 5.41 us  [local(): after = lax.ppermute(first, 'lat', down)]
    ppermute x2 -> x1, starting transfers between devices: 7.67 us -> 5.07 us  [local(): before = lax.ppermute(last, 'lat', up)]
    ppermute x2 -> x1, waiting for transfers between devices: 4.84 us -> 2.69 us  [local(): before = lax.ppermute(last, 'lat', up)]
    pallas_call x1 -> x3, Pallas kernels: 0.06 us -> 2 us  [the longest x2 1.01 us: packed_edges(): pl.pallas_call(functools.partial(edge_kernel, label_rows), out_shape=(edg...]
  transfers between devices with their start and end apart: 5 -> 9, of which waited for: 5 -> 5; matrix products, arithmetic and copies ran while one was open for 1% -> 0% of each run, Pallas kernels for 0% -> 2%
where the time goes in v5:
time: 125 us
  starting transfers between devices  66.1 us (53%)
  waiting for transfers between devices  40.1 us (32%)
  Pallas kernels  14.8 us (12%)
  local copies, waits for them, and re-layouts  1.88 us (2%)
    all_to_all x1, waiting for transfers between devices, local(): everyone = lax.all_to_all(pieces, 'mem', 0, 0, tiled=True)  21.6 us
    ppermute x1, starting transfers between devices, local(): b_before = lax.ppermute(last, 'lat', up)  20.1 us
    all_to_all x1, starting transfers between devices, local(): everyone = lax.all_to_all(pieces, 'mem', 0, 0, tiled=True)  11.1 us
    ppermute x1, starting transfers between devices, local(): a_before = lax.ppermute(last, 'lat', up)  10.3 us
    pallas_call x2, Pallas kernels, flow(): pl.pallas_call(functools.partial(flow_kernel, total_rows, chunks), out_sh...  9.23 us
    all_to_all x1, starting transfers between devices, local(): shares = lax.all_to_all(share, 'lat', 0, 0, tiled=True)  7.75 us
    all_to_all x1, starting transfers between devices, local(): back = lax.all_to_all(spread, 'mem', 0, 0, tiled=True)  6.12 us
    all_to_all x1, waiting for transfers between devices, local(): shares = lax.all_to_all(share, 'lat', 0, 0, tiled=True)  5.81 us
  transfers between devices with their start and end apart: 9, of which 5 were waited for; matrix products, arithmetic and copies ran while one was open for 0% of the time, Pallas kernels for 2%

profile of v5, /device:TPU:1, one launch (start us, length us, event | category | flops | bytes accessed | tf_op | source)
XLA Modules:
  0.0 124.6 jit_solution(15534266365622988186)
XLA Ops:
  0.6 0.7 add_convert_fusion
  1.3 1.2 copy-done
  2.6 5.1 %collective-permute-start = (f32[24,4096]{1,0:T(8,128)S(1)}, f32[24,4096]{1,0:T(8,128)S(1)}, u32[]{:S(2)}, u32[]{:S(2)}) collective-permute-start(f32[24,4096]{1,0:T(8,128)S(1)} %get-tuple-element.13), channel_id=1, source_target_pairs={{0,1},{1,2},{2,3},{3,4},{4,5},{5,6},{6,7},{7,8},{8,9},{9,10},{10,1... | collective-permute-start | bytes 1179656 | tf_op jit(solution)/shard_map/ppermute | solution.py:368
  7.7 1.9 %collective-permute-start.3 = (f32[24,4096]{1,0:T(8,128)S(1)}, f32[24,4096]{1,0:T(8,128)S(1)}, u32[]{:S(2)}, u32[]{:S(2)}) collective-permute-start(f32[24,4096]{1,0:T(8,128)S(1)} %get-tuple-element.16), channel_id=1, source_target_pairs={{1,0},{2,1},{3,2},{4,3},{5,4},{6,5},{7,6},{8,7},{9,8},{10,9},{11,1... | collective-permute-start | bytes 1179656 | tf_op jit(solution)/shard_map/ppermute | solution.py:369
  9.7 2.7 %collective-permute-done.after_ref.before_ref = f32[24,4096]{1,0:T(8,128)S(1)} collective-permute-done((f32[24,4096]{1,0:T(8,128)S(1)}, f32[24,4096]{1,0:T(8,128)S(1)}, u32[]{:S(2)}, u32[]{:S(2)}) %collective-permute-start) | collective-permute-done | bytes 393248 | tf_op jit(solution)/shard_map/ppermute | solution.py:368
  12.4 5.4 %collective-permute-done.3.after_ref = f32[24,4096]{1,0:T(8,128)S(1)} collective-permute-done((f32[24,4096]{1,0:T(8,128)S(1)}, f32[24,4096]{1,0:T(8,128)S(1)}, u32[]{:S(2)}, u32[]{:S(2)}) %collective-permute-start.3) | collective-permute-done | bytes 393248 | tf_op jit(solution)/shard_map/ppermute | solution.py:369
  17.8 4.6 %first_flow.1 = f32[16,4,16,256]{3,2,1,0:T(8,128)} custom-call(s32[2]{0:T(128)S(1)} %pad_add_fusion.where_ref, f32[4,16,4096]{2,1,0:T(8,128)S(1)} %bitcast.5, f32[24,4096]{1,0:T(8,128)S(1)} %collective-permute-done.after_ref.before_ref, f32[24,4096]{1,0:T(8,128)S(1)} %collective-permute-done.3.after_ref), custom_call_target="tpu_custom_call" | custom-call | flops 19660800 | bytes 4194304 | tf_op jit(solution)/shard_map/first_flow/pallas_call | solution.py:163
  22.4 11.1 %all-to-all-start = ((f32[16,4,16,256]{3,2,1,0:T(8,128)}), f32[16,4,16,256]{3,2,1,0:T(8,128)S(1)}, u32[]{:S(2)}, u32[]{:S(2)}) async-start(f32[16,4,16,256]{3,2,1,0:T(8,128)} %first_flow.1), calls=%async_computation | async-start | bytes 2097152 | tf_op jit(solution)/shard_map/all_to_all | solution.py:374
  33.5 0.1 dynamic-slice_maximum_fusion
  33.6 21.6 %all-to-all-done.all_ref = f32[16,4,16,256]{3,2,1,0:T(8,128)S(1)} async-done(((f32[16,4,16,256]{3,2,1,0:T(8,128)}), f32[16,4,16,256]{3,2,1,0:T(8,128)S(1)}, u32[]{:S(2)}, u32[]{:S(2)}) %all-to-all-start) | async-done | bytes 1048608 | tf_op jit(solution)/shard_map/all_to_all | solution.py:374
  55.2 2.2 %pair_spread.1 = f32[16,136,128]{2,1,0:T(8,128)} custom-call(s32[16]{0:T(128)S(1)} %copy-done.3, f32[16,4,16,256]{3,2,1,0:T(8,128)S(1)} %all-to-all-done.all_ref, f32[24,128]{1,0:T(8,128)S(1)} %pad.9.labels_ref), custom_call_target="tpu_custom_call" | custom-call | flops 1048576 | bytes 3145728 | tf_op jit(solution)/shard_map/pair_spread/pallas_call | solution.py:235
  57.4 6.1 %all-to-all-start.1 = ((f32[16,136,128]{2,1,0:T(8,128)}), f32[16,136,128]{2,1,0:T(8,128)S(1)}, u32[]{:S(2)}, u32[]{:S(2)}) async-start(f32[16,136,128]{2,1,0:T(8,128)} %pair_spread.1), calls=%async_computation.1 | async-start | bytes 2228224 | tf_op jit(solution)/shard_map/all_to_all | solution.py:380
  63.5 1.0 analysis_edges.1
  64.5 10.3 %collective-permute-start.1 = (f32[24,4096]{1,0:T(8,128)}, f32[24,4096]{1,0:T(8,128)S(1)}, u32[]{:S(2)}, u32[]{:S(2)}) collective-permute-start(f32[24,4096]{1,0:T(8,128)} %get-tuple-element.14), channel_id=1, source_target_pairs={{0,1},{1,2},{2,3},{3,4},{4,5},{5,6},{6,7},{7,8},{8,9},{9,10},{10,1... | collective-permute-start | bytes 1179656 | tf_op jit(solution)/shard_map/ppermute | solution.py:371
  74.8 1.9 %collective-permute-start.2 = (f32[24,4096]{1,0:T(8,128)}, f32[24,4096]{1,0:T(8,128)S(1)}, u32[]{:S(2)}, u32[]{:S(2)}) collective-permute-start(f32[24,4096]{1,0:T(8,128)} %get-tuple-element.15), channel_id=1, source_target_pairs={{1,0},{2,1},{3,2},{4,3},{5,4},{6,5},{7,6},{8,7},{9,8},{10,9},{11,1... | collective-permute-start | bytes 1179656 | tf_op jit(solution)/shard_map/ppermute | solution.py:372
  76.7 4.6 %all-to-all-done.1.back_ref = f32[16,136,128]{2,1,0:T(8,128)S(1)} async-done(((f32[16,136,128]{2,1,0:T(8,128)}), f32[16,136,128]{2,1,0:T(8,128)S(1)}, u32[]{:S(2)}, u32[]{:S(2)}) %all-to-all-start.1) | async-done | bytes 1114144 | tf_op jit(solution)/shard_map/all_to_all | solution.py:380
  81.3 1.0 spread_edges.1
  82.2 20.1 %collective-permute-start.4 = (f32[24,4096]{1,0:T(8,128)}, f32[24,4096]{1,0:T(8,128)S(1)}, u32[]{:S(2)}, u32[]{:S(2)}) collective-permute-start(f32[24,4096]{1,0:T(8,128)} %get-tuple-element.17), channel_id=1, source_target_pairs={{0,1},{1,2},{2,3},{3,4},{4,5},{5,6},{6,7},{7,8},{8,9},{9,10},{10,1... | collective-permute-start | bytes 1179656 | tf_op jit(solution)/shard_map/ppermute | solution.py:382
  102.3 1.9 %collective-permute-start.5 = (f32[24,4096]{1,0:T(8,128)}, f32[24,4096]{1,0:T(8,128)}, u32[]{:S(2)}, u32[]{:S(2)}) collective-permute-start(f32[24,4096]{1,0:T(8,128)} %get-tuple-element.18), channel_id=1, source_target_pairs={{1,0},{2,1},{3,2},{4,3},{5,4},{6,5},{7,6},{8,7},{9,8},{10,9},{11,1... | collective-permute-start | bytes 1179656 | tf_op jit(solution)/shard_map/ppermute | solution.py:383
  104.3 7.8 %all-to-all-start.2 = ((f32[16,8,128]{2,1,0:T(8,128)}), f32[16,8,128]{2,1,0:T(8,128)S(1)}, u32[]{:S(2)}, u32[]{:S(2)}) async-start(f32[16,8,128]{2,1,0:T(8,128)} %get-tuple-element.19), calls=%async_computation.2 | async-start | bytes 131072 | tf_op jit(solution)/shard_map/all_to_all | solution.py:384
  112.0 5.8 %all-to-all-done.2.shares_ref = f32[16,8,128]{2,1,0:T(8,128)S(1)} async-done(((f32[16,8,128]{2,1,0:T(8,128)}), f32[16,8,128]{2,1,0:T(8,128)S(1)}, u32[]{:S(2)}, u32[]{:S(2)}) %all-to-all-start.2) | async-done | bytes 65568 | tf_op jit(solution)/shard_map/all_to_all | solution.py:384
  117.8 1.4 %recentre.1 = (f32[4,16,4096]{2,1,0:T(8,128)S(1)}, f32[24,4096]{1,0:T(8,128)S(1)}, f32[24,4096]{1,0:T(8,128)S(1)}, f32[8,128]{1,0:T(8,128)S(1)}) custom-call(f32[16,128]{1,0:T(8,128)S(1)} %pad.8.labels_ref.after_ref, f32[4,16,4096]{2,1,0:T(8,128)S(1)} %copy-done.2, f32[24,4096]{1,0:T(8,128)S(1)} %collective-permute-done.1.a_before_ref, ...), custom_call_target="tpu_custom_call" | custom-call | flops 1048576 | bytes 4194304 | tf_op jit(solution)/shard_map/recentre/pallas_call | solution.py:336
  119.3 0.6 slice_reduce_fusion
  119.9 4.6 %closing_flow.1 = f32[4,16,4096]{2,1,0:T(8,128)} custom-call(s32[2]{0:T(128)S(1)} %pad_add_fusion.where_ref, f32[4,16,4096]{2,1,0:T(8,128)S(1)} %get-tuple-element.20.mid_ref, f32[24,4096]{1,0:T(8,128)S(1)} %get-tuple-element.21.before_ref, f32[24,4096]{1,0:T(8,128)S(1)} %get-tuple-element.22.after_ref), custom_call_target="tpu_custom_call" | custom-call | flops 19660800 | bytes 4194304 | tf_op jit(solution)/shard_map/closing_flow/pallas_call | solution.py:163
  (17 shorter events, 0.2 us)
Async XLA Ops:
  1.3 1.2 copy-start
  2.6 15.3 %copy-start.1 = (f32[1,4,16,4096]{3,2,1,0:T(8,128)S(1)}, f32[1,4,16,4096]{3,2,1,0:T(8,128)}, u32[]{:S(2)}) copy-start(f32[1,4,16,4096]{3,2,1,0:T(8,128)} %param.4) | copy-start | bytes 3145732
  2.6 9.8 %collective-permute-start = (f32[24,4096]{1,0:T(8,128)S(1)}, f32[24,4096]{1,0:T(8,128)S(1)}, u32[]{:S(2)}, u32[]{:S(2)}) collective-permute-start(f32[24,4096]{1,0:T(8,128)S(1)} %get-tuple-element.13), channel_id=1, source_target_pairs={{0,1},{1,2},{2,3},{3,4},{4,5},{5,6},{6,7},{7,8},{8,9},{9,10},{10,1... | collective-permute-start | bytes 1179656 | tf_op jit(solution)/shard_map/ppermute | solution.py:368
  7.7 10.1 %collective-permute-start.3 = (f32[24,4096]{1,0:T(8,128)S(1)}, f32[24,4096]{1,0:T(8,128)S(1)}, u32[]{:S(2)}, u32[]{:S(2)}) collective-permute-start(f32[24,4096]{1,0:T(8,128)S(1)} %get-tuple-element.16), channel_id=1, source_target_pairs={{1,0},{2,1},{3,2},{4,3},{5,4},{6,5},{7,6},{8,7},{9,8},{10,9},{11,1... | collective-permute-start | bytes 1179656 | tf_op jit(solution)/shard_map/ppermute | solution.py:369
  22.4 32.8 %copy-start.3 = (s32[16]{0:T(128)S(1)}, s32[16]{0:T(128)}, u32[]{:S(2)}) copy-start(s32[16]{0:T(128)} %pairing_ref.1) | copy-start | bytes 196
  22.4 32.8 %all-to-all-start = ((f32[16,4,16,256]{3,2,1,0:T(8,128)}), f32[16,4,16,256]{3,2,1,0:T(8,128)S(1)}, u32[]{:S(2)}, u32[]{:S(2)}) async-start(f32[16,4,16,256]{3,2,1,0:T(8,128)} %first_flow.1), calls=%async_computation | async-start | bytes 2097152 | tf_op jit(solution)/shard_map/all_to_all | solution.py:374
  57.4 6.1 %copy-start.2 = (f32[4,16,4096]{2,1,0:T(8,128)S(1)}, f32[4,16,4096]{2,1,0:T(8,128)}, u32[]{:S(2)}) copy-start(f32[4,16,4096]{2,1,0:T(8,128)} %analysis_ref.1) | copy-start | bytes 3145732
  57.4 23.9 %all-to-all-start.1 = ((f32[16,136,128]{2,1,0:T(8,128)}), f32[16,136,128]{2,1,0:T(8,128)S(1)}, u32[]{:S(2)}, u32[]{:S(2)}) async-start(f32[16,136,128]{2,1,0:T(8,128)} %pair_spread.1), calls=%async_computation.1 | async-start | bytes 2228224 | tf_op jit(solution)/shard_map/all_to_all | solution.py:380
  64.5 47.5 %collective-permute-start.1 = (f32[24,4096]{1,0:T(8,128)}, f32[24,4096]{1,0:T(8,128)S(1)}, u32[]{:S(2)}, u32[]{:S(2)}) collective-permute-start(f32[24,4096]{1,0:T(8,128)} %get-tuple-element.14), channel_id=1, source_target_pairs={{0,1},{1,2},{2,3},{3,4},{4,5},{5,6},{6,7},{7,8},{8,9},{9,10},{10,1... | collective-permute-start | bytes 1179656 | tf_op jit(solution)/shard_map/ppermute | solution.py:371
  74.8 37.3 %collective-permute-start.2 = (f32[24,4096]{1,0:T(8,128)}, f32[24,4096]{1,0:T(8,128)S(1)}, u32[]{:S(2)}, u32[]{:S(2)}) collective-permute-start(f32[24,4096]{1,0:T(8,128)} %get-tuple-element.15), channel_id=1, source_target_pairs={{1,0},{2,1},{3,2},{4,3},{5,4},{6,5},{7,6},{8,7},{9,8},{10,9},{11,1... | collective-permute-start | bytes 1179656 | tf_op jit(solution)/shard_map/ppermute | solution.py:372
  82.2 35.6 %collective-permute-start.4 = (f32[24,4096]{1,0:T(8,128)}, f32[24,4096]{1,0:T(8,128)S(1)}, u32[]{:S(2)}, u32[]{:S(2)}) collective-permute-start(f32[24,4096]{1,0:T(8,128)} %get-tuple-element.17), channel_id=1, source_target_pairs={{0,1},{1,2},{2,3},{3,4},{4,5},{5,6},{6,7},{7,8},{8,9},{9,10},{10,1... | collective-permute-start | bytes 1179656 | tf_op jit(solution)/shard_map/ppermute | solution.py:382
  102.3 15.5 %collective-permute-start.5 = (f32[24,4096]{1,0:T(8,128)}, f32[24,4096]{1,0:T(8,128)}, u32[]{:S(2)}, u32[]{:S(2)}) collective-permute-start(f32[24,4096]{1,0:T(8,128)} %get-tuple-element.18), channel_id=1, source_target_pairs={{1,0},{2,1},{3,2},{4,3},{5,4},{6,5},{7,6},{8,7},{9,8},{10,9},{11,1... | collective-permute-start | bytes 1179656 | tf_op jit(solution)/shard_map/ppermute | solution.py:383
  104.3 13.6 %all-to-all-start.2 = ((f32[16,8,128]{2,1,0:T(8,128)}), f32[16,8,128]{2,1,0:T(8,128)S(1)}, u32[]{:S(2)}, u32[]{:S(2)}) async-start(f32[16,8,128]{2,1,0:T(8,128)} %get-tuple-element.19), calls=%async_computation.2 | async-start | bytes 131072 | tf_op jit(solution)/shard_map/all_to_all | solution.py:384

commit v6 on v5

--- a/solution.py
+++ b/solution.py
@@ -11,6 +11,7 @@
 REGIONS = 8
 STEPS = 3
 STRIP = 8
+PARTS = 8
 
 grav_coef = 0.1
 depth_coef = 0.1
@@ -42,30 +43,55 @@
     down_ref[16:24, at] = jnp.where(row >= 5, pltpu.roll(q[0:8], 5, 0), u[0:8])
 
 
-def edge_kernel(label_rows, fields_ref, labels_ref, after_ref, up_ref, down_ref):
+def first_edge_kernel(fields_ref, labels_ref, up_ref, down_ref, coded_ref):
     width = fields_ref.shape[2]
-    size = width // 8
-    for c in range(8):
+    size = width // PARTS
+    for c in range(PARTS):
         at = slice(c * size, (c + 1) * size)
-        h, u, v, q = [fields_ref[i, :, at] for i in range(4)]
-        pack_rows(up_ref, down_ref, at, h, u, v, q)
-    for k in range(label_rows):
+        pack_rows(up_ref, down_ref, at, *[fields_ref[i, :, at] for i in range(4)])
+    local_rows, columns = labels_ref.shape
+    coded_ref[...] = jnp.zeros(coded_ref.shape, jnp.float32)
+    coded_ref[:, 0:columns] = labels_ref[...].astype(jnp.float32) + 1.0
+    up_ref[8:9, 0:TILE] = coded_ref[local_rows - 1 :, :]
+    down_ref[15:16, 0:TILE] = coded_ref[0:1, :]
+
+
+def first_edges(fields, labels):
+    edge = jax.ShapeDtypeStruct((3 * STRIP, fields.shape[2]), jnp.float32)
+    return pl.pallas_call(
+        first_edge_kernel,
+        out_shape=(edge, edge, jax.ShapeDtypeStruct((labels.shape[0], TILE), jnp.float32)),
+        in_specs=[VMEM] * 2,
+        out_specs=(VMEM,) * 3,
+        compiler_params=pltpu.CompilerParams(vmem_limit_bytes=8 << 20),
+        cost_estimate=pl.CostEstimate(flops=1 << 18, bytes_accessed=2 << 20, transcendentals=0),
+        name="first_edges",
+    )(fields, labels)
+
+
+def edge_kernel(fields_ref, labels_ref, after_ref, up_ref, down_ref):
+    width = fields_ref.shape[2]
+    size = width // PARTS
+    for c in range(PARTS):
+        at = slice(c * size, (c + 1) * size)
+        pack_rows(up_ref, down_ref, at, *[fields_ref[i, :, at] for i in range(4)])
+    for k in range(STRIP):
         at = slice(k * TILE, (k + 1) * TILE)
-        row = labels_ref.shape[0] - label_rows + k
+        row = labels_ref.shape[0] - STRIP + k
         up_ref[8:9, at] = labels_ref[row : row + 1, :]
         down_ref[15:16, at] = labels_ref[k : k + 1, :]
 
 
-def packed_edges(fields, labels, after, label_rows, name):
+def packed_edges(fields, labels, after):
     edge = jax.ShapeDtypeStruct((3 * STRIP, fields.shape[2]), jnp.float32)
     return pl.pallas_call(
-        functools.partial(edge_kernel, label_rows),
+        edge_kernel,
         out_shape=(edge, edge),
         in_specs=[VMEM, VMEM, pl.BlockSpec(memory_space=pl.ANY)],
         out_specs=(VMEM, VMEM),
         compiler_params=pltpu.CompilerParams(vmem_limit_bytes=8 << 20),
         cost_estimate=pl.CostEstimate(flops=1 << 18, bytes_accessed=2 << 20, transcendentals=0),
-        name=name,
+        name="analysis_edges",
     )(fields, labels, after)
 
 
@@ -174,7 +200,9 @@
     )(where, middle, before, after)
 
 
-def pair_kernel(pairing_ref, all_ref, labels_ref, spread_ref):
+def pair_kernel(
+    where_ref, pairing_ref, all_ref, labels_ref, before_ref, after_ref, spread_ref, near_ref
+):
     members, fields, local_rows, size = all_ref.shape
     tiles = size // TILE
     lane = lax.broadcasted_iota(jnp.int32, (REGIONS, TILE), 1)
@@ -183,13 +211,18 @@
         return x[:STRIP] + x[STRIP:]
 
     weights, counts = [], []
-    shown = [
-        [
-            jnp.broadcast_to(labels_ref[i : i + local_rows, t : t + 1], (local_rows, TILE))
-            for t in range(tiles)
-        ]
-        for i in range(3)
-    ]
+    near_ref[0:STRIP, :] = jnp.broadcast_to(before_ref[8:9, 0:TILE], (STRIP, TILE))
+    near_ref[STRIP : STRIP + local_rows, :] = labels_ref[...]
+    near_ref[STRIP + local_rows :, :] = jnp.broadcast_to(after_ref[15:16, 0:TILE], (STRIP, TILE))
+    column_of = lax.broadcasted_iota(jnp.int32, (local_rows, TILE), 1)
+    shown = []
+    for i in range(3):
+        near = near_ref[STRIP - 1 + i : STRIP - 1 + i + local_rows, :]
+        shown.append([])
+        for t in range(tiles):
+            own = jnp.where(column_of == where_ref[2] * tiles + t, near, 0.0)
+            own = jnp.sum(own, axis=1, keepdims=True)
+            shown[-1].append(jnp.broadcast_to(own, (local_rows, TILE)))
     for r in range(REGIONS):
 
         def is_r(x):
@@ -229,18 +262,19 @@
         )
 
 
-def pair_spread(pairing, everyone, labels):
+def pair_spread(where, pairing, everyone, labels, before, after):
     members, fields, local_rows, size = everyone.shape
     rows = fields * local_rows * size // TILE + REGIONS
     return pl.pallas_call(
         pair_kernel,
         out_shape=jax.ShapeDtypeStruct((members, rows, TILE), jnp.float32),
-        in_specs=[SMEM, VMEM, VMEM],
+        in_specs=[SMEM, SMEM, VMEM, VMEM, VMEM, VMEM],
         out_specs=VMEM,
+        scratch_shapes=[pltpu.VMEM((local_rows + 2 * STRIP, TILE), jnp.float32)],
         compiler_params=pltpu.CompilerParams(vmem_limit_bytes=8 << 20),
         cost_estimate=pl.CostEstimate(flops=1 << 20, bytes_accessed=3 << 20, transcendentals=0),
         name="pair_spread",
-    )(pairing, everyone, labels)
+    )(where, pairing, everyone, labels, before, after)
 
 
 def spread_edge_kernel(shape, back_ref, up_ref, down_ref, share_ref):
@@ -288,7 +322,11 @@
     region_sum = jnp.broadcast_to(sums[:, 0:1], (REGIONS, TILE))
     cells = jnp.broadcast_to(sums[:, 1:2], (REGIONS, TILE))
     factor = target_size / jnp.sqrt(region_sum / cells + small_eps)
-    factor_ref[...] = factor
+    diagonal = lax.broadcasted_iota(jnp.int32, factor.shape, 0) == lax.broadcasted_iota(
+        jnp.int32, factor.shape, 1
+    )
+    in_lanes = jnp.sum(jnp.where(diagonal, factor, 0.0), axis=0, keepdims=True)
+    factor_ref[...] = in_lanes[:, 0:REGIONS]
 
     def scale_of(labels):
         scale = jnp.zeros(labels.shape, jnp.float32)
@@ -339,7 +377,7 @@
             jax.ShapeDtypeStruct(analysis.shape, jnp.float32),
             edge,
             edge,
-            jax.ShapeDtypeStruct((REGIONS, TILE), jnp.float32),
+            jax.ShapeDtypeStruct((1, REGIONS), jnp.float32),
         ),
         in_specs=[VMEM] * 8,
         out_specs=(VMEM,) * 4,
@@ -356,27 +394,21 @@
     member = lax.axis_index("mem")
     x = replica_variables[0]
     fields, local_rows, width = x.shape
-    tiles = width // members // TILE
     total_rows = float(local_rows * lat_size)
-    where = jnp.stack([lat, jnp.int32(lat_size - 1)]).astype(jnp.int32)
+    where = jnp.stack([lat, jnp.int32(lat_size - 1), member]).astype(jnp.int32)
     up = [(i, i + 1) for i in range(lat_size - 1)]
     down = [(j, i) for i, j in up]
 
-    coded = (labels + 1).astype(jnp.float32)
-    coded = jnp.pad(coded, ((0, 0), (0, TILE - labels.shape[1])))
-    last, first = packed_edges(x, coded, coded, 1, "packed_edges")
+    last, first, coded = first_edges(x, labels)
     before = lax.ppermute(last, "lat", up)
     after = lax.ppermute(first, "lat", down)
-    last, first = packed_edges(analysis, coded, before, STRIP, "analysis_edges")
+    last, first = packed_edges(analysis, coded, before)
     a_before = lax.ppermute(last, "lat", up)
     a_after = lax.ppermute(first, "lat", down)
     pieces = flow(where, x, before, after, total_rows, members, "first_flow")
     everyone = lax.all_to_all(pieces, "mem", 0, 0, tiled=True)
 
-    rows = jnp.concatenate([before[8:9, :TILE], coded, after[15:16, :TILE]], axis=0)
-    own = lax.dynamic_slice_in_dim(rows, member * tiles, tiles, axis=1)
-    own = jnp.pad(own, ((0, 6), (0, TILE - tiles)))
-    spread = pair_spread(pairing, everyone, own)
+    spread = pair_spread(where, pairing, everyone, coded, before, after)
     back = lax.all_to_all(spread, "mem", 0, 0, tiled=True)
     last, first, share = spread_edges(back, x.shape, lat_size)
     b_before = lax.ppermute(last, "lat", up)
@@ -386,7 +418,7 @@
         coded, analysis, a_before, a_after, back, b_before, b_after, shares
     )
     closing = flow(where, middle, before, after, total_rows, 1, "closing_flow")
-    return closing[None], factor[:, 0].reshape(1, REGIONS)
+    return closing[None], factor
 
 
 def solution(mesh):

time: 125 us -> 122 us (0.976)
  blocking collectives: 0 us -> 29.5 us
  starting transfers between devices: 66.1 us -> 49.1 us
  waiting for transfers between devices: 40.1 us -> 25.8 us
    all_to_all x0 -> x1, blocking collectives: none -> 29.5 us  [local(): everyone = lax.all_to_all(pieces, 'mem', 0, 0, tiled=True)]
    all_to_all x1 -> x0, waiting for transfers between devices: 21.6 us -> none  [local(): everyone = lax.all_to_all(pieces, 'mem', 0, 0, tiled=True)]
    all_to_all x1 -> x0, starting transfers between devices: 11.1 us -> none  [local(): everyone = lax.all_to_all(pieces, 'mem', 0, 0, tiled=True)]
    ppermute x1, starting transfers between devices: 20.1 us -> 12.7 us  [local(): b_before = lax.ppermute(last, 'lat', up)]
    all_to_all x1, waiting for transfers between devices: 4.57 us -> 11.9 us  [local(): back = lax.all_to_all(spread, 'mem', 0, 0, tiled=True)]
    all_to_all x1, starting transfers between devices: 7.75 us -> 9.61 us  [local(): shares = lax.all_to_all(share, 'lat', 0, 0, tiled=True)]
    ppermute x1, starting transfers between devices: 10.3 us -> 8.87 us  [local(): a_before = lax.ppermute(last, 'lat', up)]
  transfers between devices with their start and end apart: 9 -> 8, of which waited for: 5 -> 4; matrix products, arithmetic and copies ran while one was open for 0% -> 0% of each run, Pallas kernels for 2% -> 2%
where the time goes in v6:
time: 122 us; the launch traced here: 121 us
  starting transfers between devices  49.1 us (40%)
  blocking collectives  29.5 us (24%)
  waiting for transfers between devices  25.8 us (21%)
  Pallas kernels  14.2 us (12%)
  local copies, waits for them, and re-layouts  1.93 us (2%)
    all_to_all x1, blocking collectives, local(): everyone = lax.all_to_all(pieces, 'mem', 0, 0, tiled=True)  29.5 us
    ppermute x1, starting transfers between devices, local(): b_before = lax.ppermute(last, 'lat', up)  12.7 us
    all_to_all x1, waiting for transfers between devices, local(): back = lax.all_to_all(spread, 'mem', 0, 0, tiled=True)  11.9 us
    all_to_all x1, starting transfers between devices, local(): shares = lax.all_to_all(share, 'lat', 0, 0, tiled=True)  9.61 us
    ppermute x1, starting transfers between devices, local(): a_before = lax.ppermute(last, 'lat', up)  8.87 us
    pallas_call x2, Pallas kernels, flow(): pl.pallas_call(functools.partial(flow_kernel, total_rows, chunks), out_sh...  8.26 us
    all_to_all x1, starting transfers between devices, local(): back = lax.all_to_all(spread, 'mem', 0, 0, tiled=True)  7.07 us
    all_to_all x1, waiting for transfers between devices, local(): shares = lax.all_to_all(share, 'lat', 0, 0, tiled=True)  5.81 us
  transfers between devices with their start and end apart: 8, of which 4 were waited for; matrix products, arithmetic and copies ran while one was open for 0% of the time, Pallas kernels for 2%

profile of v6, /device:TPU:1, one launch (start us, length us, event | category | flops | bytes accessed | tf_op | source)
XLA Modules:
  0.0 121.3 jit_solution(8244831054216471108)
XLA Ops:
  0.6 1.2 %copy-done = f32[1,4,16,4096]{3,2,1,0:T(8,128)S(1)} copy-done((f32[1,4,16,4096]{3,2,1,0:T(8,128)S(1)}, f32[1,4,16,4096]{3,2,1,0:T(8,128)}, u32[]{:S(2)}) %copy-start) | copy-done | bytes 1048600
  1.9 0.7 copy-done.3
  2.6 0.1 first_edges.1
  2.6 5.1 %collective-permute-start = (f32[24,4096]{1,0:T(8,128)S(1)}, f32[24,4096]{1,0:T(8,128)S(1)}, u32[]{:S(2)}, u32[]{:S(2)}) collective-permute-start(f32[24,4096]{1,0:T(8,128)S(1)} %get-tuple-element.15), channel_id=1, source_target_pairs={{0,1},{1,2},{2,3},{3,4},{4,5},{5,6},{6,7},{7,8},{8,9},{9,10},{10,1... | collective-permute-start | bytes 1179656 | tf_op jit(solution)/shard_map/ppermute | solution.py:403
  7.7 1.9 %collective-permute-start.3 = (f32[24,4096]{1,0:T(8,128)S(1)}, f32[24,4096]{1,0:T(8,128)S(1)}, u32[]{:S(2)}, u32[]{:S(2)}) collective-permute-start(f32[24,4096]{1,0:T(8,128)S(1)} %get-tuple-element.18), channel_id=1, source_target_pairs={{1,0},{2,1},{3,2},{4,3},{5,4},{6,5},{7,6},{8,7},{9,8},{10,9},{11,1... | collective-permute-start | bytes 1179656 | tf_op jit(solution)/shard_map/ppermute | solution.py:404
  9.6 0.1 pad_add_fusion.where_ref
  9.7 2.7 %collective-permute-done.after_ref.before_ref = f32[24,4096]{1,0:T(8,128)S(1)} collective-permute-done((f32[24,4096]{1,0:T(8,128)S(1)}, f32[24,4096]{1,0:T(8,128)S(1)}, u32[]{:S(2)}, u32[]{:S(2)}) %collective-permute-start) | collective-permute-done | bytes 393248 | tf_op jit(solution)/shard_map/ppermute | solution.py:403
  12.4 5.4 %collective-permute-done.3.after_ref = f32[24,4096]{1,0:T(8,128)S(1)} collective-permute-done((f32[24,4096]{1,0:T(8,128)S(1)}, f32[24,4096]{1,0:T(8,128)S(1)}, u32[]{:S(2)}, u32[]{:S(2)}) %collective-permute-start.3) | collective-permute-done | bytes 393248 | tf_op jit(solution)/shard_map/ppermute | solution.py:404
  17.8 3.6 %first_flow.1 = f32[16,4,16,256]{3,2,1,0:T(8,128)S(1)} custom-call(s32[3]{0:T(128)S(1)} %pad_add_fusion.where_ref, f32[4,16,4096]{2,1,0:T(8,128)S(1)} %bitcast.5, f32[24,4096]{1,0:T(8,128)S(1)} %collective-permute-done.after_ref.before_ref, f32[24,4096]{1,0:T(8,128)S(1)} %collective-permute-done.3.after_ref), custom_call_target="tpu_custom_call" | custom-call | flops 19660800 | bytes 4194304 | tf_op jit(solution)/shard_map/first_flow/pallas_call | solution.py:189
  21.4 0.0 copy-start.4
  21.4 29.5 %all_to_all.15.all_ref = f32[16,4,16,256]{3,2,1,0:T(8,128)S(1)} all-to-all(f32[16,4,16,256]{3,2,1,0:T(8,128)S(1)} %first_flow.1), channel_id=1, replica_groups=mesh['mem'=16,'lat'=16] {'mem'}, dimensions={0} | all-to-all | bytes 2097152 | tf_op jit(solution)/shard_map/all_to_all | solution.py:409
  50.9 2.2 %pair_spread.1 = f32[16,136,128]{2,1,0:T(8,128)} custom-call(s32[3]{0:T(128)S(1)} %pad_add_fusion.where_ref, s32[16]{0:T(128)S(1)} %copy-done.4, f32[16,4,16,256]{3,2,1,0:T(8,128)S(1)} %all_to_all.15.all_ref, f32[16,128]{1,0:T(8,128)S(1)} %get-tuple-element.14.labels_ref, f32[24,4096]{1,0:T(8,128)S(1)} %collective-permute-done.after_ref.before_ref, ...), custom_call_target="tpu_custom_call" | custom-call | flops 1048576 | bytes 3145728 | tf_op jit(solution)/shard_map/pair_spread/pallas_call | solution.py:268
  53.1 7.1 %all-to-all-start.1 = ((f32[16,136,128]{2,1,0:T(8,128)}), f32[16,136,128]{2,1,0:T(8,128)S(1)}, u32[]{:S(2)}, u32[]{:S(2)}) async-start(f32[16,136,128]{2,1,0:T(8,128)} %pair_spread.1), calls=%async_computation.1 | async-start | bytes 2228224 | tf_op jit(solution)/shard_map/all_to_all | solution.py:412
  60.2 0.9 analysis_edges.1
  61.2 8.9 %collective-permute-start.1 = (f32[24,4096]{1,0:T(8,128)}, f32[24,4096]{1,0:T(8,128)S(1)}, u32[]{:S(2)}, u32[]{:S(2)}) collective-permute-start(f32[24,4096]{1,0:T(8,128)} %get-tuple-element.16), channel_id=1, source_target_pairs={{0,1},{1,2},{2,3},{3,4},{4,5},{5,6},{6,7},{7,8},{8,9},{9,10},{10,1... | collective-permute-start | bytes 1179656 | tf_op jit(solution)/shard_map/ppermute | solution.py:406
  70.1 1.9 %collective-permute-start.2 = (f32[24,4096]{1,0:T(8,128)}, f32[24,4096]{1,0:T(8,128)S(1)}, u32[]{:S(2)}, u32[]{:S(2)}) collective-permute-start(f32[24,4096]{1,0:T(8,128)} %get-tuple-element.17), channel_id=1, source_target_pairs={{1,0},{2,1},{3,2},{4,3},{5,4},{6,5},{7,6},{8,7},{9,8},{10,9},{11,1... | collective-permute-start | bytes 1179656 | tf_op jit(solution)/shard_map/ppermute | solution.py:407
  72.0 11.9 %all-to-all-done.1.back_ref = f32[16,136,128]{2,1,0:T(8,128)S(1)} async-done(((f32[16,136,128]{2,1,0:T(8,128)}), f32[16,136,128]{2,1,0:T(8,128)S(1)}, u32[]{:S(2)}, u32[]{:S(2)}) %all-to-all-start.1) | async-done | bytes 1114144 | tf_op jit(solution)/shard_map/all_to_all | solution.py:412
  83.8 1.0 spread_edges.1
  84.8 12.7 %collective-permute-start.4 = (f32[24,4096]{1,0:T(8,128)}, f32[24,4096]{1,0:T(8,128)S(1)}, u32[]{:S(2)}, u32[]{:S(2)}) collective-permute-start(f32[24,4096]{1,0:T(8,128)} %get-tuple-element.19), channel_id=1, source_target_pairs={{0,1},{1,2},{2,3},{3,4},{4,5},{5,6},{6,7},{7,8},{8,9},{9,10},{10,1... | collective-permute-start | bytes 1179656 | tf_op jit(solution)/shard_map/ppermute | solution.py:414
  97.6 1.9 %collective-permute-start.5 = (f32[24,4096]{1,0:T(8,128)}, f32[24,4096]{1,0:T(8,128)}, u32[]{:S(2)}, u32[]{:S(2)}) collective-permute-start(f32[24,4096]{1,0:T(8,128)} %get-tuple-element.20), channel_id=1, source_target_pairs={{1,0},{2,1},{3,2},{4,3},{5,4},{6,5},{7,6},{8,7},{9,8},{10,9},{11,1... | collective-permute-start | bytes 1179656 | tf_op jit(solution)/shard_map/ppermute | solution.py:415
  99.5 9.6 %all-to-all-start.2 = ((f32[16,8,128]{2,1,0:T(8,128)}), f32[16,8,128]{2,1,0:T(8,128)S(1)}, u32[]{:S(2)}, u32[]{:S(2)}) async-start(f32[16,8,128]{2,1,0:T(8,128)} %get-tuple-element.21), calls=%async_computation.2 | async-start | bytes 131072 | tf_op jit(solution)/shard_map/all_to_all | solution.py:416
  109.2 5.8 %all-to-all-done.2.shares_ref = f32[16,8,128]{2,1,0:T(8,128)S(1)} async-done(((f32[16,8,128]{2,1,0:T(8,128)}), f32[16,8,128]{2,1,0:T(8,128)S(1)}, u32[]{:S(2)}, u32[]{:S(2)}) %all-to-all-start.2) | async-done | bytes 65568 | tf_op jit(solution)/shard_map/all_to_all | solution.py:416
  115.0 1.7 %recentre.1 = (f32[4,16,4096]{2,1,0:T(8,128)S(1)}, f32[24,4096]{1,0:T(8,128)S(1)}, f32[24,4096]{1,0:T(8,128)S(1)}, f32[1,8]{1,0:T(1,128)}) custom-call(f32[16,128]{1,0:T(8,128)S(1)} %get-tuple-element.14.labels_ref, f32[4,16,4096]{2,1,0:T(8,128)S(1)} %copy-done.2, f32[24,4096]{1,0:T(8,128)S(1)} %collective-permute-done.1.a_before_ref, ...), custom_call_target="tpu_custom_call" | custom-call | flops 1048576 | bytes 4194304 | tf_op jit(solution)/shard_map/recentre/pallas_call | solution.py:374
  116.7 4.6 %closing_flow.1 = f32[4,16,4096]{2,1,0:T(8,128)} custom-call(s32[3]{0:T(128)S(1)} %pad_add_fusion.where_ref, f32[4,16,4096]{2,1,0:T(8,128)S(1)} %get-tuple-element.22.mid_ref, f32[24,4096]{1,0:T(8,128)S(1)} %get-tuple-element.23.before_ref, f32[24,4096]{1,0:T(8,128)S(1)} %get-tuple-element.24.after_ref), custom_call_target="tpu_custom_call" | custom-call | flops 19660800 | bytes 4194304 | tf_op jit(solution)/shard_map/closing_flow/pallas_call | solution.py:189
  (11 shorter events, 0.0 us)
Async XLA Ops:
  0.6 1.2 %copy-start = (f32[1,4,16,4096]{3,2,1,0:T(8,128)S(1)}, f32[1,4,16,4096]{3,2,1,0:T(8,128)}, u32[]{:S(2)}) copy-start(f32[1,4,16,4096]{3,2,1,0:T(8,128)} %param.4) | copy-start | bytes 3145732
  1.9 0.7 copy-start.3
  2.6 15.3 %copy-start.1 = (f32[1,4,16,4096]{3,2,1,0:T(8,128)S(1)}, f32[1,4,16,4096]{3,2,1,0:T(8,128)}, u32[]{:S(2)}) copy-start(f32[1,4,16,4096]{3,2,1,0:T(8,128)} %param.4) | copy-start | bytes 3145732
  2.6 9.8 %collective-permute-start = (f32[24,4096]{1,0:T(8,128)S(1)}, f32[24,4096]{1,0:T(8,128)S(1)}, u32[]{:S(2)}, u32[]{:S(2)}) collective-permute-start(f32[24,4096]{1,0:T(8,128)S(1)} %get-tuple-element.15), channel_id=1, source_target_pairs={{0,1},{1,2},{2,3},{3,4},{4,5},{5,6},{6,7},{7,8},{8,9},{9,10},{10,1... | collective-permute-start | bytes 1179656 | tf_op jit(solution)/shard_map/ppermute | solution.py:403
  7.7 10.1 %collective-permute-start.3 = (f32[24,4096]{1,0:T(8,128)S(1)}, f32[24,4096]{1,0:T(8,128)S(1)}, u32[]{:S(2)}, u32[]{:S(2)}) collective-permute-start(f32[24,4096]{1,0:T(8,128)S(1)} %get-tuple-element.18), channel_id=1, source_target_pairs={{1,0},{2,1},{3,2},{4,3},{5,4},{6,5},{7,6},{8,7},{9,8},{10,9},{11,1... | collective-permute-start | bytes 1179656 | tf_op jit(solution)/shard_map/ppermute | solution.py:404
  21.4 29.5 %copy-start.4 = (s32[16]{0:T(128)S(1)}, s32[16]{0:T(128)}, u32[]{:S(2)}) copy-start(s32[16]{0:T(128)} %pairing_ref.1) | copy-start | bytes 196
  53.1 7.1 %copy-start.2 = (f32[4,16,4096]{2,1,0:T(8,128)S(1)}, f32[4,16,4096]{2,1,0:T(8,128)}, u32[]{:S(2)}) copy-start(f32[4,16,4096]{2,1,0:T(8,128)} %analysis_ref.1) | copy-start | bytes 3145732
  53.1 30.7 %all-to-all-start.1 = ((f32[16,136,128]{2,1,0:T(8,128)}), f32[16,136,128]{2,1,0:T(8,128)S(1)}, u32[]{:S(2)}, u32[]{:S(2)}) async-start(f32[16,136,128]{2,1,0:T(8,128)} %pair_spread.1), calls=%async_computation.1 | async-start | bytes 2228224 | tf_op jit(solution)/shard_map/all_to_all | solution.py:412
  61.2 48.0 %collective-permute-start.1 = (f32[24,4096]{1,0:T(8,128)}, f32[24,4096]{1,0:T(8,128)S(1)}, u32[]{:S(2)}, u32[]{:S(2)}) collective-permute-start(f32[24,4096]{1,0:T(8,128)} %get-tuple-element.16), channel_id=1, source_target_pairs={{0,1},{1,2},{2,3},{3,4},{4,5},{5,6},{6,7},{7,8},{8,9},{9,10},{10,1... | collective-permute-start | bytes 1179656 | tf_op jit(solution)/shard_map/ppermute | solution.py:406
  70.1 39.1 %collective-permute-start.2 = (f32[24,4096]{1,0:T(8,128)}, f32[24,4096]{1,0:T(8,128)S(1)}, u32[]{:S(2)}, u32[]{:S(2)}) collective-permute-start(f32[24,4096]{1,0:T(8,128)} %get-tuple-element.17), channel_id=1, source_target_pairs={{1,0},{2,1},{3,2},{4,3},{5,4},{6,5},{7,6},{8,7},{9,8},{10,9},{11,1... | collective-permute-start | bytes 1179656 | tf_op jit(solution)/shard_map/ppermute | solution.py:407
  84.8 30.1 %collective-permute-start.4 = (f32[24,4096]{1,0:T(8,128)}, f32[24,4096]{1,0:T(8,128)S(1)}, u32[]{:S(2)}, u32[]{:S(2)}) collective-permute-start(f32[24,4096]{1,0:T(8,128)} %get-tuple-element.19), channel_id=1, source_target_pairs={{0,1},{1,2},{2,3},{3,4},{4,5},{5,6},{6,7},{7,8},{8,9},{9,10},{10,1... | collective-permute-start | bytes 1179656 | tf_op jit(solution)/shard_map/ppermute | solution.py:414
  97.6 17.4 %collective-permute-start.5 = (f32[24,4096]{1,0:T(8,128)}, f32[24,4096]{1,0:T(8,128)}, u32[]{:S(2)}, u32[]{:S(2)}) collective-permute-start(f32[24,4096]{1,0:T(8,128)} %get-tuple-element.20), channel_id=1, source_target_pairs={{1,0},{2,1},{3,2},{4,3},{5,4},{6,5},{7,6},{8,7},{9,8},{10,9},{11,1... | collective-permute-start | bytes 1179656 | tf_op jit(solution)/shard_map/ppermute | solution.py:415
  99.5 15.4 %all-to-all-start.2 = ((f32[16,8,128]{2,1,0:T(8,128)}), f32[16,8,128]{2,1,0:T(8,128)S(1)}, u32[]{:S(2)}, u32[]{:S(2)}) async-start(f32[16,8,128]{2,1,0:T(8,128)} %get-tuple-element.21), calls=%async_computation.2 | async-start | bytes 131072 | tf_op jit(solution)/shard_map/all_to_all | solution.py:416

commit v7 on v6

--- a/solution.py
+++ b/solution.py
@@ -63,7 +63,7 @@
         out_shape=(edge, edge, jax.ShapeDtypeStruct((labels.shape[0], TILE), jnp.float32)),
         in_specs=[VMEM] * 2,
         out_specs=(VMEM,) * 3,
-        compiler_params=pltpu.CompilerParams(vmem_limit_bytes=8 << 20),
+        compiler_params=pltpu.CompilerParams(vmem_limit_bytes=6 << 20),
         cost_estimate=pl.CostEstimate(flops=1 << 18, bytes_accessed=2 << 20, transcendentals=0),
         name="first_edges",
     )(fields, labels)
@@ -89,7 +89,7 @@
         out_shape=(edge, edge),
         in_specs=[VMEM, VMEM, pl.BlockSpec(memory_space=pl.ANY)],
         out_specs=(VMEM, VMEM),
-        compiler_params=pltpu.CompilerParams(vmem_limit_bytes=8 << 20),
+        compiler_params=pltpu.CompilerParams(vmem_limit_bytes=6 << 20),
         cost_estimate=pl.CostEstimate(flops=1 << 18, bytes_accessed=2 << 20, transcendentals=0),
         name="analysis_edges",
     )(fields, labels, after)
@@ -192,7 +192,7 @@
         in_specs=[SMEM, VMEM, VMEM, VMEM],
         out_specs=VMEM,
         scratch_shapes=[state] * 5,
-        compiler_params=pltpu.CompilerParams(vmem_limit_bytes=24 << 20),
+        compiler_params=pltpu.CompilerParams(vmem_limit_bytes=6 << 20),
         cost_estimate=pl.CostEstimate(
             flops=60 * 10 * STRIP * width, bytes_accessed=1 << 22, transcendentals=0
         ),
@@ -271,7 +271,7 @@
         in_specs=[SMEM, SMEM, VMEM, VMEM, VMEM, VMEM],
         out_specs=VMEM,
         scratch_shapes=[pltpu.VMEM((local_rows + 2 * STRIP, TILE), jnp.float32)],
-        compiler_params=pltpu.CompilerParams(vmem_limit_bytes=8 << 20),
+        compiler_params=pltpu.CompilerParams(vmem_limit_bytes=6 << 20),
         cost_estimate=pl.CostEstimate(flops=1 << 20, bytes_accessed=3 << 20, transcendentals=0),
         name="pair_spread",
     )(where, pairing, everyone, labels, before, after)
@@ -305,7 +305,7 @@
         out_shape=(edge, edge, jax.ShapeDtypeStruct((lat_size, REGIONS, TILE), jnp.float32)),
         in_specs=[VMEM],
         out_specs=(VMEM,) * 3,
-        compiler_params=pltpu.CompilerParams(vmem_limit_bytes=8 << 20),
+        compiler_params=pltpu.CompilerParams(vmem_limit_bytes=6 << 20),
         cost_estimate=pl.CostEstimate(flops=1 << 18, bytes_accessed=2 << 20, transcendentals=0),
         name="spread_edges",
     )(back)
@@ -381,7 +381,7 @@
         ),
         in_specs=[VMEM] * 8,
         out_specs=(VMEM,) * 4,
-        compiler_params=pltpu.CompilerParams(vmem_limit_bytes=16 << 20),
+        compiler_params=pltpu.CompilerParams(vmem_limit_bytes=6 << 20),
         cost_estimate=pl.CostEstimate(flops=1 << 20, bytes_accessed=4 << 20, transcendentals=0),
         name="recentre",
     )(labels, analysis, a_before, a_after, back, b_before, b_after, shares)

time: 122 us -> 122 us (level)
  no operation moved by 1% of the time
where the time goes in v7:
time: 122 us; the launch traced here: 121 us
  starting transfers between devices  49.1 us (40%)
  blocking collectives  29.5 us (24%)
  waiting for transfers between devices  25.8 us (21%)
  Pallas kernels  14.1 us (12%)
  local copies, waits for them, and re-layouts  1.93 us (2%)
    all_to_all x1, blocking collectives, local(): everyone = lax.all_to_all(pieces, 'mem', 0, 0, tiled=True)  29.5 us
    ppermute x1, starting transfers between devices, local(): b_before = lax.ppermute(last, 'lat', up)  12.7 us
    all_to_all x1, waiting for transfers between devices, local(): back = lax.all_to_all(spread, 'mem', 0, 0, tiled=True)  11.9 us
    all_to_all x1, starting transfers between devices, local(): shares = lax.all_to_all(share, 'lat', 0, 0, tiled=True)  9.61 us
    ppermute x1, starting transfers between devices, local(): a_before = lax.ppermute(last, 'lat', up)  8.87 us
    pallas_call x2, Pallas kernels, flow(): pl.pallas_call(functools.partial(flow_kernel, total_rows, chunks), out_sh...  8.27 us
    all_to_all x1, starting transfers between devices, local(): back = lax.all_to_all(spread, 'mem', 0, 0, tiled=True)  7.07 us
    all_to_all x1, waiting for transfers between devices, local(): shares = lax.all_to_all(share, 'lat', 0, 0, tiled=True)  5.81 us
  transfers between devices with their start and end apart: 8, of which 4 were waited for; matrix products, arithmetic and copies ran while one was open for 0% of the time, Pallas kernels for 2%

profile of v7, /device:TPU:1, one launch (start us, length us, event | category | flops | bytes accessed | tf_op | source)
XLA Modules:
  0.0 121.3 jit_solution(10618342661856783557)
XLA Ops:
  0.6 1.2 %copy-done = f32[1,4,16,4096]{3,2,1,0:T(8,128)S(1)} copy-done((f32[1,4,16,4096]{3,2,1,0:T(8,128)S(1)}, f32[1,4,16,4096]{3,2,1,0:T(8,128)}, u32[]{:S(2)}) %copy-start) | copy-done | bytes 1048600
  1.9 0.7 copy-done.3
  2.6 0.1 first_edges.1
  2.6 5.1 %collective-permute-start = (f32[24,4096]{1,0:T(8,128)S(1)}, f32[24,4096]{1,0:T(8,128)S(1)}, u32[]{:S(2)}, u32[]{:S(2)}) collective-permute-start(f32[24,4096]{1,0:T(8,128)S(1)} %get-tuple-element.15), channel_id=1, source_target_pairs={{0,1},{1,2},{2,3},{3,4},{4,5},{5,6},{6,7},{7,8},{8,9},{9,10},{10,1... | collective-permute-start | bytes 1179656 | tf_op jit(solution)/shard_map/ppermute | solution.py:403
  7.7 1.9 %collective-permute-start.3 = (f32[24,4096]{1,0:T(8,128)S(1)}, f32[24,4096]{1,0:T(8,128)S(1)}, u32[]{:S(2)}, u32[]{:S(2)}) collective-permute-start(f32[24,4096]{1,0:T(8,128)S(1)} %get-tuple-element.18), channel_id=1, source_target_pairs={{1,0},{2,1},{3,2},{4,3},{5,4},{6,5},{7,6},{8,7},{9,8},{10,9},{11,1... | collective-permute-start | bytes 1179656 | tf_op jit(solution)/shard_map/ppermute | solution.py:404
  9.6 0.1 pad_add_fusion.where_ref
  9.7 2.7 %collective-permute-done.after_ref.before_ref = f32[24,4096]{1,0:T(8,128)S(1)} collective-permute-done((f32[24,4096]{1,0:T(8,128)S(1)}, f32[24,4096]{1,0:T(8,128)S(1)}, u32[]{:S(2)}, u32[]{:S(2)}) %collective-permute-start) | collective-permute-done | bytes 393248 | tf_op jit(solution)/shard_map/ppermute | solution.py:403
  12.4 5.4 %collective-permute-done.3.after_ref = f32[24,4096]{1,0:T(8,128)S(1)} collective-permute-done((f32[24,4096]{1,0:T(8,128)S(1)}, f32[24,4096]{1,0:T(8,128)S(1)}, u32[]{:S(2)}, u32[]{:S(2)}) %collective-permute-start.3) | collective-permute-done | bytes 393248 | tf_op jit(solution)/shard_map/ppermute | solution.py:404
  17.8 3.6 %first_flow.1 = f32[16,4,16,256]{3,2,1,0:T(8,128)S(1)} custom-call(s32[3]{0:T(128)S(1)} %pad_add_fusion.where_ref, f32[4,16,4096]{2,1,0:T(8,128)S(1)} %bitcast.5, f32[24,4096]{1,0:T(8,128)S(1)} %collective-permute-done.after_ref.before_ref, f32[24,4096]{1,0:T(8,128)S(1)} %collective-permute-done.3.after_ref), custom_call_target="tpu_custom_call" | custom-call | flops 19660800 | bytes 4194304 | tf_op jit(solution)/shard_map/first_flow/pallas_call | solution.py:189
  21.4 0.0 copy-start.4
  21.4 29.5 %all_to_all.15.all_ref = f32[16,4,16,256]{3,2,1,0:T(8,128)S(1)} all-to-all(f32[16,4,16,256]{3,2,1,0:T(8,128)S(1)} %first_flow.1), channel_id=1, replica_groups=mesh['mem'=16,'lat'=16] {'mem'}, dimensions={0} | all-to-all | bytes 2097152 | tf_op jit(solution)/shard_map/all_to_all | solution.py:409
  50.9 2.2 %pair_spread.1 = f32[16,136,128]{2,1,0:T(8,128)} custom-call(s32[3]{0:T(128)S(1)} %pad_add_fusion.where_ref, s32[16]{0:T(128)S(1)} %copy-done.4, f32[16,4,16,256]{3,2,1,0:T(8,128)S(1)} %all_to_all.15.all_ref, f32[16,128]{1,0:T(8,128)S(1)} %get-tuple-element.14.labels_ref, f32[24,4096]{1,0:T(8,128)S(1)} %collective-permute-done.after_ref.before_ref, ...), custom_call_target="tpu_custom_call" | custom-call | flops 1048576 | bytes 3145728 | tf_op jit(solution)/shard_map/pair_spread/pallas_call | solution.py:268
  53.1 7.1 %all-to-all-start.1 = ((f32[16,136,128]{2,1,0:T(8,128)}), f32[16,136,128]{2,1,0:T(8,128)S(1)}, u32[]{:S(2)}, u32[]{:S(2)}) async-start(f32[16,136,128]{2,1,0:T(8,128)} %pair_spread.1), calls=%async_computation.1 | async-start | bytes 2228224 | tf_op jit(solution)/shard_map/all_to_all | solution.py:412
  60.2 0.9 analysis_edges.1
  61.2 8.9 %collective-permute-start.1 = (f32[24,4096]{1,0:T(8,128)}, f32[24,4096]{1,0:T(8,128)S(1)}, u32[]{:S(2)}, u32[]{:S(2)}) collective-permute-start(f32[24,4096]{1,0:T(8,128)} %get-tuple-element.16), channel_id=1, source_target_pairs={{0,1},{1,2},{2,3},{3,4},{4,5},{5,6},{6,7},{7,8},{8,9},{9,10},{10,1... | collective-permute-start | bytes 1179656 | tf_op jit(solution)/shard_map/ppermute | solution.py:406
  70.1 1.9 %collective-permute-start.2 = (f32[24,4096]{1,0:T(8,128)}, f32[24,4096]{1,0:T(8,128)S(1)}, u32[]{:S(2)}, u32[]{:S(2)}) collective-permute-start(f32[24,4096]{1,0:T(8,128)} %get-tuple-element.17), channel_id=1, source_target_pairs={{1,0},{2,1},{3,2},{4,3},{5,4},{6,5},{7,6},{8,7},{9,8},{10,9},{11,1... | collective-permute-start | bytes 1179656 | tf_op jit(solution)/shard_map/ppermute | solution.py:407
  72.0 11.9 %all-to-all-done.1.back_ref = f32[16,136,128]{2,1,0:T(8,128)S(1)} async-done(((f32[16,136,128]{2,1,0:T(8,128)}), f32[16,136,128]{2,1,0:T(8,128)S(1)}, u32[]{:S(2)}, u32[]{:S(2)}) %all-to-all-start.1) | async-done | bytes 1114144 | tf_op jit(solution)/shard_map/all_to_all | solution.py:412
  83.8 1.0 spread_edges.1
  84.8 12.7 %collective-permute-start.4 = (f32[24,4096]{1,0:T(8,128)}, f32[24,4096]{1,0:T(8,128)S(1)}, u32[]{:S(2)}, u32[]{:S(2)}) collective-permute-start(f32[24,4096]{1,0:T(8,128)} %get-tuple-element.19), channel_id=1, source_target_pairs={{0,1},{1,2},{2,3},{3,4},{4,5},{5,6},{6,7},{7,8},{8,9},{9,10},{10,1... | collective-permute-start | bytes 1179656 | tf_op jit(solution)/shard_map/ppermute | solution.py:414
  97.6 1.9 %collective-permute-start.5 = (f32[24,4096]{1,0:T(8,128)}, f32[24,4096]{1,0:T(8,128)}, u32[]{:S(2)}, u32[]{:S(2)}) collective-permute-start(f32[24,4096]{1,0:T(8,128)} %get-tuple-element.20), channel_id=1, source_target_pairs={{1,0},{2,1},{3,2},{4,3},{5,4},{6,5},{7,6},{8,7},{9,8},{10,9},{11,1... | collective-permute-start | bytes 1179656 | tf_op jit(solution)/shard_map/ppermute | solution.py:415
  99.5 9.6 %all-to-all-start.2 = ((f32[16,8,128]{2,1,0:T(8,128)}), f32[16,8,128]{2,1,0:T(8,128)S(1)}, u32[]{:S(2)}, u32[]{:S(2)}) async-start(f32[16,8,128]{2,1,0:T(8,128)} %get-tuple-element.21), calls=%async_computation.2 | async-start | bytes 131072 | tf_op jit(solution)/shard_map/all_to_all | solution.py:416
  109.2 5.8 %all-to-all-done.2.shares_ref = f32[16,8,128]{2,1,0:T(8,128)S(1)} async-done(((f32[16,8,128]{2,1,0:T(8,128)}), f32[16,8,128]{2,1,0:T(8,128)S(1)}, u32[]{:S(2)}, u32[]{:S(2)}) %all-to-all-start.2) | async-done | bytes 65568 | tf_op jit(solution)/shard_map/all_to_all | solution.py:416
  115.0 1.6 %recentre.1 = (f32[4,16,4096]{2,1,0:T(8,128)S(1)}, f32[24,4096]{1,0:T(8,128)S(1)}, f32[24,4096]{1,0:T(8,128)S(1)}, f32[1,8]{1,0:T(1,128)}) custom-call(f32[16,128]{1,0:T(8,128)S(1)} %get-tuple-element.14.labels_ref, f32[4,16,4096]{2,1,0:T(8,128)S(1)} %copy-done.2, f32[24,4096]{1,0:T(8,128)S(1)} %collective-permute-done.1.a_before_ref, ...), custom_call_target="tpu_custom_call" | custom-call | flops 1048576 | bytes 4194304 | tf_op jit(solution)/shard_map/recentre/pallas_call | solution.py:374
  116.6 4.7 %closing_flow.1 = f32[4,16,4096]{2,1,0:T(8,128)} custom-call(s32[3]{0:T(128)S(1)} %pad_add_fusion.where_ref, f32[4,16,4096]{2,1,0:T(8,128)S(1)} %get-tuple-element.22.mid_ref, f32[24,4096]{1,0:T(8,128)S(1)} %get-tuple-element.23.before_ref, f32[24,4096]{1,0:T(8,128)S(1)} %get-tuple-element.24.after_ref), custom_call_target="tpu_custom_call" | custom-call | flops 19660800 | bytes 4194304 | tf_op jit(solution)/shard_map/closing_flow/pallas_call | solution.py:189
  (11 shorter events, 0.0 us)
Async XLA Ops:
  0.6 1.2 %copy-start = (f32[1,4,16,4096]{3,2,1,0:T(8,128)S(1)}, f32[1,4,16,4096]{3,2,1,0:T(8,128)}, u32[]{:S(2)}) copy-start(f32[1,4,16,4096]{3,2,1,0:T(8,128)} %param.4) | copy-start | bytes 3145732
  1.9 0.7 copy-start.3
  2.6 15.3 %copy-start.1 = (f32[1,4,16,4096]{3,2,1,0:T(8,128)S(1)}, f32[1,4,16,4096]{3,2,1,0:T(8,128)}, u32[]{:S(2)}) copy-start(f32[1,4,16,4096]{3,2,1,0:T(8,128)} %param.4) | copy-start | bytes 3145732
  2.6 9.8 %collective-permute-start = (f32[24,4096]{1,0:T(8,128)S(1)}, f32[24,4096]{1,0:T(8,128)S(1)}, u32[]{:S(2)}, u32[]{:S(2)}) collective-permute-start(f32[24,4096]{1,0:T(8,128)S(1)} %get-tuple-element.15), channel_id=1, source_target_pairs={{0,1},{1,2},{2,3},{3,4},{4,5},{5,6},{6,7},{7,8},{8,9},{9,10},{10,1... | collective-permute-start | bytes 1179656 | tf_op jit(solution)/shard_map/ppermute | solution.py:403
  7.7 10.1 %collective-permute-start.3 = (f32[24,4096]{1,0:T(8,128)S(1)}, f32[24,4096]{1,0:T(8,128)S(1)}, u32[]{:S(2)}, u32[]{:S(2)}) collective-permute-start(f32[24,4096]{1,0:T(8,128)S(1)} %get-tuple-element.18), channel_id=1, source_target_pairs={{1,0},{2,1},{3,2},{4,3},{5,4},{6,5},{7,6},{8,7},{9,8},{10,9},{11,1... | collective-permute-start | bytes 1179656 | tf_op jit(solution)/shard_map/ppermute | solution.py:404
  21.4 29.5 %copy-start.4 = (s32[16]{0:T(128)S(1)}, s32[16]{0:T(128)}, u32[]{:S(2)}) copy-start(s32[16]{0:T(128)} %pairing_ref.1) | copy-start | bytes 196
  53.1 7.1 %copy-start.2 = (f32[4,16,4096]{2,1,0:T(8,128)S(1)}, f32[4,16,4096]{2,1,0:T(8,128)}, u32[]{:S(2)}) copy-start(f32[4,16,4096]{2,1,0:T(8,128)} %analysis_ref.1) | copy-start | bytes 3145732
  53.1 30.7 %all-to-all-start.1 = ((f32[16,136,128]{2,1,0:T(8,128)}), f32[16,136,128]{2,1,0:T(8,128)S(1)}, u32[]{:S(2)}, u32[]{:S(2)}) async-start(f32[16,136,128]{2,1,0:T(8,128)} %pair_spread.1), calls=%async_computation.1 | async-start | bytes 2228224 | tf_op jit(solution)/shard_map/all_to_all | solution.py:412
  61.2 48.0 %collective-permute-start.1 = (f32[24,4096]{1,0:T(8,128)}, f32[24,4096]{1,0:T(8,128)S(1)}, u32[]{:S(2)}, u32[]{:S(2)}) collective-permute-start(f32[24,4096]{1,0:T(8,128)} %get-tuple-element.16), channel_id=1, source_target_pairs={{0,1},{1,2},{2,3},{3,4},{4,5},{5,6},{6,7},{7,8},{8,9},{9,10},{10,1... | collective-permute-start | bytes 1179656 | tf_op jit(solution)/shard_map/ppermute | solution.py:406
  70.1 39.1 %collective-permute-start.2 = (f32[24,4096]{1,0:T(8,128)}, f32[24,4096]{1,0:T(8,128)S(1)}, u32[]{:S(2)}, u32[]{:S(2)}) collective-permute-start(f32[24,4096]{1,0:T(8,128)} %get-tuple-element.17), channel_id=1, source_target_pairs={{1,0},{2,1},{3,2},{4,3},{5,4},{6,5},{7,6},{8,7},{9,8},{10,9},{11,1... | collective-permute-start | bytes 1179656 | tf_op jit(solution)/shard_map/ppermute | solution.py:407
  84.8 30.1 %collective-permute-start.4 = (f32[24,4096]{1,0:T(8,128)}, f32[24,4096]{1,0:T(8,128)S(1)}, u32[]{:S(2)}, u32[]{:S(2)}) collective-permute-start(f32[24,4096]{1,0:T(8,128)} %get-tuple-element.19), channel_id=1, source_target_pairs={{0,1},{1,2},{2,3},{3,4},{4,5},{5,6},{6,7},{7,8},{8,9},{9,10},{10,1... | collective-permute-start | bytes 1179656 | tf_op jit(solution)/shard_map/ppermute | solution.py:414
  97.6 17.4 %collective-permute-start.5 = (f32[24,4096]{1,0:T(8,128)}, f32[24,4096]{1,0:T(8,128)}, u32[]{:S(2)}, u32[]{:S(2)}) collective-permute-start(f32[24,4096]{1,0:T(8,128)} %get-tuple-element.20), channel_id=1, source_target_pairs={{1,0},{2,1},{3,2},{4,3},{5,4},{6,5},{7,6},{8,7},{9,8},{10,9},{11,1... | collective-permute-start | bytes 1179656 | tf_op jit(solution)/shard_map/ppermute | solution.py:415
  99.5 15.4 %all-to-all-start.2 = ((f32[16,8,128]{2,1,0:T(8,128)}), f32[16,8,128]{2,1,0:T(8,128)S(1)}, u32[]{:S(2)}, u32[]{:S(2)}) async-start(f32[16,8,128]{2,1,0:T(8,128)} %get-tuple-element.21), calls=%async_computation.2 | async-start | bytes 131072 | tf_op jit(solution)/shard_map/all_to_all | solution.py:416

commit v8 on v6

--- a/solution.py
+++ b/solution.py
@@ -201,7 +201,8 @@
 
 
 def pair_kernel(
-    where_ref, pairing_ref, all_ref, labels_ref, before_ref, after_ref, spread_ref, near_ref
+    where_ref, pairing_ref, all_ref, labels_ref, before_ref, after_ref, out_hbm, near_ref,
+    spread_ref, sems
 ):
     members, fields, local_rows, size = all_ref.shape
     tiles = size // TILE
@@ -240,6 +241,7 @@
         return jnp.sum(jnp.concatenate(rows, axis=0), axis=1, keepdims=True)
 
     empty = jnp.where(lane == 1, column(counts), 0.0)
+    copies = []
     for m in range(members):
         partner = pairing_ref[m]
         squares = [None] * tiles
@@ -260,6 +262,10 @@
         spread_ref[m, fields * tiles * local_rows :, :] = jnp.where(
             lane == 0, column(parts), empty
         )
+        copies.append(pltpu.make_async_copy(spread_ref.at[m], out_hbm.at[m], sems.at[m]))
+        copies[m].start()
+    for copy in copies:
+        copy.wait()
 
 
 def pair_spread(where, pairing, everyone, labels, before, after):
@@ -269,8 +275,12 @@
         pair_kernel,
         out_shape=jax.ShapeDtypeStruct((members, rows, TILE), jnp.float32),
         in_specs=[SMEM, SMEM, VMEM, VMEM, VMEM, VMEM],
-        out_specs=VMEM,
-        scratch_shapes=[pltpu.VMEM((local_rows + 2 * STRIP, TILE), jnp.float32)],
+        out_specs=pl.BlockSpec(memory_space=pltpu.MemorySpace.HBM),
+        scratch_shapes=[
+            pltpu.VMEM((local_rows + 2 * STRIP, TILE), jnp.float32),
+            pltpu.VMEM((members, rows, TILE), jnp.float32),
+            pltpu.SemaphoreType.DMA((members,)),
+        ],
         compiler_params=pltpu.CompilerParams(vmem_limit_bytes=8 << 20),
         cost_estimate=pl.CostEstimate(flops=1 << 20, bytes_accessed=3 << 20, transcendentals=0),
         name="pair_spread",

time: 122 us -> 122 us (level)
  no operation moved by 1% of the time
where the time goes in v8:
time: 122 us; the launch traced here: 121 us
  starting transfers between devices  48.9 us (40%)
  blocking collectives  29.5 us (24%)
  waiting for transfers between devices  26.1 us (21%)
  Pallas kernels  14.2 us (12%)
  local copies, waits for them, and re-layouts  1.93 us (2%)
    all_to_all x1, blocking collectives, local(): everyone = lax.all_to_all(pieces, 'mem', 0, 0, tiled=True)  29.5 us
    ppermute x1, starting transfers between devices, local(): b_before = lax.ppermute(last, 'lat', up)  12.5 us
    all_to_all x1, waiting for transfers between devices, local(): back = lax.all_to_all(spread, 'mem', 0, 0, tiled=True)  12.1 us
    all_to_all x1, starting transfers between devices, local(): shares = lax.all_to_all(share, 'lat', 0, 0, tiled=True)  9.67 us
    ppermute x1, starting transfers between devices, local(): a_before = lax.ppermute(last, 'lat', up)  8.8 us
    pallas_call x2, Pallas kernels, flow(): pl.pallas_call(functools.partial(flow_kernel, total_rows, chunks), out_sh...  8.26 us
    all_to_all x1, starting transfers between devices, local(): back = lax.all_to_all(spread, 'mem', 0, 0, tiled=True)  7.08 us
    all_to_all x1, waiting for transfers between devices, local(): shares = lax.all_to_all(share, 'lat', 0, 0, tiled=True)  5.81 us
  transfers between devices with their start and end apart: 8, of which 4 were waited for; matrix products, arithmetic and copies ran while one was open for 0% of the time, Pallas kernels for 2%

profile of v8, /device:TPU:1, one launch (start us, length us, event | category | flops | bytes accessed | tf_op | source)
XLA Modules:
  0.0 121.4 jit_solution(466545506582120708)
XLA Ops:
  0.6 1.2 %copy-done = f32[1,4,16,4096]{3,2,1,0:T(8,128)S(1)} copy-done((f32[1,4,16,4096]{3,2,1,0:T(8,128)S(1)}, f32[1,4,16,4096]{3,2,1,0:T(8,128)}, u32[]{:S(2)}) %copy-start) | copy-done | bytes 1048600
  1.9 0.7 copy-done.3
  2.6 0.1 first_edges.1
  2.6 5.1 %collective-permute-start = (f32[24,4096]{1,0:T(8,128)S(1)}, f32[24,4096]{1,0:T(8,128)S(1)}, u32[]{:S(2)}, u32[]{:S(2)}) collective-permute-start(f32[24,4096]{1,0:T(8,128)S(1)} %get-tuple-element.15), channel_id=1, source_target_pairs={{0,1},{1,2},{2,3},{3,4},{4,5},{5,6},{6,7},{7,8},{8,9},{9,10},{10,1... | collective-permute-start | bytes 1179656 | tf_op jit(solution)/shard_map/ppermute | solution.py:413
  7.7 1.9 %collective-permute-start.3 = (f32[24,4096]{1,0:T(8,128)S(1)}, f32[24,4096]{1,0:T(8,128)S(1)}, u32[]{:S(2)}, u32[]{:S(2)}) collective-permute-start(f32[24,4096]{1,0:T(8,128)S(1)} %get-tuple-element.18), channel_id=1, source_target_pairs={{1,0},{2,1},{3,2},{4,3},{5,4},{6,5},{7,6},{8,7},{9,8},{10,9},{11,1... | collective-permute-start | bytes 1179656 | tf_op jit(solution)/shard_map/ppermute | solution.py:414
  9.6 0.1 pad_add_fusion.where_ref
  9.7 2.7 %collective-permute-done.after_ref.before_ref = f32[24,4096]{1,0:T(8,128)S(1)} collective-permute-done((f32[24,4096]{1,0:T(8,128)S(1)}, f32[24,4096]{1,0:T(8,128)S(1)}, u32[]{:S(2)}, u32[]{:S(2)}) %collective-permute-start) | collective-permute-done | bytes 393248 | tf_op jit(solution)/shard_map/ppermute | solution.py:413
  12.4 5.4 %collective-permute-done.3.after_ref = f32[24,4096]{1,0:T(8,128)S(1)} collective-permute-done((f32[24,4096]{1,0:T(8,128)S(1)}, f32[24,4096]{1,0:T(8,128)S(1)}, u32[]{:S(2)}, u32[]{:S(2)}) %collective-permute-start.3) | collective-permute-done | bytes 393248 | tf_op jit(solution)/shard_map/ppermute | solution.py:414
  17.8 3.6 %first_flow.1 = f32[16,4,16,256]{3,2,1,0:T(8,128)S(1)} custom-call(s32[3]{0:T(128)S(1)} %pad_add_fusion.where_ref, f32[4,16,4096]{2,1,0:T(8,128)S(1)} %bitcast.5, f32[24,4096]{1,0:T(8,128)S(1)} %collective-permute-done.after_ref.before_ref, f32[24,4096]{1,0:T(8,128)S(1)} %collective-permute-done.3.after_ref), custom_call_target="tpu_custom_call" | custom-call | flops 19660800 | bytes 4194304 | tf_op jit(solution)/shard_map/first_flow/pallas_call | solution.py:189
  21.4 0.0 copy-start.4
  21.4 29.5 %all_to_all.15.all_ref = f32[16,4,16,256]{3,2,1,0:T(8,128)S(1)} all-to-all(f32[16,4,16,256]{3,2,1,0:T(8,128)S(1)} %first_flow.1), channel_id=1, replica_groups=mesh['mem'=16,'lat'=16] {'mem'}, dimensions={0} | all-to-all | bytes 2097152 | tf_op jit(solution)/shard_map/all_to_all | solution.py:419
  50.9 2.2 %pair_spread.1 = f32[16,136,128]{2,1,0:T(8,128)} custom-call(s32[3]{0:T(128)S(1)} %pad_add_fusion.where_ref, s32[16]{0:T(128)S(1)} %copy-done.4, f32[16,4,16,256]{3,2,1,0:T(8,128)S(1)} %all_to_all.15.all_ref, f32[16,128]{1,0:T(8,128)S(1)} %get-tuple-element.14.labels_ref, f32[24,4096]{1,0:T(8,128)S(1)} %collective-permute-done.after_ref.before_ref, ...), custom_call_target="tpu_custom_call" | custom-call | flops 1048576 | bytes 3145728 | tf_op jit(solution)/shard_map/pair_spread/pallas_call | solution.py:274
  53.2 7.1 %all-to-all-start.1 = ((f32[16,136,128]{2,1,0:T(8,128)}), f32[16,136,128]{2,1,0:T(8,128)S(1)}, u32[]{:S(2)}, u32[]{:S(2)}) async-start(f32[16,136,128]{2,1,0:T(8,128)} %pair_spread.1), calls=%async_computation.1 | async-start | bytes 2228224 | tf_op jit(solution)/shard_map/all_to_all | solution.py:422
  60.3 0.9 analysis_edges.1
  61.2 8.8 %collective-permute-start.1 = (f32[24,4096]{1,0:T(8,128)}, f32[24,4096]{1,0:T(8,128)S(1)}, u32[]{:S(2)}, u32[]{:S(2)}) collective-permute-start(f32[24,4096]{1,0:T(8,128)} %get-tuple-element.16), channel_id=1, source_target_pairs={{0,1},{1,2},{2,3},{3,4},{4,5},{5,6},{6,7},{7,8},{8,9},{9,10},{10,1... | collective-permute-start | bytes 1179656 | tf_op jit(solution)/shard_map/ppermute | solution.py:416
  70.1 1.9 %collective-permute-start.2 = (f32[24,4096]{1,0:T(8,128)}, f32[24,4096]{1,0:T(8,128)S(1)}, u32[]{:S(2)}, u32[]{:S(2)}) collective-permute-start(f32[24,4096]{1,0:T(8,128)} %get-tuple-element.17), channel_id=1, source_target_pairs={{1,0},{2,1},{3,2},{4,3},{5,4},{6,5},{7,6},{8,7},{9,8},{10,9},{11,1... | collective-permute-start | bytes 1179656 | tf_op jit(solution)/shard_map/ppermute | solution.py:417
  72.0 12.1 %all-to-all-done.1.back_ref = f32[16,136,128]{2,1,0:T(8,128)S(1)} async-done(((f32[16,136,128]{2,1,0:T(8,128)}), f32[16,136,128]{2,1,0:T(8,128)S(1)}, u32[]{:S(2)}, u32[]{:S(2)}) %all-to-all-start.1) | async-done | bytes 1114144 | tf_op jit(solution)/shard_map/all_to_all | solution.py:422
  84.1 1.0 spread_edges.1
  85.1 12.5 %collective-permute-start.4 = (f32[24,4096]{1,0:T(8,128)}, f32[24,4096]{1,0:T(8,128)S(1)}, u32[]{:S(2)}, u32[]{:S(2)}) collective-permute-start(f32[24,4096]{1,0:T(8,128)} %get-tuple-element.19), channel_id=1, source_target_pairs={{0,1},{1,2},{2,3},{3,4},{4,5},{5,6},{6,7},{7,8},{8,9},{9,10},{10,1... | collective-permute-start | bytes 1179656 | tf_op jit(solution)/shard_map/ppermute | solution.py:424
  97.6 1.9 %collective-permute-start.5 = (f32[24,4096]{1,0:T(8,128)}, f32[24,4096]{1,0:T(8,128)}, u32[]{:S(2)}, u32[]{:S(2)}) collective-permute-start(f32[24,4096]{1,0:T(8,128)} %get-tuple-element.20), channel_id=1, source_target_pairs={{1,0},{2,1},{3,2},{4,3},{5,4},{6,5},{7,6},{8,7},{9,8},{10,9},{11,1... | collective-permute-start | bytes 1179656 | tf_op jit(solution)/shard_map/ppermute | solution.py:425
  99.5 9.7 %all-to-all-start.2 = ((f32[16,8,128]{2,1,0:T(8,128)}), f32[16,8,128]{2,1,0:T(8,128)S(1)}, u32[]{:S(2)}, u32[]{:S(2)}) async-start(f32[16,8,128]{2,1,0:T(8,128)} %get-tuple-element.21), calls=%async_computation.2 | async-start | bytes 131072 | tf_op jit(solution)/shard_map/all_to_all | solution.py:426
  109.2 5.8 %all-to-all-done.2.shares_ref = f32[16,8,128]{2,1,0:T(8,128)S(1)} async-done(((f32[16,8,128]{2,1,0:T(8,128)}), f32[16,8,128]{2,1,0:T(8,128)S(1)}, u32[]{:S(2)}, u32[]{:S(2)}) %all-to-all-start.2) | async-done | bytes 65568 | tf_op jit(solution)/shard_map/all_to_all | solution.py:426
  115.0 1.7 %recentre.1 = (f32[4,16,4096]{2,1,0:T(8,128)S(1)}, f32[24,4096]{1,0:T(8,128)S(1)}, f32[24,4096]{1,0:T(8,128)S(1)}, f32[1,8]{1,0:T(1,128)}) custom-call(f32[16,128]{1,0:T(8,128)S(1)} %get-tuple-element.14.labels_ref, f32[4,16,4096]{2,1,0:T(8,128)S(1)} %copy-done.2, f32[24,4096]{1,0:T(8,128)S(1)} %collective-permute-done.1.a_before_ref, ...), custom_call_target="tpu_custom_call" | custom-call | flops 1048576 | bytes 4194304 | tf_op jit(solution)/shard_map/recentre/pallas_call | solution.py:384
  116.7 4.6 %closing_flow.1 = f32[4,16,4096]{2,1,0:T(8,128)} custom-call(s32[3]{0:T(128)S(1)} %pad_add_fusion.where_ref, f32[4,16,4096]{2,1,0:T(8,128)S(1)} %get-tuple-element.22.mid_ref, f32[24,4096]{1,0:T(8,128)S(1)} %get-tuple-element.23.before_ref, f32[24,4096]{1,0:T(8,128)S(1)} %get-tuple-element.24.after_ref), custom_call_target="tpu_custom_call" | custom-call | flops 19660800 | bytes 4194304 | tf_op jit(solution)/shard_map/closing_flow/pallas_call | solution.py:189
  (11 shorter events, 0.0 us)
Async XLA Ops:
  0.6 1.2 %copy-start = (f32[1,4,16,4096]{3,2,1,0:T(8,128)S(1)}, f32[1,4,16,4096]{3,2,1,0:T(8,128)}, u32[]{:S(2)}) copy-start(f32[1,4,16,4096]{3,2,1,0:T(8,128)} %param.4) | copy-start | bytes 3145732
  1.9 0.7 copy-start.3
  2.6 15.3 %copy-start.1 = (f32[1,4,16,4096]{3,2,1,0:T(8,128)S(1)}, f32[1,4,16,4096]{3,2,1,0:T(8,128)}, u32[]{:S(2)}) copy-start(f32[1,4,16,4096]{3,2,1,0:T(8,128)} %param.4) | copy-start | bytes 3145732
  2.6 9.8 %collective-permute-start = (f32[24,4096]{1,0:T(8,128)S(1)}, f32[24,4096]{1,0:T(8,128)S(1)}, u32[]{:S(2)}, u32[]{:S(2)}) collective-permute-start(f32[24,4096]{1,0:T(8,128)S(1)} %get-tuple-element.15), channel_id=1, source_target_pairs={{0,1},{1,2},{2,3},{3,4},{4,5},{5,6},{6,7},{7,8},{8,9},{9,10},{10,1... | collective-permute-start | bytes 1179656 | tf_op jit(solution)/shard_map/ppermute | solution.py:413
  7.7 10.1 %collective-permute-start.3 = (f32[24,4096]{1,0:T(8,128)S(1)}, f32[24,4096]{1,0:T(8,128)S(1)}, u32[]{:S(2)}, u32[]{:S(2)}) collective-permute-start(f32[24,4096]{1,0:T(8,128)S(1)} %get-tuple-element.18), channel_id=1, source_target_pairs={{1,0},{2,1},{3,2},{4,3},{5,4},{6,5},{7,6},{8,7},{9,8},{10,9},{11,1... | collective-permute-start | bytes 1179656 | tf_op jit(solution)/shard_map/ppermute | solution.py:414
  21.4 29.5 %copy-start.4 = (s32[16]{0:T(128)S(1)}, s32[16]{0:T(128)}, u32[]{:S(2)}) copy-start(s32[16]{0:T(128)} %pairing_ref.1) | copy-start | bytes 196
  53.2 7.1 %copy-start.2 = (f32[4,16,4096]{2,1,0:T(8,128)S(1)}, f32[4,16,4096]{2,1,0:T(8,128)}, u32[]{:S(2)}) copy-start(f32[4,16,4096]{2,1,0:T(8,128)} %analysis_ref.1) | copy-start | bytes 3145732
  53.2 30.9 %all-to-all-start.1 = ((f32[16,136,128]{2,1,0:T(8,128)}), f32[16,136,128]{2,1,0:T(8,128)S(1)}, u32[]{:S(2)}, u32[]{:S(2)}) async-start(f32[16,136,128]{2,1,0:T(8,128)} %pair_spread.1), calls=%async_computation.1 | async-start | bytes 2228224 | tf_op jit(solution)/shard_map/all_to_all | solution.py:422
  61.2 48.0 %collective-permute-start.1 = (f32[24,4096]{1,0:T(8,128)}, f32[24,4096]{1,0:T(8,128)S(1)}, u32[]{:S(2)}, u32[]{:S(2)}) collective-permute-start(f32[24,4096]{1,0:T(8,128)} %get-tuple-element.16), channel_id=1, source_target_pairs={{0,1},{1,2},{2,3},{3,4},{4,5},{5,6},{6,7},{7,8},{8,9},{9,10},{10,1... | collective-permute-start | bytes 1179656 | tf_op jit(solution)/shard_map/ppermute | solution.py:416
  70.1 39.2 %collective-permute-start.2 = (f32[24,4096]{1,0:T(8,128)}, f32[24,4096]{1,0:T(8,128)S(1)}, u32[]{:S(2)}, u32[]{:S(2)}) collective-permute-start(f32[24,4096]{1,0:T(8,128)} %get-tuple-element.17), channel_id=1, source_target_pairs={{1,0},{2,1},{3,2},{4,3},{5,4},{6,5},{7,6},{8,7},{9,8},{10,9},{11,1... | collective-permute-start | bytes 1179656 | tf_op jit(solution)/shard_map/ppermute | solution.py:417
  85.1 29.9 %collective-permute-start.4 = (f32[24,4096]{1,0:T(8,128)}, f32[24,4096]{1,0:T(8,128)S(1)}, u32[]{:S(2)}, u32[]{:S(2)}) collective-permute-start(f32[24,4096]{1,0:T(8,128)} %get-tuple-element.19), channel_id=1, source_target_pairs={{0,1},{1,2},{2,3},{3,4},{4,5},{5,6},{6,7},{7,8},{8,9},{9,10},{10,1... | collective-permute-start | bytes 1179656 | tf_op jit(solution)/shard_map/ppermute | solution.py:424
  97.6 17.4 %collective-permute-start.5 = (f32[24,4096]{1,0:T(8,128)}, f32[24,4096]{1,0:T(8,128)}, u32[]{:S(2)}, u32[]{:S(2)}) collective-permute-start(f32[24,4096]{1,0:T(8,128)} %get-tuple-element.20), channel_id=1, source_target_pairs={{1,0},{2,1},{3,2},{4,3},{5,4},{6,5},{7,6},{8,7},{9,8},{10,9},{11,1... | collective-permute-start | bytes 1179656 | tf_op jit(solution)/shard_map/ppermute | solution.py:425
  99.5 15.5 %all-to-all-start.2 = ((f32[16,8,128]{2,1,0:T(8,128)}), f32[16,8,128]{2,1,0:T(8,128)S(1)}, u32[]{:S(2)}, u32[]{:S(2)}) async-start(f32[16,8,128]{2,1,0:T(8,128)} %get-tuple-element.21), calls=%async_computation.2 | async-start | bytes 131072 | tf_op jit(solution)/shard_map/all_to_all | solution.py:426
